TPU v7x, 32 devices: a whole 2x2x4 slice. The times are simulated.
32 devices in a mesh: groups: 2 (over x), ctx: 16 (over z, y, core).
Axes of the slice: x: 2, y: 2, z: 4, core: 2. Of those that a mesh axis runs over, the one named last changes fastest.
Arguments:
- conv_input: bfloat16 [4096, 5120], P(('groups', 'ctx')), parts along dimension 0, may hold values from -6 to 6
- step_raw: float32 [4096, 64], P(('groups', 'ctx')), parts along dimension 0, may hold values from -5 to 5.5
- step_bias: float32 [64], replicated, may hold values from -14 to -2
- decay_log: float32 [64], replicated, may hold values from -3 to 0.7
- skip_gain: float32 [64], replicated, may hold values from 0.5 to 1.5
- conv_weight: float32 [4, 5120], replicated, may hold values from -3 to 3
- conv_bias: float32 [5120], replicated, may hold values from -1 to 0.5
- doc_lengths: int32 [8], P('groups'), parts along dimension 0, may hold values from 1 to 1024, 2048 in all
- grad_out: bfloat16 [4096, 4096], P(('groups', 'ctx')), parts along dimension 0, may hold values from -400 to 400
Outputs:
- mixer_out: bfloat16 [4096, 4096], P(('groups', 'ctx')), parts along dimension 0
- grad_input: bfloat16 [4096, 5120], P(('groups', 'ctx')), parts along dimension 0
- grad_step: float32 [4096, 64], P(('groups', 'ctx')), parts along dimension 0
- grad_conv: float32 [10, 5120], P('groups'), parts along dimension 0
- grad_heads: float32 [6, 64], P('groups'), parts along dimension 0
There are 2 independent parts, one for each index of `groups`. A program takes and returns all parts, laid end to end along the dimension named above; an argument that names none is the same for every part. Nothing has to cross between parts.
Inputs may be any that keep to these rules, and one draw needn't show every extreme that they name: doc_lengths lists the lengths of the 4 documents that follow one another from token 0; they sum to 2048, and the longest has exactly 1024 tokens.
All inputs are finite; a program needn't handle non-finite values.
Results may differ from a plain program's by a relative error of at most 0.001.
Values may be sent and summed in bfloat16 or wider, within the bound.
No kernel may reach another device: no remote copies, remote signals or barrier semaphores. Data moves between devices by JAX's collectives and lax.ppermute only.
A program may use at most 192 MiB of HBM per device.

v0:
```python
from functools import partial
import math

import jax
import jax.numpy as jnp
from jax import lax
from jax.sharding import PartitionSpec as P

GROUPS = 4


HIGH = lax.Precision.HIGHEST


def passed_along(value, axis, steps):
    count = lax.axis_size(axis)
    initial, last = (max(0, -steps), min(count, count - steps))
    return lax.ppermute(value, axis, [(source, source + steps) for source in range(initial, last)])


def doc_offsets(doc_lengths, positions):
    ends = jnp.cumsum(doc_lengths, dtype=jnp.int32)
    starts = ends - doc_lengths
    before = starts[None, :] <= positions[:, None]
    opening = jnp.max(jnp.where(before, starts[None, :], 0), axis=1)
    return positions - opening


def convolve(extended, conv_weight, conv_bias, inside):
    count = inside.shape[0]
    taps = conv_weight.shape[0]
    total = jnp.zeros((count, extended.shape[1]), jnp.float32) + conv_bias[None, :]
    for lag in range(taps):
        reach = taps - 1 - lag
        valid = (inside >= reach).astype(jnp.float32)[:, None]
        total = total + conv_weight[lag][None, :] * extended[lag : lag + count] * valid
    return jax.nn.silu(total)


def prepare(
    extended, step_raw, step_bias, decay_log, skip_gain, conv_weight, conv_bias, inside, layout
):
    groups, headdim, block = layout
    length, heads = step_raw.shape
    share = heads // groups
    count = length // block
    inner = heads * headdim
    act = convolve(extended, conv_weight, conv_bias, inside)
    width = (act.shape[1] - inner) // 2
    inputs = act[:, :inner].reshape(count, block, groups, share, headdim)
    b_values = act[:, inner : inner + width].reshape(count, block, groups, width // groups)
    c_values = act[:, inner + width :].reshape(count, block, groups, width // groups)
    step_size = jax.nn.softplus(step_raw + step_bias[None, :])
    log_rate = (-step_size * jnp.exp(decay_log)[None, :]).reshape(count, block, groups, share)
    cum_decay = jnp.cumsum(log_rate, axis=1)
    return (
        inputs,
        b_values,
        c_values,
        step_size.reshape(count, block, groups, share),
        cum_decay,
        skip_gain.reshape(groups, share),
    )


def state_part(inputs, b_values, step_size, cum_decay, doc_count):
    whole = jnp.exp(cum_decay[:, -1]) * (doc_count[:, -1] == 0)[:, None, None]
    tail = (
        jnp.exp(cum_decay[:, -1:] - cum_decay) * (doc_count == doc_count[:, -1:])[:, :, None, None]
    )
    local = jnp.einsum(
        "cqgrp,cqgn->cgrpn", inputs * (tail * step_size)[..., None], b_values, precision=HIGH
    )

    def carry_step(carried, pieces):
        scale, state = carried
        factor, piece = pieces
        return ((factor * scale, factor[..., None, None] * state + piece), (scale, state))

    initial = (jnp.ones(whole.shape[1:], jnp.float32), jnp.zeros(local.shape[1:], jnp.float32))
    final, chains = lax.scan(carry_step, initial, (whole, local))
    return (final[0], final[1], chains[0], chains[1])


def out_part(
    inputs, b_values, c_values, step_size, cum_decay, skip_heads, a_chain, b_chain, doc_count
):
    block = doc_count.shape[1]
    order = jnp.arange(block, dtype=jnp.int32)
    allowed = (doc_count[:, :, None] == doc_count[:, None, :]) & (order[:, None] >= order[None, :])[
        None
    ]
    by_head = jnp.moveaxis(cum_decay, 1, -1)
    spread = by_head[..., :, None] - by_head[..., None, :]
    decay = jnp.exp(jnp.where(allowed[:, None, None], spread, -1e30))
    scores = jnp.einsum("ctgn,csgn->cgts", c_values, b_values, precision=HIGH)
    weights = scores[:, :, None] * decay * jnp.moveaxis(step_size, 1, -1)[..., None, :]
    y_diag = jnp.einsum("cgrts,csgrp->ctgrp", weights, inputs, precision=HIGH)
    head_in = jnp.exp(cum_decay) * (doc_count == 0)[:, :, None, None]
    y_carry = head_in[..., None] * jnp.einsum(
        "ctgn,cgrpn->ctgrp", c_values, b_chain, precision=HIGH
    )
    mixed = y_diag + y_carry + skip_heads[None, None, :, :, None] * inputs
    return (mixed, head_in * a_chain[:, None])


def outer_part(c_values, head_reach, state_in):
    return head_reach[..., None] * jnp.einsum(
        "ctgn,grpn->ctgrp", c_values, state_in, precision=HIGH
    )


def owner_join(earlier, later):
    factor_early, value_early = earlier
    factor_late, value_late = later
    return (factor_late * factor_early, factor_late * value_early + value_late)


def owner_prefix(pieces, reverse):
    values, factors = pieces
    scales, totals = lax.associative_scan(owner_join, (factors, values), reverse=reverse, axis=1)
    blank = jnp.zeros_like(totals[:, :1])
    if reverse:
        return jnp.concatenate([totals[:, 1:], blank], axis=1)
    return jnp.concatenate([blank, totals[:, :-1]], axis=1)


def body(
    conv_input,
    step_raw,
    step_bias,
    decay_log,
    skip_gain,
    conv_weight,
    conv_bias,
    doc_lengths,
    grad_out,
):
    length, feature_lanes = conv_input.shape
    heads = step_raw.shape[1]
    taps = conv_weight.shape[0]
    inner = grad_out.shape[1]
    headdim = inner // heads
    groups = GROUPS
    devices = lax.axis_size("ctx")
    block = math.gcd(length, 64)
    count = length // block
    border = length - taps + 1
    rim_rows = passed_along(conv_input[border:], "ctx", 1)
    extended = jnp.concatenate([rim_rows, conv_input], axis=0).astype(jnp.float32)
    positions = lax.axis_index("ctx") * length + jnp.arange(length, dtype=jnp.int32)
    inside = doc_offsets(doc_lengths, positions)
    doc_count = jnp.cumsum((inside == 0).astype(jnp.float32).reshape(count, block), axis=1)
    layout = (groups, headdim, block)
    prepared, prep_pull = jax.vjp(
        partial(prepare, inside=inside, layout=layout),
        extended,
        step_raw,
        step_bias,
        decay_log,
        skip_gain,
        conv_weight,
        conv_bias,
    )
    inputs, b_values, c_values, step_size, cum_decay, skip_heads = prepared
    summary, state_pull = jax.vjp(
        partial(state_part, doc_count=doc_count), inputs, b_values, step_size, cum_decay
    )
    decay_all, state_all, a_chain, b_chain = summary
    local_out, out_pull = jax.vjp(
        partial(out_part, doc_count=doc_count),
        inputs,
        b_values,
        c_values,
        step_size,
        cum_decay,
        skip_heads,
        a_chain,
        b_chain,
    )
    y_local, head_reach = local_out
    rates = jnp.broadcast_to(decay_all.reshape(heads, 1, 1), (heads, devices, 1))
    flat_states = state_all.reshape(heads, devices, -1)
    ready = owner_prefix(
        (
            lax.all_to_all(flat_states, "ctx", split_axis=1, concat_axis=1, tiled=True),
            lax.all_to_all(rates, "ctx", split_axis=1, concat_axis=1, tiled=True),
        ),
        False,
    )
    state_in = lax.all_to_all(ready, "ctx", split_axis=1, concat_axis=1, tiled=True).reshape(
        state_all.shape
    )
    y_state, exterior_vjp_fn = jax.vjp(outer_part, c_values, head_reach, state_in)
    mixer_out = (y_local + y_state).reshape(length, inner).astype(jnp.bfloat16)
    upstream = grad_out.astype(jnp.float32).reshape(y_local.shape)
    grad_c_outer, grad_reach, incoming_state_gradient = exterior_vjp_fn(upstream)
    pulled_out = out_pull((upstream, grad_reach))
    grad_inputs, grad_b, grad_c, grad_steps, grad_cum, grad_skip, grad_a_chain, grad_b_chain = (
        pulled_out
    )
    flat_grads = incoming_state_gradient.reshape(heads, devices, -1)
    ready = owner_prefix(
        (
            lax.all_to_all(flat_grads, "ctx", split_axis=1, concat_axis=1, tiled=True),
            lax.all_to_all(rates, "ctx", split_axis=1, concat_axis=1, tiled=True),
        ),
        True,
    )
    adjoint = lax.all_to_all(ready, "ctx", split_axis=1, concat_axis=1, tiled=True).reshape(
        state_all.shape
    )
    grad_decay_all = jnp.sum(adjoint * state_in, axis=(2, 3))
    grad_inputs_two, grad_b_two, grad_steps_two, grad_cum_two = state_pull(
        (grad_decay_all, adjoint, grad_a_chain, grad_b_chain)
    )
    pulled = prep_pull(
        (
            grad_inputs + grad_inputs_two,
            grad_b + grad_b_two,
            grad_c + grad_c_outer,
            grad_steps + grad_steps_two,
            grad_cum + grad_cum_two,
            grad_skip,
        )
    )
    grad_extended, grad_step, grad_bias, grad_log, grad_gain, grad_kernel, grad_kernel_bias = pulled
    returned = passed_along(grad_extended[: taps - 1], "ctx", -1)
    own_rows = grad_extended[taps - 1 :]
    grad_input = jnp.concatenate([own_rows[:border], own_rows[border:] + returned], axis=0).astype(
        jnp.bfloat16
    )
    totals = lax.psum(
        (
            jnp.concatenate([grad_kernel, grad_kernel_bias[None, :]], axis=0),
            jnp.stack([grad_bias, grad_log, grad_gain]),
        ),
        "ctx",
    )
    scale = (length * devices) ** (-0.5)
    return (mixer_out, grad_input, grad_step, totals[0] * scale, totals[1] * scale)


def solution(mesh):
    placed = (
        P(("groups", "ctx"), None),
        P(("groups", "ctx"), None),
        P(),
        P(),
        P(),
        P(),
        P(),
        P("groups"),
        P(("groups", "ctx"), None),
    )
    return jax.shard_map(
        body,
        mesh=mesh,
        in_specs=placed,
        out_specs=(
            P(("groups", "ctx"), None),
            P(("groups", "ctx"), None),
            P(("groups", "ctx"), None),
            P("groups", None),
            P("groups", None),
        ),
        check_vma=False,
    )
```

profile of v0, /device:TPU:0, one launch (start us, length us, event | category | flops | bytes accessed | tf_op | source)
XLA Modules:
  0.0 590.4 jit_solution(1007790423436295223)
XLA Ops:
  31.4 5.8 copy.292
  38.3 7.0 %fusion.35 = f32[2,4,16,64,128]{4,3,2,1,0:T(8,128)} fusion(f32[2,64,4,16,64]{1,4,3,2,0:T(8,128)} %copy.292, f32[2,64,4,16]{1,3,2,0:T(8,128)S(1)} %copy_multiply_fusion, f32[2,64,4,128,1]{3,2,1,0,4:T(4,128)S(1)} %bitcast.262), kind=kOutput, calls=%fused_computation.60 | convolution fusion | flops 805830656 | bytes 6586368 | tf_op jit(solution)/shard_map/jvp(cqgrp,cqgn->cgrpn)/dot_general | solution.py:71
  47.8 6.6 %while.40 = (s32[]{:T(128)}, f32[4,16]{1,0:T(4,128)S(1)}, f32[4,16,64,128]{3,2,1,0:T(8,128)S(1)}, f32[2,4,16]{2,1,0:T(4,128)S(1)}, f32[2,4,16,64,128]{4,3,2,1,0:...) while((s32[]{:T(128)}, f32[4,16]{1,0:T(4,128)S(1)}, ...), condition=%wide.region_5.6_spmd.clone, body=%wide.region_4.5_spmd.clone.sunk | while | flops 2097347 | bytes 27272616 | solution.py:81
  55.1 6.6 %all-to-all-start.1 = ((f32[64,16,1]{0,2,1:T(1,128)}), f32[64,16,1]{0,2,1:T(1,128)S(1)}, u32[]{:S(2)}, u32[]{:S(2)}) async-start(f32[64,16,1]{0,2,1:T(1,128)} %broadcast_in_dim.115), calls=%async_computation.1 | async-start | bytes 16384 | tf_op jit(solution)/shard_map/all_to_all | solution.py:187
  68.1 5.6 all-to-all-start
  76.1 38.7 %all-to-all-done = f32[64,16,512]{2,0,1:T(8,128)S(1)} async-done(((f32[64,16,512]{2,0,1:T(8,128)}), f32[64,16,512]{2,0,1:T(8,128)S(1)}, u32[]{:S(2)}, u32[]{:S(2)}) %all-to-all-start) | async-done | bytes 2097184 | tf_op jit(solution)/shard_map/all_to_all | solution.py:186
  151.5 11.2 %all-to-all-start.2 = ((f32[64,16,512]{2,0,1:T(8,128)}), f32[64,16,512]{2,0,1:T(8,128)S(1)}, u32[]{:S(2)}, u32[]{:S(2)}) async-start(f32[64,16,512]{2,0,1:T(8,128)} %concatenate.38), calls=%async_computation.2 | async-start | bytes 4194304 | tf_op jit(solution)/shard_map/all_to_all | solution.py:191
  166.1 5.9 %copy.305 = f32[2,64,4,16,64]{1,4,3,2,0:T(8,128)} copy(f32[2,64,4,16,64]{4,3,2,1,0:T(8,128)} %reshape.291) | data formatting | bytes 4194304 | tf_op jit(solution)/shard_map/reshape | solution.py:196
  172.1 31.8 %all-to-all-done.2 = f32[64,16,512]{2,0,1:T(8,128)S(1)} async-done(((f32[64,16,512]{2,0,1:T(8,128)}), f32[64,16,512]{2,0,1:T(8,128)S(1)}, u32[]{:S(2)}, u32[]{:S(2)}) %all-to-all-start.2) | async-done | bytes 2097184 | tf_op jit(solution)/shard_map/all_to_all | solution.py:191
  213.0 10.0 %fusion.22 = (f32[2,64,4,16]{1,3,2,0:T(8,128)}, f32[2,64,4,16]{1,3,2,0:T(8,128)S(1)}, f32[2,4,16,64,64]{4,3,2,1,0:T(8,128)}) fusion(f32[2,64,4,16,64]{1,4,3,2,0:T(8,128)S(1)} %copy-done, f32[4,16,64,2,64]{4,2,1,0,3:T(8,128)S(1)} %fusion.90, f32[2,4,16,64,128]{4,3,2,1,0:T(8,128)} %get-tuple-element.578, f32[2,64,4,128,1]{3,2,1,0,4:T(4,128)S(1)} %bitcast.257), kind=kOutput, calls=%fused_computation.45 | convolution fusion | flops 807387136 | bytes 10813440 | tf_op jit(solution)/shard_map/jvp(ctgn,cgrpn->ctgrp)/dot_general | solution.py:100
  235.9 11.4 %all-to-all-start.3 = ((f32[64,16,512]{2,0,1:T(8,128)}), f32[64,16,512]{2,0,1:T(8,128)}, u32[]{:S(2)}, u32[]{:S(2)}) async-start(f32[64,16,512]{2,0,1:T(8,128)} %copy.317), calls=%async_computation.3 | async-start | bytes 4194304 | tf_op jit(solution)/shard_map/all_to_all | solution.py:205
  247.4 41.0 %all-to-all-done.3 = f32[64,16,512]{2,0,1:T(8,128)} async-done(((f32[64,16,512]{2,0,1:T(8,128)}), f32[64,16,512]{2,0,1:T(8,128)}, u32[]{:S(2)}, u32[]{:S(2)}) %all-to-all-start.3) | async-done | bytes 2097184 | tf_op jit(solution)/shard_map/all_to_all | solution.py:205
  314.4 6.4 %pad.145 = f32[64,15,512]{2,0,1:T(8,128)} pad(f32[64,8,512]{2,0,1:T(8,128)} %pad_maximum_fusion.2, f32[]{:T(128)} %constant.116.clone.1), padding=0_0_0x0_0_1x0_0_0 | pad | bytes 3014660 | tf_op jit(solution)/shard_map/slice | solution.py:124
  320.8 6.5 %pad.222 = f32[64,16,512]{2,0,1:T(8,128)} pad(f32[64,8,512]{2,0,1:T(8,128)} %add.278, f32[]{:T(128)} %constant.116.clone.1), padding=0_0_0x1_0_1x0_0_0 | pad | bytes 3145732
  337.4 11.3 %all-to-all-start.4 = ((f32[64,16,512]{2,0,1:T(8,128)}), f32[64,16,512]{2,0,1:T(8,128)}, u32[]{:S(2)}, u32[]{:S(2)}) async-start(f32[64,16,512]{2,0,1:T(8,128)} %concatenate.42), calls=%async_computation.4 | async-start | bytes 4194304 | tf_op jit(solution)/shard_map/all_to_all | solution.py:210
  348.7 4.7 reshape.292
  353.6 4.9 copy.307
  359.9 9.6 %fusion.43 = (f32[2,4,16,64]{3,2,1,0:T(8,128)}, f32[2,4,16,64]{3,2,1,0:T(8,128)}, f32[2,4,16,64]{3,2,1,0:T(8,128)}, f32[2,4,64,64]{3,2,1,0:T(8,128)}) fusion(f32[2,4,16,64]{3,2,1,0:T(8,128)S(1)} %copy.291, f32[2,4,16,64]{3,2,1,0:T(8,128)S(1)} %copy.289, f32[2,4,64,64]{3,2,1,0:T(8,128)S(1)} %fusion.85, pred[2,64,64]{2,1,0:T(8,128)(4,1)S(1)} %compare_and_fusion, ...), kind=kOutput, calls=%fused_computation.79 | convolution fusion | flops 409411584 | bytes 3579904 | tf_op jit(solution)/shard_map/transpose(jvp(cgrts,csgrp->ctgrp))/dot_general | solution.py:98
  369.6 9.6 %fusion.18 = bf16[2,64,4,16,64]{1,4,3,2,0:T(8,128)(2,1)} fusion(f32[4,16,64,2,64]{4,2,1,0,3:T(8,128)S(1)} %copy-done.14, f32[2,4,16,64,64]{4,3,2,1,0:T(8,128)S(1)} %copy-done.17, f32[2,64,4,16,64]{1,4,3,2,0:T(8,128)S(1)} %copy-done.6, f32[2,64,4,16]{1,3,2,0:T(8,128)S(1)} %copy-done.39, f32[4,16]{1,0:T(4,128)S(1)} %mul.662, ...), kind=kOutput, calls=%fused_computation.39 | convolution fusion | flops 408420352 | bytes 7610624 | tf_op jit(solution)/shard_map/jvp(cgrts,csgrp->ctgrp)/dot_general | solution.py:98
  379.2 5.3 copy.304
  388.8 9.1 %convolution_bitcast_fusion.1 = f32[2,64,4,128]{3,1,2,0:T(8,128)S(1)} fusion(f32[4,16,64,128,1]{3,2,1,0,4:T(8,128)S(1)} %reshape.310, f32[2,64,4,16,64]{1,4,3,2,0:T(8,128)} %copy.305, f32[2,64,4,16]{1,3,2,0:T(8,128)S(1)} %copy-done.39), kind=kOutput, calls=%fused_computation.108 | convolution fusion | flops 805830656 | bytes 4489216 | tf_op jit(solution)/shard_map/transpose(jvp(ctgn,grpn->ctgrp))/dot_general | solution.py:108
  398.0 8.9 %fusion.70 = f32[2,4,64,128]{3,2,1,0:T(8,128)S(1)} fusion(f32[2,4,16,64,128]{4,3,2,1,0:T(8,128)} %get-tuple-element.578, f32[2,64,4,16,64]{1,4,3,2,0:T(8,128)S(1)} %copy-done.1, f32[2,64,4,16]{1,3,2,0:T(8,128)S(1)} %get-tuple-element.358), kind=kOutput, calls=%fused_computation.105 | convolution fusion | flops 805830656 | bytes 6586368 | tf_op jit(solution)/shard_map/transpose(jvp(ctgn,cgrpn->ctgrp))/dot_general | solution.py:100
  408.2 5.6 fusion.13
  424.0 10.6 %while.39 = (s32[]{:T(128)}, f32[4,16]{1,0:T(4,128)S(1)}, f32[4,16,64,128]{3,2,1,0:T(8,128)S(1)}, f32[2,4,16]{2,1,0:T(4,128)S(1)}, f32[2,4,16,64,128]{4,3,2,1,0:...) while((s32[]{:T(128)}, f32[4,16]{1,0:T(4,128)S(1)}, ...), condition=%wide.region_12.13_spmd, body=%wide.region_10.12_spmd.sunk | while | flops 2097347 | bytes 29370552 | solution.py:81
  434.7 7.9 %fusion.11 = (f32[2,64,4,16]{1,3,2,0:T(8,128)}, f32[2,4,16,64,64]{4,3,2,1,0:T(8,128)S(1)}) fusion(f32[2,64,4,16,64]{1,4,3,2,0:T(8,128)} %copy.292, f32[2,4,16,64,128]{4,3,2,1,0:T(8,128)} %get-tuple-element.274, f32[2,64,4,128,1]{3,2,1,0,4:T(4,128)S(1)} %bitcast.263), kind=kOutput, calls=%fused_computation.27 | convolution fusion | flops 806346752 | bytes 8683520 | tf_op jit(solution)/shard_map/transpose(jvp(cqgrp,cqgn->cgrpn))/dot_general | solution.py:71
  442.6 7.9 %fusion.67 = f32[2,64,4,128]{3,1,2,0:T(8,128)} fusion(f32[2,4,16,64,128]{4,3,2,1,0:T(8,128)S(1)} %copy-done.12, f32[2,64,4,16,64]{1,4,3,2,0:T(8,128)S(1)} %copy-done.7, f32[2,64,4,16]{1,3,2,0:T(8,128)S(1)} %copy-done.37), kind=kOutput, calls=%fused_computation.104 | convolution fusion | flops 805830656 | bytes 6586368 | tf_op jit(solution)/shard_map/transpose(jvp(cqgrp,cqgn->cgrpn))/dot_general | solution.py:71
  450.6 5.8 fusion.10
  456.4 6.3 %copy.327 = f32[2,64,4,16,64]{4,3,2,1,0:T(8,128)} copy(f32[2,64,4,16,64]{1,4,3,2,0:T(8,128)} %fusion.10) | data formatting | bytes 4194304 | tf_op jit(solution)/shard_map/add | solution.py:219
  462.7 4.9 reshape.297
  470.6 5.0 multiply_reduce_fusion.4
  490.9 34.8 %psum.15 = f32[3,64]{1,0:T(4,128)S(1)} all-reduce(f32[3,64]{1,0:T(4,128)S(1)} %pad_maximum_fusion.8), channel_id=1, replica_groups=mesh['groups'=2,'ctx'=16] {'ctx'}, use_global_device_ids=true, to_apply=%region_30.31 | all-reduce | flops 192 | bytes 1536 | tf_op jit(solution)/shard_map/psum | solution.py:233
  529.0 49.8 %all-reduce.33.cloned.1.call-done = f32[5,5120]{1,0:T(8,128)} async-done(((f32[5,5120]{1,0:T(8,128)}), f32[5,5120]{1,0:T(8,128)}) %all-reduce.33.cloned.1.call-update) | async-done | bytes 102416 | tf_op jit(solution)/shard_map/psum | solution.py:233
  (367 shorter events, 195.0 us)
Async XLA Ops:
  7.2 12.1 %copy-start.35 = (bf16[128,5120]{1,0:T(8,128)(2,1)S(1)}, bf16[128,5120]{1,0:T(8,128)(2,1)}, u32[]{:S(2)}) copy-start(bf16[128,5120]{1,0:T(8,128)(2,1)} %param.13) | copy-start | bytes 3932164
  8.8 10.5 %collective-permute-start = (bf16[3,5120]{1,0:T(4,128)(2,1)}, bf16[3,5120]{1,0:T(4,128)(2,1)}, u32[]{:S(2)}, u32[]{:S(2)}) collective-permute-start(bf16[3,5120]{1,0:T(4,128)(2,1)} %slice.256), channel_id=1, source_target_pairs={{0,1},{1,2},{2,3},{3,4},{4,5},{5,6},{6,7},{7,8},{8,9},{9,10},{10,1... | collective-permute-start | bytes 92168 | tf_op jit(solution)/shard_map/ppermute | solution.py:18
  13.4 7.1 %copy-start.71 = (f32[128]{0:T(128)}, f32[128]{0:T(128)S(1)}, u32[]{:S(2)}) copy-start(f32[128]{0:T(128)S(1)} %get-tuple-element.361) | copy-start | bytes 1540
  18.6 19.7 %copy-start.36 = (f32[2,64,4,16]{1,3,2,0:T(8,128)}, f32[2,64,4,16]{1,3,2,0:T(8,128)S(1)}, u32[]{:S(2)}) copy-start(f32[2,64,4,16]{1,3,2,0:T(8,128)S(1)} %copy_multiply_fusion) | copy-start | bytes 98308
  54.4 13.1 %copy-start.60 = (f32[2,4,16,1,1]{2,1,4,3,0:T(4,128)}, f32[2,4,16,1,1]{2,1,4,3,0:T(4,128)S(1)}, u32[]{:S(2)}) copy-start(f32[2,4,16,1,1]{2,1,4,3,0:T(4,128)S(1)} %get-tuple-element.577) | copy-start | bytes 1540
  55.1 13.0 %all-to-all-start.1 = ((f32[64,16,1]{0,2,1:T(1,128)}), f32[64,16,1]{0,2,1:T(1,128)S(1)}, u32[]{:S(2)}, u32[]{:S(2)}) async-start(f32[64,16,1]{0,2,1:T(1,128)} %broadcast_in_dim.115), calls=%async_computation.1 | async-start | bytes 16384 | tf_op jit(solution)/shard_map/all_to_all | solution.py:187
  68.1 46.7 %all-to-all-start = ((f32[64,16,512]{2,0,1:T(8,128)}), f32[64,16,512]{2,0,1:T(8,128)S(1)}, u32[]{:S(2)}, u32[]{:S(2)}) async-start(f32[64,16,512]{2,0,1:T(8,128)} %copy.300), calls=%async_computation | async-start | bytes 4194304 | tf_op jit(solution)/shard_map/all_to_all | solution.py:186
  116.3 8.5 %copy-start.79 = (f32[64,3,1]{0,1,2:T(4,128)S(1)}, f32[64,3,1]{0,1,2:T(4,128)}, u32[]{:S(2)}) copy-start(f32[64,3,1]{0,1,2:T(4,128)} %copy.423) | copy-start | bytes 2308
  120.2 10.7 %slice-start.1 = ((f32[64,8,512]{2,0,1:T(8,128)}), f32[64,1,512]{2,0,1:T(8,128)S(1)}, s32[]{:S(2)}) async-start(f32[64,8,512]{2,0,1:T(8,128)} %copy-done.26), calls=%async_computation.7 | async-start | bytes 262144 | tf_op jit(solution)/shard_map/slice | solution.py:121
  151.5 52.3 %all-to-all-start.2 = ((f32[64,16,512]{2,0,1:T(8,128)}), f32[64,16,512]{2,0,1:T(8,128)S(1)}, u32[]{:S(2)}, u32[]{:S(2)}) async-start(f32[64,16,512]{2,0,1:T(8,128)} %concatenate.38), calls=%async_computation.2 | async-start | bytes 4194304 | tf_op jit(solution)/shard_map/all_to_all | solution.py:191
  213.0 10.1 %copy-start.13 = (f32[4,16,64,2,64]{4,2,1,0,3:T(8,128)}, f32[4,16,64,2,64]{4,2,1,0,3:T(8,128)S(1)}, u32[]{:S(2)}) copy-start(f32[4,16,64,2,64]{4,2,1,0,3:T(8,128)S(1)} %fusion.90) | copy-start | bytes 6291460
  213.0 10.1 %copy-start.31 = (f32[2,64,4,16]{1,3,2,0:T(8,128)S(1)}, f32[2,64,4,16]{1,3,2,0:T(8,128)}, u32[]{:S(2)}) copy-start(f32[2,64,4,16]{1,3,2,0:T(8,128)} %copy-done.30) | copy-start | bytes 98308
  213.0 10.1 %copy-start.69 = (f32[2,64]{1,0:T(2,128)S(1)}, f32[2,64]{1,0:T(2,128)}, u32[]{:S(2)}) copy-start(f32[2,64]{1,0:T(2,128)} %get-tuple-element.405) | copy-start | bytes 1540
  235.9 11.4 %copy-start.59 = (f32[64,8,1]{0,2,1:T(1,128)S(1)}, f32[64,8,1]{0,2,1:T(1,128)}, u32[]{:S(2)}) copy-start(f32[64,8,1]{0,2,1:T(1,128)} %get-tuple-element.394) | copy-start | bytes 6148
  235.9 11.5 %copy-start.68 = (f32[64,7,1]{0,2,1:T(1,128)S(1)}, f32[64,7,1]{0,2,1:T(1,128)}, u32[]{:S(2)}) copy-start(f32[64,7,1]{0,2,1:T(1,128)} %get-tuple-element.392) | copy-start | bytes 5380
  235.9 52.6 %all-to-all-start.3 = ((f32[64,16,512]{2,0,1:T(8,128)}), f32[64,16,512]{2,0,1:T(8,128)}, u32[]{:S(2)}, u32[]{:S(2)}) async-start(f32[64,16,512]{2,0,1:T(8,128)} %copy.317), calls=%async_computation.3 | async-start | bytes 4194304 | tf_op jit(solution)/shard_map/all_to_all | solution.py:205
  294.2 10.5 %slice-start = ((f32[64,8,512]{2,0,1:T(8,128)}), f32[64,1,512]{2,0,1:T(8,128)S(1)}, s32[]{:S(2)}) async-start(f32[64,8,512]{2,0,1:T(8,128)} %copy-done.25), calls=%async_computation.6 | async-start | bytes 262144 | tf_op jit(solution)/shard_map/slice | solution.py:121
  337.4 76.4 %all-to-all-start.4 = ((f32[64,16,512]{2,0,1:T(8,128)}), f32[64,16,512]{2,0,1:T(8,128)}, u32[]{:S(2)}, u32[]{:S(2)}) async-start(f32[64,16,512]{2,0,1:T(8,128)} %concatenate.42), calls=%async_computation.4 | async-start | bytes 4194304 | tf_op jit(solution)/shard_map/all_to_all | solution.py:210
  348.7 230.2 %all-reduce.33.cloned.1.call-start = ((), (), s32[]{:S(2)}) async-start(), calls=%async_computation.5 | async-start | bytes 327680 | tf_op jit(solution)/shard_map/psum | solution.py:233
  359.9 9.7 %copy-start.6 = (f32[2,64,4,16,64]{1,4,3,2,0:T(8,128)S(1)}, f32[2,64,4,16,64]{1,4,3,2,0:T(8,128)}, u32[]{:S(2)}) copy-start(f32[2,64,4,16,64]{1,4,3,2,0:T(8,128)} %copy.292) | copy-start | bytes 6291460
  359.9 9.7 %copy-start.14 = (f32[4,16,64,2,64]{4,2,1,0,3:T(8,128)S(1)}, f32[4,16,64,2,64]{4,2,1,0,3:T(8,128)}, u32[]{:S(2)}) copy-start(f32[4,16,64,2,64]{4,2,1,0,3:T(8,128)} %copy-done.13) | copy-start | bytes 6291460
  359.9 9.7 %copy-start.17 = (f32[2,4,16,64,64]{4,3,2,1,0:T(8,128)S(1)}, f32[2,4,16,64,64]{4,3,2,1,0:T(8,128)}, u32[]{:S(2)}) copy-start(f32[2,4,16,64,64]{4,3,2,1,0:T(8,128)} %get-tuple-element.410) | copy-start | bytes 6291460
  359.9 9.7 %copy-start.39 = (f32[2,64,4,16]{1,3,2,0:T(8,128)S(1)}, f32[2,64,4,16]{1,3,2,0:T(8,128)}, u32[]{:S(2)}) copy-start(f32[2,64,4,16]{1,3,2,0:T(8,128)} %copy-done.38) | copy-start | bytes 98308
  388.8 9.2 %copy-start.1 = (f32[2,64,4,16,64]{1,4,3,2,0:T(8,128)S(1)}, f32[2,64,4,16,64]{1,4,3,2,0:T(8,128)}, u32[]{:S(2)}) copy-start(f32[2,64,4,16,64]{1,4,3,2,0:T(8,128)} %copy.305) | copy-start | bytes 6291460
  397.9 8.9 %copy-start.40 = (f32[2,4,64,64]{3,2,1,0:T(8,128)S(1)}, f32[2,4,64,64]{3,2,1,0:T(8,128)}, u32[]{:S(2)}) copy-start(f32[2,4,64,64]{3,2,1,0:T(8,128)} %get-tuple-element.310) | copy-start | bytes 393220
  434.7 8.0 %copy-start.7 = (f32[2,64,4,16,64]{1,4,3,2,0:T(8,128)S(1)}, f32[2,64,4,16,64]{1,4,3,2,0:T(8,128)}, u32[]{:S(2)}) copy-start(f32[2,64,4,16,64]{1,4,3,2,0:T(8,128)} %copy.292) | copy-start | bytes 6291460
  434.7 7.9 %copy-start.12 = (f32[2,4,16,64,128]{4,3,2,1,0:T(8,128)S(1)}, f32[2,4,16,64,128]{4,3,2,1,0:T(8,128)}, u32[]{:S(2)}) copy-start(f32[2,4,16,64,128]{4,3,2,1,0:T(8,128)} %get-tuple-element.274) | copy-start | bytes 12582916
  434.7 7.9 %copy-start.37 = (f32[2,64,4,16]{1,3,2,0:T(8,128)S(1)}, f32[2,64,4,16]{1,3,2,0:T(8,128)}, u32[]{:S(2)}) copy-start(f32[2,64,4,16]{1,3,2,0:T(8,128)} %copy-done.36) | copy-start | bytes 98308
  442.6 7.9 %copy-start.2 = (f32[2,64,4,16,64]{1,4,3,2,0:T(8,128)S(1)}, f32[2,64,4,16,64]{1,4,3,2,0:T(8,128)}, u32[]{:S(2)}) copy-start(f32[2,64,4,16,64]{1,4,3,2,0:T(8,128)} %copy.305) | copy-start | bytes 6291460
  442.6 7.9 %copy-start.24 = (bf16[2,64,4,16,64]{1,4,3,2,0:T(8,128)(2,1)S(1)}, bf16[2,64,4,16,64]{1,4,3,2,0:T(8,128)(2,1)}, u32[]{:S(2)}) copy-start(bf16[2,64,4,16,64]{1,4,3,2,0:T(8,128)(2,1)} %copy.307) | copy-start | bytes 3145732
  462.7 7.8 %copy-start.4 = (f32[131,5120]{1,0:T(8,128)S(1)}, f32[131,5120]{1,0:T(8,128)}, u32[]{:S(2)}) copy-start(f32[131,5120]{1,0:T(8,128)} %copy-done.3) | copy-start | bytes 8048644
  482.4 98.1 %collective-permute-start.1 = (f32[3,5120]{1,0:T(4,128)S(1)}, f32[3,5120]{1,0:T(4,128)S(1)}, u32[]{:S(2)}, u32[]{:S(2)}) collective-permute-start(f32[3,5120]{1,0:T(4,128)S(1)} %pad_add_fusion.3), channel_id=1, source_target_pairs={{1,0},{2,1},{3,2},{4,3},{5,4},{6,5},{7,6},{8,7},{9,8},{10,9},{11,1... | collective-permute-start | bytes 184328 | tf_op jit(solution)/shard_map/ppermute | solution.py:18
  (66 other events, 241.7 us)
Sparse Core Ops, SparseCore 0:
  488.8 89.9 all-reduce.32
where the time goes:
time: 601 us; the launch traced here: 590 us
  local copies, waits for them, and re-layouts  166 us (28%)
  waiting for transfers between devices  162 us (27%)
  matrix products  91.4 us (15%)
  other arithmetic  69.4 us (12%)
  starting transfers between devices  50.5 us (8%)
  blocking collectives  34.8 us (6%)
  between operations  15.9 us (3%)
    psum x1, waiting for transfers between devices, body(): lax.psum((jnp.concatenate([grad_kernel, grad_kernel_bias[None, :]], axis=...  49.8 us
    all_to_all x1, waiting for transfers between devices, body(): lax.all_to_all(flat_grads, 'ctx', split_axis=1, concat_axis=1, tiled=True)  41 us
    all_to_all x1, waiting for transfers between devices, body(): lax.all_to_all(flat_states, 'ctx', split_axis=1, concat_axis=1, tiled=True)  38.7 us
    psum x1, blocking collectives, body(): lax.psum((jnp.concatenate([grad_kernel, grad_kernel_bias[None, :]], axis=...  34.8 us
    all_to_all x2, waiting for transfers between devices, body(): lax.all_to_all(ready, 'ctx', split_axis=1, concat_axis=1, tiled=True)  31.8 us
    dot_general x3, matrix products, out_part(): y_diag = jnp.einsum('cgrts,csgrp->ctgrp', weights, inputs, precision=HIGH)  25 us
    dot_general x3, matrix products, out_part(): jnp.einsum('ctgn,cgrpn->ctgrp', c_values, b_chain, precision=HIGH)  24.5 us
    pad x8, local copies, waits for them, and re-layouts, owner_prefix(): lax.associative_scan(owner_join, (factors, values), reverse=reverse, axis=1)  22.9 us
  transfers between devices with their start and end apart: 8, of which 5 were waited for; matrix products, arithmetic and copies ran while one was open for 17% of the time, Pallas kernels for 0%

commit v1 on v0

v1 whole, which is shorter than its diff:
```python
import functools

import jax
import jax.numpy as jnp
from jax import lax
from jax.experimental import pallas as pl
from jax.experimental.pallas import tpu as pltpu
from jax.sharding import PartitionSpec as P

GROUPS = 4
F32 = jnp.float32
BF16 = jnp.bfloat16
NEG = -1e30
LIMIT = 12 * 1024 * 1024
STEP, CUM, TAIL, HEAD, TP, HP, WHOLE, SIG = range(8)

NN = (((1,), (0,)), ((), ()))
NT = (((1,), (1,)), ((), ()))
TN = (((0,), (0,)), ((), ()))


def mm(a, b, dims):
    return lax.dot_general(a, b, dims, preferred_element_type=F32)


def halves(a):
    high = a.astype(BF16)
    return high, (a - high.astype(F32)).astype(BF16)


def thirds(a):
    high = a.astype(BF16)
    rest = a - high.astype(F32)
    mid = rest.astype(BF16)
    return high, mid, (rest - mid.astype(F32)).astype(BF16)


def dot3(a, b, dims):
    ah, al = halves(a)
    bh, bl = halves(b)
    return mm(ah, bh, dims) + (mm(ah, bl, dims) + mm(al, bh, dims))


def spread_matrix(share, headdim):
    lanes = lax.broadcasted_iota(jnp.int32, (share, share * headdim), 1)
    rows = lax.broadcasted_iota(jnp.int32, (share, share * headdim), 0)
    return (lanes // headdim == rows).astype(BF16)


def spread(values, matrix):
    high, mid, low = thirds(values)
    return mm(high, matrix, TN) + (mm(mid, matrix, TN) + mm(low, matrix, TN))


def head_sums(products, matrix):
    high, low = halves(products)
    return mm(matrix, high, NT) + mm(matrix, low, NT)


def by_triangle(values, triangle):
    high, mid, low = thirds(values)
    return mm(high, triangle, NN) + (mm(mid, triangle, NN) + mm(low, triangle, NN))


def triangle(size, kind):
    rows = lax.broadcasted_iota(jnp.int32, (size, size), 0)
    cols = lax.broadcasted_iota(jnp.int32, (size, size), 1)
    kept = {"upto": rows <= cols, "before": rows < cols, "from": rows >= cols}[kind]
    return kept.astype(BF16)


def doc_start(position, table, docs):
    start = jnp.zeros_like(position)
    first = table[2]
    for i in range(1, docs):
        start = jnp.where(first <= position, first, start)
        first = first + table[2 + i]
    return start


def pack_kernel(s, x_ref, step_ref, *refs, share, inner, state, groups):
    outs, rims, turned = refs[:groups], refs[groups:-1], refs[-1]
    me = s[0]
    tokens = x_ref.shape[0]
    part = inner // groups
    width = part + 2 * state
    turned[...] = step_ref[...].T
    for k in range(groups):
        q = me ^ k
        xs = outs[k]
        xs[:, :part] = x_ref[:, pl.ds(pl.multiple_of(q * part, part), part)]
        xs[:, part : part + state] = x_ref[
            :, pl.ds(pl.multiple_of(inner + q * state, state), state)
        ]
        xs[:, part + state : width] = x_ref[
            :, pl.ds(pl.multiple_of(inner + (groups + q) * state, state), state)
        ]
        rims[k][...] = xs[tokens - 16 :, :width]
        raw = turned[pl.ds(pl.multiple_of(q * share, share), share), :]
        xs[:, width:] = jnp.zeros((tokens, tokens), BF16)
        for i, piece in enumerate(thirds(raw)):
            xs[i * share : (i + 1) * share, width:] = piece


def pack_grad_kernel(s, g_ref, *outs):
    part = outs[0].shape[1]
    for k, out in enumerate(outs):
        q = s[0] ^ k
        out[...] = g_ref[:, pl.ds(pl.multiple_of(q * part, part), part)]


def convolve_pair(s, first, pieces, rim, wx, wb, wc, bx, bb, bc, act_ref, dsl_ref, xall_ref, ext,
                  sizes, docs):
    me, plane = s[0], s[1]
    share, headdim, state = sizes
    part = share * headdim
    width = part + 2 * state
    tokens = pieces[0].shape[0]
    taps = wx.shape[0]
    ext[:8, :] = rim[8:]
    for k, ref in enumerate(pieces):
        place = (me & 1) ^ k
        value = ref[:, :width]
        ext[pl.ds(pl.multiple_of(8 + place * tokens, 8), tokens), :] = value.astype(F32)
        xall_ref[pl.ds(pl.multiple_of(16 + (first + place) * tokens, 16), tokens), :] = value

    for c in range(2):
        chunk = first + c
        pos = plane + chunk * tokens + lax.broadcasted_iota(jnp.int32, (tokens, 1), 0)
        inside = pos - doc_start(pos, s, docs)
        valid = [(inside >= reach).astype(F32) for reach in range(taps)]

        def convolve(lo, w_ref, b_ref, wlo, paired):
            rows = ext[c * tokens : c * tokens + tokens + 8, lo : lo + 128]
            u = jnp.zeros((tokens, 128), F32) + b_ref[:, wlo : wlo + 128]
            for k in range(taps):
                reach = taps - 1 - k
                shifted = rows[8 - reach : 8 - reach + tokens]
                if reach:
                    shifted = shifted * valid[reach]
                u = u + w_ref[k : k + 1, wlo : wlo + 128] * shifted
            sig = 1.0 / (1.0 + jnp.exp(-u))
            value = u * sig
            if paired:
                high, low = halves(value)
                value = high.astype(F32) + low.astype(F32)
            act_ref[chunk, :, lo : lo + 128] = value
            dsl_ref[chunk, :, lo : lo + 128] = sig * (1.0 + u * (1.0 - sig))

        for lo in range(0, part, 128):
            convolve(lo, wx, bx, lo, True)
        for lo in range(0, state, 128):
            convolve(part + lo, wb, bb, lo, False)
            convolve(part + state + lo, wc, bc, lo, False)


def conv_kernel(
    s, x0, x1, r2, r3, wx, wb, wc, bx, bb, bc, act_ref, dsl_ref, xall_ref, ext, *, sizes, docs
):
    rim = r2[...].astype(F32) + r3[...].astype(F32)
    convolve_pair(
        s, s[0] & 2, (x0, x1), rim, wx, wb, wc, bx, bb, bc, act_ref, dsl_ref, xall_ref, ext,
        sizes, docs,
    )

    @pl.when((s[0] & 2) == 0)
    def _():
        xall_ref[:16, :] = rim.astype(BF16)


def conv_state_kernel(
    s, x0, x1, x2, x3, r0, r1, wx, wb, wc, bx, bb, bc, hpar, act_in, dsl_in, xall_in,
    act_ref, dsl_ref, xall_ref, pay_ref, chain_ref, vec_ref,
    ext, raws, *, share, headdim, state, docs,
):
    me = s[0]
    plane = s[1]
    part = share * headdim
    width = part + 2 * state
    tokens = x0.shape[0]
    chunks = 4
    for k, ref in enumerate((x0, x1, x2, x3)):
        block = ref[: 3 * share, width:].astype(F32)
        raws[me ^ k] = block[:share] + block[share : 2 * share] + block[2 * share :]
    upper_chip = (me & 2) == 2
    inner_rim = xall_ref[2 * tokens : 2 * tokens + 16, :].astype(F32)
    rim = jnp.where(upper_chip, r0[...].astype(F32) + r1[...].astype(F32), inner_rim)

    @pl.when(upper_chip)
    def _():
        xall_ref[:16, :] = rim.astype(BF16)

    convolve_pair(
        s, (me & 2) ^ 2, (x2, x3), rim, wx, wb, wc, bx, bb, bc, act_ref, dsl_ref, xall_ref, ext,
        (share, headdim, state), docs,
    )

    bias = hpar[:, 0:1]
    rate = jnp.exp(hpar[:, 1:2])
    upper = triangle(tokens, "upto")
    before = jnp.zeros((share, 1), F32)
    cums, steps, ends = [], [], []
    for c in range(chunks):
        v = raws[c] + bias
        step = jnp.maximum(v, 0.0) + jnp.log1p(jnp.exp(-jnp.abs(v)))
        cum = by_triangle(-step * rate, upper)
        vec_ref[c, STEP] = step
        vec_ref[c, CUM] = cum
        vec_ref[c, SIG] = 1.0 / (1.0 + jnp.exp(-v))
        cums.append(cum)
        steps.append(step)
        ends.append(cum[:, tokens - 1 :])
    total = ends[0] + ends[1] + ends[2] + ends[3]
    last_plane = doc_start(plane + chunks * tokens - 1, s, docs)
    for c in range(chunks):
        base = plane + c * tokens
        pos = base + lax.broadcasted_iota(jnp.int32, (1, tokens), 1)
        start = doc_start(pos, s, docs)
        last = doc_start(base + tokens - 1, s, docs)
        cum, step, end = cums[c], steps[c], ends[c]
        vec_ref[c, TAIL] = jnp.exp(end - cum) * step * (pos >= last).astype(F32)
        vec_ref[c, HEAD] = jnp.exp(cum) * (start < base).astype(F32)
        vec_ref[c, HP] = jnp.exp(cum + before) * (start < plane).astype(F32)
        before = before + end
        vec_ref[c, TP] = (
            jnp.exp(total - before + (end - cum)) * step * (pos >= last_plane).astype(F32)
        )
        open_c = jnp.where(last < base, 1.0, 0.0)
        vec_ref[c, WHOLE] = jnp.broadcast_to(jnp.exp(end) * open_c, (share, tokens))
    matrix = spread_matrix(share, headdim)
    open_plane = jnp.where(last_plane < plane, 1.0, 0.0)
    pay_ref[state:, :] = spread(jnp.broadcast_to(jnp.exp(total) * open_plane, (share, 8)), matrix)

    carried = jnp.zeros((state, part), F32)
    for c in range(chunks):
        chain_ref[c] = carried
        weighted = act_ref[c, :, :part] * spread(vec_ref[c, TAIL], matrix)
        local = dot3(act_ref[c, :, part : part + state], weighted, TN)
        carried = carried * spread(vec_ref[c, WHOLE], matrix) + local
    pay_ref[:state, :] = carried


def grad_state_kernel(
    s, g0, g1, g2, g3, act_ref, vec_ref, pay_in, gall_ref, pay_ref, chain_ref,
    *, share, headdim, state,
):
    me = s[0]
    part = share * headdim
    chunks = 4
    for k, ref in enumerate((g0, g1, g2, g3)):
        gall_ref[me ^ k] = ref[...]
    matrix = spread_matrix(share, headdim)
    carried = jnp.zeros((state, part), F32)
    for c in range(chunks - 1, -1, -1):
        chain_ref[c] = carried
        weighted = gall_ref[c].astype(F32) * spread(vec_ref[c, HEAD], matrix)
        local = dot3(act_ref[c, :, part + state :], weighted, TN)
        carried = carried * spread(vec_ref[c, WHOLE], matrix) + local
    pay_ref[:state, :] = carried
    pay_ref[state:, :] = pay_in[state:, :]


def local_kernel(
    s, act_ref, vec_ref, gall_ref, schain, gchain, *refs, first, share, headdim, state, docs,
):
    y_ref, dx_ref, db_ref, dc_ref, flow_ref, xd_ref, wide, yd, dxd = refs[-9:]
    plane = s[1]
    part = share * headdim
    tokens = act_ref.shape[1]
    matrix = spread_matrix(share, headdim)
    lanes = lax.broadcasted_iota(jnp.int32, (tokens, 2 * headdim), 1)
    left = lanes < headdim
    to_lanes = spread_matrix(share, tokens)
    start_sums = triangle(tokens, "from")
    end_sums = triangle(tokens, "before")

    def chunk(c, carry):
        base = plane + c * tokens
        tpos = base + lax.broadcasted_iota(jnp.int32, (tokens, tokens), 0)
        spos = base + lax.broadcasted_iota(jnp.int32, (tokens, tokens), 1)
        tstart = doc_start(tpos, s, docs)
        mask = jnp.where((spos <= tpos) & (spos >= tstart), 0.0, NEG)
        b = act_ref[c, :, part : part + state]
        cc = act_ref[c, :, part + state :]
        m = dot3(cc, b, NT)
        cum = vec_ref[c, CUM]
        step = vec_ref[c, STEP]
        wide[...] = spread(cum, to_lanes)
        dm = jnp.zeros((tokens, tokens), F32)
        for pair in range(share // 2):
            lo = pair * 2 * headdim
            xp = act_ref[c, :, lo : lo + 2 * headdim]
            gp = gall_ref[c, :, lo : lo + 2 * headdim]
            zero = jnp.zeros_like(gp)
            gst = jnp.concatenate([jnp.where(left, gp, zero), jnp.where(left, zero, gp)], axis=0)
            xh, xl = halves(xp)
            factors = []
            for h in (2 * pair, 2 * pair + 1):
                diff = wide[:, h * tokens : (h + 1) * tokens] - cum[h : h + 1, :]
                factors.append(jnp.exp(diff + mask) * step[h : h + 1, :])
            dw = mm(gst, xh, NT) + mm(gst, xl, NT)
            dm = dm + dw[:tokens] * factors[0] + dw[tokens:] * factors[1]
            w = jnp.concatenate([m * factors[0], m * factors[1]], axis=0)
            wh, wl = halves(w)
            yst = mm(wh, xh, NN) + (mm(wh, xl, NN) + mm(wl, xh, NN) + mm(wl, xl, NN))
            yd[:, lo : lo + 2 * headdim] = jnp.where(left, yst[:tokens], yst[tokens:])
            dxd[:, lo : lo + 2 * headdim] = mm(wh, gst, TN) + mm(wl, gst, TN)
        head_in = spread(vec_ref[c, HEAD], matrix)
        tail = spread(vec_ref[c, TAIL], matrix)
        x = act_ref[c, :, :part]
        g = gall_ref[c].astype(F32)
        y = yd[...] + head_in * dot3(cc, schain[c], NN)
        y_ref[c] = y
        dx_tail = tail * dot3(b, gchain[c], NN)
        near = head_sums(x * dxd[...], matrix)
        away = head_sums(x * dx_tail, matrix)
        dx_ref[c] = dxd[...] + dx_tail
        xd_ref[c] = near + away
        inner = jnp.sum(schain[c] * gchain[c], axis=0, keepdims=True)
        through = head_sums(jnp.broadcast_to(inner, (8, part)), matrix)[:, :1]
        flow_ref[c] = (
            by_triangle(head_sums(g * y, matrix) - near, start_sums)
            + by_triangle(away, end_sums)
            + through * vec_ref[c, WHOLE]
        )
        dc_ref[c] = dot3(dm, b, NN) + dot3(g * head_in, schain[c], NT)
        db_ref[c] = dot3(dm, cc, TN) + dot3(x * tail, gchain[c], NT)
        return carry

    lax.fori_loop(first, first + 2, chunk, 0)


def out_kernel(
    s, one, two, act_ref, y_ref, gall_ref, vec_ref, skip, dcl_ref,
    m0, m1, m2, m3, gy_ref, in_ref, dc_ref, *, share, headdim, state,
):
    me = s[0]
    part = share * headdim
    matrix = spread_matrix(share, headdim)
    arrived = one[:state, :] + one[state : state + 1, :] * two[:state, :]
    in_ref[...] = arrived
    ih, il = halves(arrived)
    for k, out in enumerate((m0, m1, m2, m3)):
        c = me ^ k
        reach = spread(vec_ref[c, HP], matrix)
        ch, cl = halves(act_ref[c, :, part + state :])
        carry = mm(ch, ih, NN) + (mm(ch, il, NN) + mm(cl, ih, NN))
        y = reach * carry
        g = gall_ref[c].astype(F32)
        gy_ref[c] = head_sums(g * y, matrix)
        y = y + y_ref[c]
        out[...] = (y + skip[...] * act_ref[c, :, :part]).astype(BF16)
        gh, gl = halves(g * reach)
        dc_ref[c] = dcl_ref[c] + mm(gh, ih, NT) + (mm(gh, il, NT) + mm(gl, ih, NT))


def back_kernel(
    s, one, two, in_ref, pay, act_ref, dsl_ref, dxl_ref, dbl_ref, dc_ref, gy_ref, flow_ref,
    xd_ref, gall_ref, vec_ref, skip, hpar, xall_ref, du_ref, par_ref, gs_ref,
    *, share, headdim, state, docs, taps,
):
    plane = s[1]
    part = share * headdim
    tokens = act_ref.shape[1]
    chunks = 4
    matrix = spread_matrix(share, headdim)
    adjoint = one[:state, :] + one[state : state + 1, :] * two[:state, :]
    inner = jnp.sum(adjoint * in_ref[...], axis=0, keepdims=True) * pay[state : state + 1, :]
    through = head_sums(jnp.broadcast_to(inner, (8, part)), matrix)[:, :1]
    ah, al = halves(adjoint)
    rate = jnp.exp(hpar[:, 1:2])
    start_sums = triangle(tokens, "from")
    end_sums = triangle(tokens, "before")
    away = []
    g_bias = jnp.zeros((share, 1), F32)
    g_decay = jnp.zeros((share, 1), F32)
    g_skip = jnp.zeros((share, 1), F32)
    for c in range(chunks):
        x = act_ref[c, :, :part]
        g = gall_ref[c].astype(F32)
        tail = spread(vec_ref[c, TP], matrix)
        bh, bl = halves(act_ref[c, :, part : part + state])
        dx = tail * (mm(bh, ah, NN) + (mm(bh, al, NN) + mm(bl, ah, NN)))
        away.append(head_sums(x * dx, matrix))
        dx = dx + dxl_ref[c]
        xh, xl = halves(x * tail)
        db = dbl_ref[c] + mm(xh, ah, NT) + (mm(xh, al, NT) + mm(xl, ah, NT))
        du_ref[c * tokens : (c + 1) * tokens, :part] = (dx + skip[...] * g) * dsl_ref[c, :, :part]
        du_ref[c * tokens : (c + 1) * tokens, part : part + state] = (
            db * dsl_ref[c, :, part : part + state]
        )
        du_ref[c * tokens : (c + 1) * tokens, part + state :] = (
            dc_ref[c] * dsl_ref[c, :, part + state :]
        )
        g_skip = g_skip + jnp.sum(head_sums(g * x, matrix), axis=1, keepdims=True)
    for c in range(chunks):
        flow = (
            flow_ref[c] + by_triangle(gy_ref[c], start_sums) + by_triangle(away[c], end_sums)
        ) + through
        for d in range(chunks):
            if d > c:
                flow = flow + jnp.sum(gy_ref[d], axis=1, keepdims=True)
            if d < c:
                flow = flow + jnp.sum(away[d], axis=1, keepdims=True)
        step = vec_ref[c, STEP]
        grad_step = ((xd_ref[c] + away[c]) / step - rate * flow) * vec_ref[c, SIG]
        gs_ref[c] = grad_step
        g_bias = g_bias + jnp.sum(grad_step, axis=1, keepdims=True)
        g_decay = g_decay - rate * jnp.sum(flow * step, axis=1, keepdims=True)
    lane = lax.broadcasted_iota(jnp.int32, (share, 128), 1)
    heads = jnp.where(lane == 0, g_bias, jnp.where(lane == 1, g_decay, g_skip))
    width = part + 2 * state
    par_ref[...] = jnp.zeros_like(par_ref)
    par_ref[:, width : width + 128] = heads[:8]
    par_ref[:, width + 128 :] = heads[8:]
    for lo in range(0, width, 128):
        sums = [jnp.zeros((8, 128), F32) for _ in range(taps + 1)]
        for c in range(chunks):
            rows = xall_ref[c * tokens : c * tokens + tokens + 16, lo : lo + 128].astype(F32)
            pos = plane + c * tokens + lax.broadcasted_iota(jnp.int32, (tokens, 1), 0)
            inside = pos - doc_start(pos, s, docs)
            du = du_ref[c * tokens : (c + 1) * tokens, lo : lo + 128]
            for k in range(taps):
                reach = taps - 1 - k
                shifted = rows[16 - reach : 16 - reach + tokens]
                if reach:
                    shifted = shifted * (inside >= reach).astype(F32)
                sums[k] = sums[k] + jnp.sum((du * shifted).reshape(tokens // 8, 8, 128), axis=0)
            sums[taps] = sums[taps] + jnp.sum(du.reshape(tokens // 8, 8, 128), axis=0)
        for k in range(taps + 1):
            par_ref[k : k + 1, lo : lo + 128] = jnp.sum(sums[k], axis=0, keepdims=True)


def conv_back_kernel(
    s, du_ref, rim_ref, wx, wb, wc, gs_ref, o0, o1, o2, o3, ext,
    *, share, headdim, state, docs, taps,
):
    me = s[0]
    plane = s[1]
    part = share * headdim
    width = part + 2 * state
    tokens = o0.shape[0]
    chunks = 4
    ext[: chunks * tokens, :] = du_ref[...]
    ext[chunks * tokens :, :] = rim_ref[...]
    for k, out in enumerate((o0, o1, o2, o3)):
        c = me ^ k
        pos = plane + c * tokens + lax.broadcasted_iota(jnp.int32, (tokens, 1), 0)
        valid = []
        for reach in range(1, taps):
            ahead = pos + reach
            valid.append((ahead - doc_start(ahead, s, docs) >= reach).astype(F32))
        first = pl.multiple_of(c * tokens, tokens)
        for lo in range(0, width, 128):
            rows = ext[pl.ds(first, tokens + 8), lo : lo + 128]
            if lo < part:
                w = wx[:, lo : lo + 128]
            elif lo < part + state:
                w = wb[:, lo - part : lo - part + 128]
            else:
                w = wc[:, lo - part - state : lo - part - state + 128]
            total = w[taps - 1 : taps] * rows[:tokens]
            for reach in range(1, taps):
                k_tap = taps - 1 - reach
                total = total + w[k_tap : k_tap + 1] * (
                    rows[reach : reach + tokens] * valid[reach - 1]
                )
            out[:, lo : lo + 128] = total.astype(BF16)
        out[:, width:] = jnp.zeros((tokens, tokens), BF16)
        for i, piece in enumerate(thirds(gs_ref[c])):
            out[i * share : (i + 1) * share, width:] = piece


def join_kernel(s, p0, p1, p2, p3, out_ref):
    part = p0.shape[1]
    for k, ref in enumerate((p0, p1, p2, p3)):
        q = s[0] ^ k
        out_ref[:, pl.ds(pl.multiple_of(q * part, part), part)] = ref[...]


def join_grad_kernel(s, p0, p1, p2, p3, out_ref, gs_ref, turned, *, share, inner, state, groups):
    part = inner // groups
    for k, ref in enumerate((p0, p1, p2, p3)):
        q = s[0] ^ k
        out_ref[:, pl.ds(pl.multiple_of(q * part, part), part)] = ref[:, :part]
        out_ref[:, pl.ds(pl.multiple_of(inner + q * state, state), state)] = ref[
            :, part : part + state
        ]
        out_ref[:, pl.ds(pl.multiple_of(inner + (groups + q) * state, state), state)] = ref[
            :, part + state : part + 2 * state
        ]
        block = ref[: 3 * share, part + 2 * state :].astype(F32)
        turned[pl.ds(pl.multiple_of(q * share, share), share), :] = (
            block[:share] + block[share : 2 * share] + block[2 * share :]
        )
    gs_ref[...] = turned[...].T


def join_params_kernel(
    s, p0, p1, p2, p3, conv_ref, head_ref, turned, *, share, inner, state, groups, scale
):
    part = inner // groups
    width = part + 2 * state
    rows = conv_ref.shape[0]
    for k, ref in enumerate((p0, p1, p2, p3)):
        q = s[0] ^ k
        conv_ref[:, pl.ds(pl.multiple_of(q * part, part), part)] = ref[:rows, :part] * scale
        conv_ref[:, pl.ds(pl.multiple_of(inner + q * state, state), state)] = (
            ref[:rows, part : part + state] * scale
        )
        conv_ref[:, pl.ds(pl.multiple_of(inner + (groups + q) * state, state), state)] = (
            ref[:rows, part + state : width] * scale
        )
        turned[pl.ds(pl.multiple_of(q * share, 8), 8), :] = ref[:, width : width + 128]
        turned[pl.ds(pl.multiple_of(q * share + 8, 8), 8), :] = ref[:, width + 128 :]
    head_ref[...] = turned[...].T[: head_ref.shape[0], :] * scale


def call(kernel, table, operands, specs, outs, scratch=(), name=None, vmem=True, aliases=None):
    here = pl.BlockSpec(memory_space=pltpu.VMEM)
    in_specs = [here if spec is None else spec for spec in specs]
    return pl.pallas_call(
        kernel,
        out_shape=[
            pltpu.VMEM(shape, kind) if vmem else jax.ShapeDtypeStruct(shape, kind)
            for shape, kind in outs
        ],
        grid_spec=pltpu.PrefetchScalarGridSpec(
            num_scalar_prefetch=1,
            grid=(1,),
            in_specs=in_specs,
            out_specs=[here] * len(outs),
            scratch_shapes=[pltpu.VMEM(shape, kind) for shape, kind in scratch],
        ),
        compiler_params=pltpu.CompilerParams(vmem_limit_bytes=LIMIT),
        name=name,
        input_output_aliases=aliases or {},
    )(table, *operands)


def swapped(value, bits):
    count = lax.axis_size("ctx")
    return lax.ppermute(value, "ctx", [(i, i ^ bits) for i in range(count)])


def shifted(value, steps):
    count = lax.axis_size("ctx")
    pairs = [(i, i + steps) for i in range(count) if 0 <= i + steps < count]
    return lax.ppermute(value, "ctx", pairs)


def after(value, *others):
    return lax.optimization_barrier((value, *others))[0]


def near_of(payload, state, direction, planes):
    near = shifted(payload, direction * GROUPS)
    covered, window = 1, planes // 2
    while 2 * covered < window:
        far = shifted(near, direction * GROUPS * covered)
        factor = near[state : state + 1]
        near = jnp.concatenate(
            [near[:state] + factor * far[:state], near[state:] * far[state:]], axis=0
        )
        covered *= 2
    return near, covered


def body(
    conv_input, step_raw, step_bias, decay_log, skip_gain, conv_weight, conv_bias, doc_lengths,
    grad_out,
):
    tokens, channels = conv_input.shape
    heads = step_raw.shape[1]
    taps = conv_weight.shape[0]
    inner = grad_out.shape[1]
    headdim = inner // heads
    groups = GROUPS
    share = heads // groups
    state = (channels - inner) // (2 * groups)
    part = inner // groups
    width = part + 2 * state
    docs = doc_lengths.shape[0]
    devices = lax.axis_size("ctx")
    planes = devices // groups
    me = lax.axis_index("ctx")
    sizes = dict(share=share, headdim=headdim, state=state)
    table = jnp.concatenate(
        [
            jnp.stack([me % groups, (me // groups) * (groups * tokens)]).astype(jnp.int32),
            doc_lengths,
        ]
    )
    hpar = jnp.pad(
        jnp.stack([step_bias, decay_log, skip_gain], axis=1), ((0, 0), (0, 128 - 3))
    )
    skips = jnp.repeat(skip_gain, headdim)[None, :]
    bias_row = conv_bias[None, :]
    hpar_spec = pl.BlockSpec((share, 128), lambda i, s: (s[0], 0))
    skip_spec = pl.BlockSpec((1, part), lambda i, s: (0, s[0]))
    b_first = inner // state

    def column_specs(rows):
        return [
            pl.BlockSpec((rows, part), lambda i, s: (0, s[0])),
            pl.BlockSpec((rows, state), lambda i, s: (0, b_first + s[0])),
            pl.BlockSpec((rows, state), lambda i, s: (0, b_first + groups + s[0])),
        ]

    shapes = dict(share=share, inner=inner, state=state, groups=groups)
    packed = call(
        functools.partial(pack_kernel, **shapes),
        table,
        [conv_input, step_raw],
        [None] * 2,
        [((tokens, width + tokens), BF16)] * groups + [((16, width), BF16)] * groups,
        [((heads, tokens), F32)],
        name="pack",
    )
    xs, edges = packed[:groups], packed[groups:]
    gs = call(
        pack_grad_kernel, table, [grad_out], [None], [((tokens, part), BF16)] * groups,
        name="pack_grad",
    )
    xr = [xs[0]] + [swapped(xs[k], k) for k in range(1, groups)]
    rims = []
    for k in range(groups):
        pairs = []
        for i in range(devices):
            source = i - 1 - i % 2 if k >= 2 else i - 1 - i % groups
            if source >= 0 and (source % groups) ^ (i % groups) == k:
                pairs.append((source, i))
        rims.append(lax.ppermute(edges[k], "ctx", pairs))
    gr = [gs[0]] + [swapped(gs[k], k) for k in range(1, groups)]
    conv_shapes = [
        ((groups, tokens, width), F32),
        ((groups, tokens, width), F32),
        ((groups * tokens + 16, width), BF16),
    ]
    conv_specs = column_specs(taps) + column_specs(1)
    conv_params = [conv_weight] * 3 + [bias_row] * 3
    ext_shape = ((2 * tokens + 8, width), F32)
    act, dsl, xall = call(
        functools.partial(conv_kernel, docs=docs, sizes=(share, headdim, state)),
        table,
        [xr[0], xr[1], rims[2], rims[3]] + conv_params,
        [None] * 4 + conv_specs,
        conv_shapes,
        [ext_shape],
        name="conv",
    )
    act, dsl, xall, spay, schain, vec = call(
        functools.partial(conv_state_kernel, docs=docs, **sizes),
        table,
        xr + rims[:2] + conv_params + [hpar, act, dsl, xall],
        [None] * 6 + conv_specs + [hpar_spec] + [None] * 3,
        conv_shapes
        + [
            ((state + 8, part), F32),
            ((groups, state, part), F32),
            ((groups, 8, share, tokens), F32),
        ],
        [ext_shape, ((groups, share, tokens), F32)],
        name="conv_state",
        aliases={14: 0, 15: 1, 16: 2},
    )
    s_near, covered = near_of(spay, state, 1, planes)
    gall, gpay, gchain = call(
        functools.partial(grad_state_kernel, **sizes),
        table,
        gr + [act, vec, spay],
        [None] * 7,
        [
            ((groups, tokens, part), BF16),
            ((state + 8, part), F32),
            ((groups, state, part), F32),
        ],
        name="grad_state",
    )
    g_near, _ = near_of(gpay, state, -1, planes)
    local_shapes = [
        ((groups, tokens, part), F32),
        ((groups, tokens, part), F32),
        ((groups, tokens, state), F32),
        ((groups, tokens, state), F32),
        ((groups, share, tokens), F32),
        ((groups, share, tokens), F32),
    ]
    locals_ = []
    for first in (0, 2):
        locals_ = call(
            functools.partial(local_kernel, first=first, docs=docs, **sizes),
            table,
            [act, vec, gall, schain, gchain] + list(locals_),
            [None] * (5 + len(locals_)),
            local_shapes,
            [((tokens, share * tokens), F32)] + [((tokens, part), F32)] * 2,
            name="local",
            aliases={6 + i: i for i in range(len(locals_))},
        )
        if first == 0:
            s_far = shifted(after(s_near, locals_[4]), GROUPS * covered)
        else:
            g_far = shifted(after(g_near, locals_[4]), -GROUPS * covered)
    y_local, dx_local, db_local, dc_local, flow, xd = locals_
    *mixed, gy, state_in, dc = call(
        functools.partial(out_kernel, **sizes),
        table,
        [s_near, s_far, act, y_local, gall, vec, skips, dc_local],
        [None] * 6 + [skip_spec, None],
        [((tokens, part), BF16)] * groups
        + [
            ((groups, share, tokens), F32),
            ((state, part), F32),
            ((groups, tokens, state), F32),
        ],
        name="out",
    )
    mr = [mixed[0]] + [swapped(mixed[k], k) for k in range(1, groups)]
    du, params, grad_steps = call(
        functools.partial(back_kernel, docs=docs, taps=taps, **sizes),
        table,
        [g_near, g_far, state_in, spay, act, dsl, dx_local, db_local, dc, gy, flow, xd, gall, vec,
         skips, hpar, xall],
        [None] * 14 + [skip_spec, hpar_spec, None],
        [
            ((groups * tokens, width), F32),
            ((8, width + 256), F32),
            ((groups, share, tokens), F32),
        ],
        name="back",
    )
    rim_back = shifted(du[:8], -groups)
    rim_back, *mr = lax.optimization_barrier((rim_back, *mr))
    back = call(
        functools.partial(conv_back_kernel, docs=docs, taps=taps, **sizes),
        table,
        [du, rim_back] + [conv_weight] * 3 + [grad_steps],
        [None] * 2 + column_specs(taps) + [None],
        [((tokens, width + tokens), BF16)] * groups,
        [((groups * tokens + 8, width), F32)],
        name="conv_back",
    )
    br = [back[0]] + [swapped(back[k], k) for k in range(1, groups)]
    params = after(params, back[1])
    step = groups
    while step < devices:
        params = params + swapped(params, step)
        step *= 2
    pr = [params] + [swapped(params, k) for k in range(1, groups)]
    (mixer_out,) = call(
        join_kernel, table, mr, [None] * groups, [((tokens, inner), BF16)], name="join_out",
        vmem=False,
    )
    grad_conv, grad_heads = call(
        functools.partial(join_params_kernel, scale=(tokens * devices) ** (-0.5), **shapes),
        table,
        pr,
        [None] * groups,
        [((taps + 1, channels), F32), ((3, heads), F32)],
        [((heads, 128), F32)],
        name="join_params",
        vmem=False,
    )
    grad_input, grad_step = call(
        functools.partial(join_grad_kernel, **shapes),
        table,
        br,
        [None] * groups,
        [((tokens, channels), BF16), ((tokens, heads), F32)],
        [((heads, tokens), F32)],
        name="join_grad",
        vmem=False,
    )
    return mixer_out, grad_input, grad_step, grad_conv, grad_heads


def solution(mesh):
    rows = P(("groups", "ctx"), None)
    return jax.shard_map(
        body,
        mesh=mesh,
        in_specs=(rows, rows, P(), P(), P(), P(), P(), P("groups"), rows),
        out_specs=(rows, rows, rows, P("groups", None), P("groups", None)),
        check_vma=False,
    )
```

time: 601 us -> 144 us (0.24); the launches traced: 590 us -> 143 us
  waiting for transfers between devices: 162 us -> 16 us
  local copies, waits for them, and re-layouts: 166 us -> 23.2 us
  matrix products: 91.4 us -> 0 us
  other arithmetic: 69.4 us -> 0.76 us
  Pallas kernels: 0 us -> 57.9 us
  blocking collectives: 34.8 us -> 0 us
  between operations: 15.9 us -> 1.15 us
  starting transfers between devices: 50.5 us -> 43.6 us
    all_to_all x5 -> x0, waiting for transfers between devices: 112 us -> none  [the longest x1 41 us: body(): lax.all_to_all(flat_grads, 'ctx', split_axis=1, concat_axis=1, tiled=True)]
    dot_general x15 -> x0, matrix products: 91.4 us -> none  [the longest x3 25 us: out_part(): y_diag = jnp.einsum('cgrts,csgrp->ctgrp', weights, inputs, precision=HIGH)]
    pallas_call x0 -> x13, Pallas kernels: none -> 57.9 us  [call(): pl.pallas_call(kernel, out_shape=[pltpu.VMEM(shape, kind) if vmem else ja...]
    reshape x24 -> x0, local copies, waits for them, and re-layouts: 53.6 us -> none  [the longest x4 18.8 us: body(): upstream = grad_out.astype(jnp.float32).reshape(y_local.shape)]
    psum x1 -> x0, waiting for transfers between devices: 49.8 us -> none  [body(): lax.psum((jnp.concatenate([grad_kernel, grad_kernel_bias[None, :]], axis=...]
    all_to_all x5 -> x0, starting transfers between devices: 46.1 us -> none  [the longest x2 22.5 us: body(): lax.all_to_all(ready, 'ctx', split_axis=1, concat_axis=1, tiled=True)]
    ppermute x2 -> x26, starting transfers between devices: 4.37 us -> 43.6 us  [the longest x17 26.8 us: swapped(): return lax.ppermute(value, 'ctx', [(i, i ^ bits) for i in range(count)])]
    psum x1 -> x0, blocking collectives: 34.8 us -> none  [body(): lax.psum((jnp.concatenate([grad_kernel, grad_kernel_bias[None, :]], axis=...]
  transfers between devices with their start and end apart: 8 -> 26, of which waited for: 5 -> 6; matrix products, arithmetic and copies ran while one was open for 17% -> 1% of each run, Pallas kernels for 0% -> 36%
where the time goes in v1:
time: 144 us; the launch traced here: 143 us
  Pallas kernels  57.9 us (40%)
  starting transfers between devices  43.6 us (30%)
  local copies, waits for them, and re-layouts  23.2 us (16%)
  waiting for transfers between devices  16 us (11%)
    pallas_call x13, Pallas kernels, call(): pl.pallas_call(kernel, out_shape=[pltpu.VMEM(shape, kind) if vmem else ja...  57.9 us
    ppermute x17, starting transfers between devices, swapped(): return lax.ppermute(value, 'ctx', [(i, i ^ bits) for i in range(count)])  26.8 us
    unnamed x78, local copies, waits for them, and re-layouts  21.6 us
    ppermute x5, starting transfers between devices, shifted(): return lax.ppermute(value, 'ctx', pairs)  14.2 us
    ppermute x17, waiting for transfers between devices, swapped(): return lax.ppermute(value, 'ctx', [(i, i ^ bits) for i in range(count)])  10.6 us
    ppermute x5, waiting for transfers between devices, shifted(): return lax.ppermute(value, 'ctx', pairs)  5.38 us
  transfers between devices with their start and end apart: 26, of which 6 were waited for; matrix products, arithmetic and copies ran while one was open for 1% of the time, Pallas kernels for 36%

profile of v1, /device:TPU:0, one launch (start us, length us, event | category | flops | bytes accessed | tf_op | source)
XLA Modules:
  0.0 142.7 jit_solution(16280778889823431640)
XLA Ops:
  3.7 1.5 %pack.1 = (bf16[128,1408]{1,0:T(8,128)(2,1)S(1)}, bf16[128,1408]{1,0:T(8,128)(2,1)S(1)}, bf16[128,1408]{1,0:T(8,128)(2,1)}, bf16[128,1408]{1,0:T(8,128)(2,1)}, b...) custom-call(s32[6]{0:T(128)S(1)} %pad_add_fusion.s, ...), custom_call_target="tpu_custom_call" | custom-call | tf_op jit(solution)/shard_map/pack/pallas_call | solution.py:522
  5.7 2.5 %collective-permute-start.4 = (bf16[128,1408]{1,0:T(8,128)(2,1)}, bf16[128,1408]{1,0:T(8,128)(2,1)}, u32[]{:S(2)}, u32[]{:S(2)}) collective-permute-start(bf16[128,1408]{1,0:T(8,128)(2,1)} %get-tuple-element.73), channel_id=1, source_target_pairs={{0,2},{1,3},{2,0},{3,1},{4,6},{5,7},{6,4},{7,5},{8,10},{9,11},{10,... | collective-permute-start | bytes 1081352 | tf_op jit(solution)/shard_map/ppermute | solution.py:543
  12.2 1.5 %pack_grad.1 = (bf16[128,1024]{1,0:T(8,128)(2,1)S(1)}, bf16[128,1024]{1,0:T(8,128)(2,1)}, bf16[128,1024]{1,0:T(8,128)(2,1)}, bf16[128,1024]{1,0:T(8,128)(2,1)}) custom-call(s32[6]{0:T(128)S(1)} %pad_add_fusion.s, bf16[128,4096]{1,0:T(8,128)(2,1)S(1)} %copy-done.19), custom_call_target="tpu_custom_call" | custom-call | tf_op jit(solution)/shard_map/pack_grad/pallas_call | solution.py:522
  14.4 10.6 %collective-permute-start = (bf16[128,1024]{1,0:T(8,128)(2,1)}, bf16[128,1024]{1,0:T(8,128)(2,1)}, u32[]{:S(2)}, u32[]{:S(2)}) collective-permute-start(bf16[128,1024]{1,0:T(8,128)(2,1)} %get-tuple-element.68), channel_id=1, source_target_pairs={{0,1},{1,0},{2,3},{3,2},{4,5},{5,4},{6,7},{7,6},{8,9},{9,8},{10,11... | collective-permute-start | bytes 786440 | tf_op jit(solution)/shard_map/ppermute | solution.py:543
  25.1 2.8 %collective-permute-start.1 = (bf16[128,1024]{1,0:T(8,128)(2,1)}, bf16[128,1024]{1,0:T(8,128)(2,1)}, u32[]{:S(2)}, u32[]{:S(2)}) collective-permute-start(bf16[128,1024]{1,0:T(8,128)(2,1)} %get-tuple-element.69), channel_id=1, source_target_pairs={{0,2},{1,3},{2,0},{3,1},{4,6},{5,7},{6,4},{7,5},{8,10},{9,11},{10,... | collective-permute-start | bytes 786440 | tf_op jit(solution)/shard_map/ppermute | solution.py:543
  28.0 2.4 %conv.1 = (f32[4,128,1280]{2,1,0:T(8,128)S(1)}, f32[4,128,1280]{2,1,0:T(8,128)S(1)}, bf16[528,1280]{1,0:T(8,128)(2,1)S(1)}) custom-call(s32[6]{0:T(128)S(1)} %pad_add_fusion.s, bf16[128,1408]{1,0:T(8,128)(2,1)S(1)} %get-tuple-element.71.x0, bf16[128,1408]{1,0:T(8,128)(2,1)S(1)} %collective-permute-done.3.x1, bf16[16,1280]{1,0:T(8,128)(2,1)S(1)} %collective-permute-done.8.r2, ...), custom_call_target="tpu_custom_call" | custom-call | tf_op jit(solution)/shard_map/conv/pallas_call | solution.py:522
  34.0 6.8 %conv_state.1 = (f32[4,128,1280]{2,1,0:T(8,128)S(1)}, f32[4,128,1280]{2,1,0:T(8,128)S(1)}, bf16[528,1280]{1,0:T(8,128)(2,1)S(1)}, f32[136,1024]{1,0:T(8,128)S(1)...) custom-call(s32[6]{0:T(128)S(1)} %pad_add_fusion.s, ...), custom_call_target="tpu_custom_call", output_to_operand_aliasing={{0}: (14, {}), {1}: (15, {}), {2}: (16, {})} | custom-call | tf_op jit(solution)/shard_map/conv_state/pallas_call | solution.py:522
  40.9 1.5 %copy-done.3 = f32[4,128,1280]{2,1,0:T(8,128)} copy-done((f32[4,128,1280]{2,1,0:T(8,128)}, f32[4,128,1280]{2,1,0:T(8,128)S(1)}, u32[]{:S(2)}) %copy-start.3) | copy-done | bytes 2621464
  43.5 4.3 %collective-permute-start.12 = (f32[136,1024]{1,0:T(8,128)S(1)}, f32[136,1024]{1,0:T(8,128)}, u32[]{:S(2)}, u32[]{:S(2)}) collective-permute-start(f32[136,1024]{1,0:T(8,128)S(1)} %get-tuple-element.84.pay_in.pay), channel_id=1, source_target_pairs={{0,4},{1,5},{2,6},{3,7},{4,8},{5,9},{6,10},{7,11},{8,12},{9,13},{1... | collective-permute-start | bytes 1671176 | tf_op jit(solution)/shard_map/ppermute | solution.py:549
  47.8 4.8 %grad_state.1 = (bf16[4,128,1024]{2,1,0:T(8,128)(2,1)S(1)}, f32[136,1024]{1,0:T(8,128)S(1)}, f32[4,128,1024]{2,1,0:T(8,128)S(1)}) custom-call(s32[6]{0:T(128)S(1)} %pad_add_fusion.s, bf16[128,1024]{1,0:T(8,128)(2,1)S(1)} %copy-done.26, bf16[128,1024]{1,0:T(8,128)(2,1)} %collective-permute-done.g1, bf16[128,1024]{1,0:T(8,128)(2,1)} %collective-permute-done.1.g2, ...), custom_call_target="tpu_custom_call" | custom-call | tf_op jit(solution)/shard_map/grad_state/pallas_call | solution.py:522
  52.6 1.5 %collective-permute-start.10 = (f32[136,1024]{1,0:T(8,128)S(1)}, f32[136,1024]{1,0:T(8,128)}, u32[]{:S(2)}, u32[]{:S(2)}) collective-permute-start(f32[136,1024]{1,0:T(8,128)S(1)} %get-tuple-element.85), channel_id=1, source_target_pairs={{4,0},{5,1},{6,2},{7,3},{8,4},{9,5},{10,6},{11,7},{12,8},{13,9},{1... | collective-permute-start | bytes 1671176 | tf_op jit(solution)/shard_map/ppermute | solution.py:549
  54.1 9.0 %local.2 = (f32[4,128,1024]{2,1,0:T(8,128)S(1)}, f32[4,128,1024]{2,1,0:T(8,128)S(1)}, f32[4,128,128]{2,1,0:T(8,128)S(1)}, f32[4,128,128]{2,1,0:T(8,128)S(1)}, f3...) custom-call(s32[6]{0:T(128)S(1)} %pad_add_fusion.s, f32[4,128,1280]{2,1,0:T(8,128)S(1)} %get-tuple-element.82.act_ref, ...), custom_call_target="tpu_custom_call" | custom-call | tf_op jit(solution)/shard_map/local/pallas_call | solution.py:522
  63.1 5.4 %collective-permute-start.13 = (f32[136,1024]{1,0:T(8,128)}, f32[136,1024]{1,0:T(8,128)}, u32[]{:S(2)}, u32[]{:S(2)}) collective-permute-start(f32[136,1024]{1,0:T(8,128)} %collective-permute-done.12.one), channel_id=1, source_target_pairs={{0,4},{1,5},{2,6},{3,7},{4,8},{5,9},{6,10},{7,11},{8,12},{9,13},{1... | collective-permute-start | bytes 1671176 | tf_op jit(solution)/shard_map/ppermute | solution.py:549
  68.5 9.0 %local.3 = (f32[4,128,1024]{2,1,0:T(8,128)S(1)}, f32[4,128,1024]{2,1,0:T(8,128)S(1)}, f32[4,128,128]{2,1,0:T(8,128)S(1)}, f32[4,128,128]{2,1,0:T(8,128)S(1)}, f3...) custom-call(s32[6]{0:T(128)S(1)} %pad_add_fusion.s, ...), custom_call_target="tpu_custom_call", output_to_operand_aliasing={{0}: (6, {}), {1}: (7, {}), {2}: (8, {}), {3}: (9, {}), {4}... | custom-call | tf_op jit(solution)/shard_map/local/pallas_call | solution.py:522
  77.5 1.3 copy-done.5
  78.8 1.3 copy-done.7
  82.8 1.5 %collective-permute-start.11 = (f32[136,1024]{1,0:T(8,128)}, f32[136,1024]{1,0:T(8,128)}, u32[]{:S(2)}, u32[]{:S(2)}) collective-permute-start(f32[136,1024]{1,0:T(8,128)} %collective-permute-done.10.one), channel_id=1, source_target_pairs={{4,0},{5,1},{6,2},{7,3},{8,4},{9,5},{10,6},{11,7},{12,8},{13,9},{1... | collective-permute-start | bytes 1671176 | tf_op jit(solution)/shard_map/ppermute | solution.py:549
  87.0 1.6 %copy-done.6 = f32[4,128,1024]{2,1,0:T(8,128)S(1)} copy-done((f32[4,128,1024]{2,1,0:T(8,128)S(1)}, f32[4,128,1024]{2,1,0:T(8,128)}, u32[]{:S(2)}) %copy-start.6) | copy-done | bytes 2097176
  89.6 6.2 %out.1 = (bf16[128,1024]{1,0:T(8,128)(2,1)S(1)}, bf16[128,1024]{1,0:T(8,128)(2,1)S(1)}, bf16[128,1024]{1,0:T(8,128)(2,1)S(1)}, bf16[128,1024]{1,0:T(8,128)(2,1)S...) custom-call(s32[6]{0:T(128)S(1)} %pad_add_fusion.s, ...), custom_call_target="tpu_custom_call" | custom-call | tf_op jit(solution)/shard_map/out/pallas_call | solution.py:522
  100.4 9.4 %back.1 = (f32[512,1280]{1,0:T(8,128)S(1)}, f32[8,1536]{1,0:T(8,128)S(1)}, f32[4,16,128]{2,1,0:T(8,128)S(1)}) custom-call(s32[6]{0:T(128)S(1)} %pad_add_fusion.s, f32[136,1024]{1,0:T(8,128)} %collective-permute-done.10.one, f32[136,1024]{1,0:T(8,128)} %collective-permute-done.11.two, f32[128,1024]{1,0:T(8,128)S(1)} %get-tuple-element.100.in_ref, ...), custom_call_target="tpu_custom_call" | custom-call | tf_op jit(solution)/shard_map/back/pallas_call | solution.py:522
  109.8 1.5 %collective-permute-start.14 = (f32[8,1280]{1,0:T(8,128)S(1)}, f32[8,1280]{1,0:T(8,128)S(1)}, u32[]{:S(2)}, u32[]{:S(2)}) collective-permute-start(f32[8,1280]{1,0:T(8,128)S(1)} %slice.3), channel_id=1, source_target_pairs={{4,0},{5,1},{6,2},{7,3},{8,4},{9,5},{10,6},{11,7},{12,8},{13,9},{1... | collective-permute-start | bytes 122888 | tf_op jit(solution)/shard_map/ppermute | solution.py:549
  111.3 4.3 %collective-permute-done.14.rim_ref = f32[8,1280]{1,0:T(8,128)S(1)} collective-permute-done((f32[8,1280]{1,0:T(8,128)S(1)}, f32[8,1280]{1,0:T(8,128)S(1)}, u32[]{:S(2)}, u32[]{:S(2)}) %collective-permute-start.14) | collective-permute-done | bytes 40992 | tf_op jit(solution)/shard_map/ppermute | solution.py:549
  115.7 2.7 %conv_back.1 = (bf16[128,1408]{1,0:T(8,128)(2,1)S(1)}, bf16[128,1408]{1,0:T(8,128)(2,1)S(1)}, bf16[128,1408]{1,0:T(8,128)(2,1)S(1)}, bf16[128,1408]{1,0:T(8,128)(2,1)S(1)}) custom-call(s32[6]{0:T(128)S(1)} %pad_add_fusion.s, f32[512,1280]{1,0:T(8,128)S(1)} %get-tuple-element.108.du_ref, f32[8,1280]{1,0:T(8,128)S(1)} %collective-permute-done.14.rim_ref, ...), custom_call_target="tpu_custom_call" | custom-call | tf_op jit(solution)/shard_map/conv_back/pallas_call | solution.py:522
  118.4 2.0 %collective-permute-start.19 = (bf16[128,1408]{1,0:T(8,128)(2,1)S(1)}, bf16[128,1408]{1,0:T(8,128)(2,1)S(1)}, u32[]{:S(2)}, u32[]{:S(2)}) collective-permute-start(bf16[128,1408]{1,0:T(8,128)(2,1)S(1)} %get-tuple-element.121), channel_id=1, source_target_pairs={{0,2},{1,3},{2,0},{3,1},{4,6},{5,7},{6,4},{7,5},{8,10},{9,11},{10,... | collective-permute-start | bytes 1081352 | tf_op jit(solution)/shard_map/ppermute | solution.py:543
  120.5 1.4 collective-permute-start.21
  121.9 2.7 %collective-permute-done.21 = f32[8,1536]{1,0:T(8,128)S(1)} collective-permute-done((f32[8,1536]{1,0:T(8,128)S(1)}, f32[8,1536]{1,0:T(8,128)S(1)}, u32[]{:S(2)}, u32[]{:S(2)}) %collective-permute-start.21) | collective-permute-done | bytes 49184 | tf_op jit(solution)/shard_map/ppermute | solution.py:543
  124.6 1.7 %collective-permute-start.22 = (f32[8,1536]{1,0:T(8,128)S(1)}, f32[8,1536]{1,0:T(8,128)S(1)}, u32[]{:S(2)}, u32[]{:S(2)}) collective-permute-start(f32[8,1536]{1,0:T(8,128)S(1)} %add.14), channel_id=1, source_target_pairs={{0,8},{1,9},{2,10},{3,11},{4,12},{5,13},{6,14},{7,15},{8,0},{9,1},... | collective-permute-start | bytes 147464 | tf_op jit(solution)/shard_map/ppermute | solution.py:543
  126.3 3.4 %collective-permute-done.22 = f32[8,1536]{1,0:T(8,128)S(1)} collective-permute-done((f32[8,1536]{1,0:T(8,128)S(1)}, f32[8,1536]{1,0:T(8,128)S(1)}, u32[]{:S(2)}, u32[]{:S(2)}) %collective-permute-start.22) | collective-permute-done | bytes 49184 | tf_op jit(solution)/shard_map/ppermute | solution.py:543
  129.8 2.2 %collective-permute-start.24 = (f32[8,1536]{1,0:T(8,128)S(1)}, f32[8,1536]{1,0:T(8,128)S(1)}, u32[]{:S(2)}, u32[]{:S(2)}) collective-permute-start(f32[8,1536]{1,0:T(8,128)S(1)} %add.15.p0), channel_id=1, source_target_pairs={{0,2},{1,3},{2,0},{3,1},{4,6},{5,7},{6,4},{7,5},{8,10},{9,11},{10,... | collective-permute-start | bytes 147464 | tf_op jit(solution)/shard_map/ppermute | solution.py:543
  132.9 1.6 %join_out.1 = bf16[128,4096]{1,0:T(8,128)(2,1)} custom-call(s32[6]{0:T(128)S(1)} %pad_add_fusion.s, bf16[128,1024]{1,0:T(8,128)(2,1)S(1)} %get-tuple-element.113.p0, bf16[128,1024]{1,0:T(8,128)(2,1)S(1)} %collective-permute-done.15.p1, bf16[128,1024]{1,0:T(8,128)(2,1)S(1)} %collective-permute-done.16.p2, bf16[128,1024]{1,0:T(8,128)(2,1)S(1)} %collective-permute-done.17.p3), custom_call_target="tpu_custom_call" | custom-call | tf_op jit(solution)/shard_map/join_out/pallas_call | solution.py:522
  134.5 4.1 %collective-permute-done.24.p2 = f32[8,1536]{1,0:T(8,128)S(1)} collective-permute-done((f32[8,1536]{1,0:T(8,128)S(1)}, f32[8,1536]{1,0:T(8,128)S(1)}, u32[]{:S(2)}, u32[]{:S(2)}) %collective-permute-start.24) | collective-permute-done | bytes 49184 | tf_op jit(solution)/shard_map/ppermute | solution.py:543
  140.2 1.7 %join_grad.1 = (bf16[128,5120]{1,0:T(8,128)(2,1)}, f32[128,64]{1,0:T(8,128)S(1)}) custom-call(s32[6]{0:T(128)S(1)} %pad_add_fusion.s, bf16[128,1408]{1,0:T(8,128)(2,1)S(1)} %get-tuple-element.119.p0, bf16[128,1408]{1,0:T(8,128)(2,1)S(1)} %collective-permute-done.18.p1, bf16[128,1408]{1,0:T(8,128)(2,1)S(1)} %collective-permute-done.19.p2, ...), custom_call_target="tpu_custom_call" | custom-call | tf_op jit(solution)/shard_map/join_grad/pallas_call | solution.py:522
  (120 shorter events, 27.3 us)
Async XLA Ops:
  0.6 27.2 %copy-start.35 = (f32[64]{0:T(128)S(1)}, f32[64]{0:T(128)}, u32[]{:S(2)}) copy-start(f32[64]{0:T(128)} %param.13) | copy-start | bytes 772
  0.6 27.2 %copy-start.36 = (f32[64]{0:T(128)S(1)}, f32[64]{0:T(128)}, u32[]{:S(2)}) copy-start(f32[64]{0:T(128)} %param.12) | copy-start | bytes 772
  0.7 27.2 %copy-start.37 = (f32[64]{0:T(128)S(1)}, f32[64]{0:T(128)}, u32[]{:S(2)}) copy-start(f32[64]{0:T(128)} %param.11) | copy-start | bytes 772
  0.7 27.3 %copy-start.9 = (f32[4,5120]{1,0:T(4,128)S(1)}, f32[4,5120]{1,0:T(4,128)}, u32[]{:S(2)}) copy-start(f32[4,5120]{1,0:T(4,128)} %wc.5) | copy-start | bytes 245764
  0.7 27.3 %copy-start.22 = (f32[5120]{0:T(1024)S(1)}, f32[5120]{0:T(1024)}, u32[]{:S(2)}) copy-start(f32[5120]{0:T(1024)} %param.15) | copy-start | bytes 61444
  5.2 25.3 %copy-start.12 = (bf16[128,1408]{1,0:T(8,128)(2,1)}, bf16[128,1408]{1,0:T(8,128)(2,1)S(1)}, u32[]{:S(2)}) copy-start(bf16[128,1408]{1,0:T(8,128)(2,1)S(1)} %get-tuple-element.71.x0) | copy-start | bytes 1081348
  5.2 22.6 %collective-permute-start.3 = (bf16[128,1408]{1,0:T(8,128)(2,1)S(1)}, bf16[128,1408]{1,0:T(8,128)(2,1)S(1)}, u32[]{:S(2)}, u32[]{:S(2)}) collective-permute-start(bf16[128,1408]{1,0:T(8,128)(2,1)S(1)} %get-tuple-element.72), channel_id=1, source_target_pairs={{0,1},{1,0},{2,3},{3,2},{4,5},{5,4},{6,7},{7,6},{8,9},{9,8},{10,11... | collective-permute-start | bytes 1081352 | tf_op jit(solution)/shard_map/ppermute | solution.py:543
  5.7 24.8 %collective-permute-start.4 = (bf16[128,1408]{1,0:T(8,128)(2,1)}, bf16[128,1408]{1,0:T(8,128)(2,1)}, u32[]{:S(2)}, u32[]{:S(2)}) collective-permute-start(bf16[128,1408]{1,0:T(8,128)(2,1)} %get-tuple-element.73), channel_id=1, source_target_pairs={{0,2},{1,3},{2,0},{3,1},{4,6},{5,7},{6,4},{7,5},{8,10},{9,11},{10,... | collective-permute-start | bytes 1081352 | tf_op jit(solution)/shard_map/ppermute | solution.py:543
  8.2 22.3 %collective-permute-start.5 = (bf16[128,1408]{1,0:T(8,128)(2,1)}, bf16[128,1408]{1,0:T(8,128)(2,1)}, u32[]{:S(2)}, u32[]{:S(2)}) collective-permute-start(bf16[128,1408]{1,0:T(8,128)(2,1)} %get-tuple-element.74), channel_id=1, source_target_pairs={{0,3},{1,2},{2,1},{3,0},{4,7},{5,6},{6,5},{7,4},{8,11},{9,10},{10,... | collective-permute-start | bytes 1081352 | tf_op jit(solution)/shard_map/ppermute | solution.py:543
  8.3 1.3 collective-permute-start.6
  9.0 2.0 %collective-permute-start.7 = (bf16[16,1280]{1,0:T(8,128)(2,1)S(1)}, bf16[16,1280]{1,0:T(8,128)(2,1)S(1)}, u32[]{:S(2)}, u32[]{:S(2)}) collective-permute-start(bf16[16,1280]{1,0:T(8,128)(2,1)S(1)} %get-tuple-element.76), channel_id=1, source_target_pairs={{3,6},{7,10},{11,14},{19,22},{23,26},{27,30}} | collective-permute-start | bytes 122888 | tf_op jit(solution)/shard_map/ppermute | solution.py:633
  10.3 4.1 %collective-permute-start.8 = (bf16[16,1280]{1,0:T(8,128)(2,1)S(1)}, bf16[16,1280]{1,0:T(8,128)(2,1)S(1)}, u32[]{:S(2)}, u32[]{:S(2)}) collective-permute-start(bf16[16,1280]{1,0:T(8,128)(2,1)S(1)} %get-tuple-element.77), channel_id=1, source_target_pairs={{1,3},{3,5},{5,7},{7,9},{9,11},{11,13},{13,15},{17,19},{19,21},{21... | collective-permute-start | bytes 122888 | tf_op jit(solution)/shard_map/ppermute | solution.py:633
  11.6 13.5 %collective-permute-start.9 = (bf16[16,1280]{1,0:T(8,128)(2,1)S(1)}, bf16[16,1280]{1,0:T(8,128)(2,1)S(1)}, u32[]{:S(2)}, u32[]{:S(2)}) collective-permute-start(bf16[16,1280]{1,0:T(8,128)(2,1)S(1)} %get-tuple-element.78), channel_id=1, source_target_pairs={{1,2},{3,4},{5,6},{7,8},{9,10},{11,12},{13,14},{17,18},{19,20},{21... | collective-permute-start | bytes 122888 | tf_op jit(solution)/shard_map/ppermute | solution.py:633
  14.4 33.4 %collective-permute-start = (bf16[128,1024]{1,0:T(8,128)(2,1)}, bf16[128,1024]{1,0:T(8,128)(2,1)}, u32[]{:S(2)}, u32[]{:S(2)}) collective-permute-start(bf16[128,1024]{1,0:T(8,128)(2,1)} %get-tuple-element.68), channel_id=1, source_target_pairs={{0,1},{1,0},{2,3},{3,2},{4,5},{5,4},{6,7},{7,6},{8,9},{9,8},{10,11... | collective-permute-start | bytes 786440 | tf_op jit(solution)/shard_map/ppermute | solution.py:543
  25.1 22.7 %collective-permute-start.1 = (bf16[128,1024]{1,0:T(8,128)(2,1)}, bf16[128,1024]{1,0:T(8,128)(2,1)}, u32[]{:S(2)}, u32[]{:S(2)}) collective-permute-start(bf16[128,1024]{1,0:T(8,128)(2,1)} %get-tuple-element.69), channel_id=1, source_target_pairs={{0,2},{1,3},{2,0},{3,1},{4,6},{5,7},{6,4},{7,5},{8,10},{9,11},{10,... | collective-permute-start | bytes 786440 | tf_op jit(solution)/shard_map/ppermute | solution.py:543
  27.8 20.0 %collective-permute-start.2 = (bf16[128,1024]{1,0:T(8,128)(2,1)}, bf16[128,1024]{1,0:T(8,128)(2,1)}, u32[]{:S(2)}, u32[]{:S(2)}) collective-permute-start(bf16[128,1024]{1,0:T(8,128)(2,1)} %get-tuple-element.70), channel_id=1, source_target_pairs={{0,3},{1,2},{2,1},{3,0},{4,7},{5,6},{6,5},{7,4},{8,11},{9,10},{10,... | collective-permute-start | bytes 786440 | tf_op jit(solution)/shard_map/ppermute | solution.py:543
  43.5 19.6 %collective-permute-start.12 = (f32[136,1024]{1,0:T(8,128)S(1)}, f32[136,1024]{1,0:T(8,128)}, u32[]{:S(2)}, u32[]{:S(2)}) collective-permute-start(f32[136,1024]{1,0:T(8,128)S(1)} %get-tuple-element.84.pay_in.pay), channel_id=1, source_target_pairs={{0,4},{1,5},{2,6},{3,7},{4,8},{5,9},{6,10},{7,11},{8,12},{9,13},{1... | collective-permute-start | bytes 1671176 | tf_op jit(solution)/shard_map/ppermute | solution.py:549
  52.6 30.1 %collective-permute-start.10 = (f32[136,1024]{1,0:T(8,128)S(1)}, f32[136,1024]{1,0:T(8,128)}, u32[]{:S(2)}, u32[]{:S(2)}) collective-permute-start(f32[136,1024]{1,0:T(8,128)S(1)} %get-tuple-element.85), channel_id=1, source_target_pairs={{4,0},{5,1},{6,2},{7,3},{8,4},{9,5},{10,6},{11,7},{12,8},{13,9},{1... | collective-permute-start | bytes 1671176 | tf_op jit(solution)/shard_map/ppermute | solution.py:549
  63.1 22.7 %collective-permute-start.13 = (f32[136,1024]{1,0:T(8,128)}, f32[136,1024]{1,0:T(8,128)}, u32[]{:S(2)}, u32[]{:S(2)}) collective-permute-start(f32[136,1024]{1,0:T(8,128)} %collective-permute-done.12.one), channel_id=1, source_target_pairs={{0,4},{1,5},{2,6},{3,7},{4,8},{5,9},{6,10},{7,11},{8,12},{9,13},{1... | collective-permute-start | bytes 1671176 | tf_op jit(solution)/shard_map/ppermute | solution.py:549
  82.8 16.0 %collective-permute-start.11 = (f32[136,1024]{1,0:T(8,128)}, f32[136,1024]{1,0:T(8,128)}, u32[]{:S(2)}, u32[]{:S(2)}) collective-permute-start(f32[136,1024]{1,0:T(8,128)} %collective-permute-done.10.one), channel_id=1, source_target_pairs={{4,0},{5,1},{6,2},{7,3},{8,4},{9,5},{10,6},{11,7},{12,8},{13,9},{1... | collective-permute-start | bytes 1671176 | tf_op jit(solution)/shard_map/ppermute | solution.py:549
  95.8 19.9 %collective-permute-start.15 = (bf16[128,1024]{1,0:T(8,128)(2,1)S(1)}, bf16[128,1024]{1,0:T(8,128)(2,1)S(1)}, u32[]{:S(2)}, u32[]{:S(2)}) collective-permute-start(bf16[128,1024]{1,0:T(8,128)(2,1)S(1)} %get-tuple-element.110), channel_id=1, source_target_pairs={{0,1},{1,0},{2,3},{3,2},{4,5},{5,4},{6,7},{7,6},{8,9},{9,8},{10,11... | collective-permute-start | bytes 786440 | tf_op jit(solution)/shard_map/ppermute | solution.py:543
  95.9 19.8 %collective-permute-start.16 = (bf16[128,1024]{1,0:T(8,128)(2,1)S(1)}, bf16[128,1024]{1,0:T(8,128)(2,1)S(1)}, u32[]{:S(2)}, u32[]{:S(2)}) collective-permute-start(bf16[128,1024]{1,0:T(8,128)(2,1)S(1)} %get-tuple-element.111), channel_id=1, source_target_pairs={{0,2},{1,3},{2,0},{3,1},{4,6},{5,7},{6,4},{7,5},{8,10},{9,11},{10,... | collective-permute-start | bytes 786440 | tf_op jit(solution)/shard_map/ppermute | solution.py:543
  97.2 18.5 %collective-permute-start.17 = (bf16[128,1024]{1,0:T(8,128)(2,1)S(1)}, bf16[128,1024]{1,0:T(8,128)(2,1)S(1)}, u32[]{:S(2)}, u32[]{:S(2)}) collective-permute-start(bf16[128,1024]{1,0:T(8,128)(2,1)S(1)} %get-tuple-element.112), channel_id=1, source_target_pairs={{0,3},{1,2},{2,1},{3,0},{4,7},{5,6},{6,5},{7,4},{8,11},{9,10},{10,... | collective-permute-start | bytes 786440 | tf_op jit(solution)/shard_map/ppermute | solution.py:543
  109.8 5.9 %collective-permute-start.14 = (f32[8,1280]{1,0:T(8,128)S(1)}, f32[8,1280]{1,0:T(8,128)S(1)}, u32[]{:S(2)}, u32[]{:S(2)}) collective-permute-start(f32[8,1280]{1,0:T(8,128)S(1)} %slice.3), channel_id=1, source_target_pairs={{4,0},{5,1},{6,2},{7,3},{8,4},{9,5},{10,6},{11,7},{12,8},{13,9},{1... | collective-permute-start | bytes 122888 | tf_op jit(solution)/shard_map/ppermute | solution.py:549
  118.4 21.9 %collective-permute-start.18 = (bf16[128,1408]{1,0:T(8,128)(2,1)S(1)}, bf16[128,1408]{1,0:T(8,128)(2,1)S(1)}, u32[]{:S(2)}, u32[]{:S(2)}) collective-permute-start(bf16[128,1408]{1,0:T(8,128)(2,1)S(1)} %get-tuple-element.120), channel_id=1, source_target_pairs={{0,1},{1,0},{2,3},{3,2},{4,5},{5,4},{6,7},{7,6},{8,9},{9,8},{10,11... | collective-permute-start | bytes 1081352 | tf_op jit(solution)/shard_map/ppermute | solution.py:543
  118.4 21.8 %collective-permute-start.19 = (bf16[128,1408]{1,0:T(8,128)(2,1)S(1)}, bf16[128,1408]{1,0:T(8,128)(2,1)S(1)}, u32[]{:S(2)}, u32[]{:S(2)}) collective-permute-start(bf16[128,1408]{1,0:T(8,128)(2,1)S(1)} %get-tuple-element.121), channel_id=1, source_target_pairs={{0,2},{1,3},{2,0},{3,1},{4,6},{5,7},{6,4},{7,5},{8,10},{9,11},{10,... | collective-permute-start | bytes 1081352 | tf_op jit(solution)/shard_map/ppermute | solution.py:543
  120.5 19.8 %collective-permute-start.20 = (bf16[128,1408]{1,0:T(8,128)(2,1)S(1)}, bf16[128,1408]{1,0:T(8,128)(2,1)S(1)}, u32[]{:S(2)}, u32[]{:S(2)}) collective-permute-start(bf16[128,1408]{1,0:T(8,128)(2,1)S(1)} %get-tuple-element.122), channel_id=1, source_target_pairs={{0,3},{1,2},{2,1},{3,0},{4,7},{5,6},{6,5},{7,4},{8,11},{9,10},{10,... | collective-permute-start | bytes 1081352 | tf_op jit(solution)/shard_map/ppermute | solution.py:543
  120.5 4.1 %collective-permute-start.21 = (f32[8,1536]{1,0:T(8,128)S(1)}, f32[8,1536]{1,0:T(8,128)S(1)}, u32[]{:S(2)}, u32[]{:S(2)}) collective-permute-start(f32[8,1536]{1,0:T(8,128)S(1)} %get-tuple-element.126), channel_id=1, source_target_pairs={{0,4},{1,5},{2,6},{3,7},{4,0},{5,1},{6,2},{7,3},{8,12},{9,13},{10,... | collective-permute-start | bytes 147464 | tf_op jit(solution)/shard_map/ppermute | solution.py:543
  124.6 5.0 %collective-permute-start.22 = (f32[8,1536]{1,0:T(8,128)S(1)}, f32[8,1536]{1,0:T(8,128)S(1)}, u32[]{:S(2)}, u32[]{:S(2)}) collective-permute-start(f32[8,1536]{1,0:T(8,128)S(1)} %add.14), channel_id=1, source_target_pairs={{0,8},{1,9},{2,10},{3,11},{4,12},{5,13},{6,14},{7,15},{8,0},{9,1},... | collective-permute-start | bytes 147464 | tf_op jit(solution)/shard_map/ppermute | solution.py:543
  129.7 2.3 %collective-permute-start.23 = (f32[8,1536]{1,0:T(8,128)S(1)}, f32[8,1536]{1,0:T(8,128)S(1)}, u32[]{:S(2)}, u32[]{:S(2)}) collective-permute-start(f32[8,1536]{1,0:T(8,128)S(1)} %add.15.p0), channel_id=1, source_target_pairs={{0,1},{1,0},{2,3},{3,2},{4,5},{5,4},{6,7},{7,6},{8,9},{9,8},{10,11... | collective-permute-start | bytes 147464 | tf_op jit(solution)/shard_map/ppermute | solution.py:543
  129.8 8.8 %collective-permute-start.24 = (f32[8,1536]{1,0:T(8,128)S(1)}, f32[8,1536]{1,0:T(8,128)S(1)}, u32[]{:S(2)}, u32[]{:S(2)}) collective-permute-start(f32[8,1536]{1,0:T(8,128)S(1)} %add.15.p0), channel_id=1, source_target_pairs={{0,2},{1,3},{2,0},{3,1},{4,6},{5,7},{6,4},{7,5},{8,10},{9,11},{10,... | collective-permute-start | bytes 147464 | tf_op jit(solution)/shard_map/ppermute | solution.py:543
  132.0 7.0 %collective-permute-start.25 = (f32[8,1536]{1,0:T(8,128)S(1)}, f32[8,1536]{1,0:T(8,128)S(1)}, u32[]{:S(2)}, u32[]{:S(2)}) collective-permute-start(f32[8,1536]{1,0:T(8,128)S(1)} %add.15.p0), channel_id=1, source_target_pairs={{0,3},{1,2},{2,1},{3,0},{4,7},{5,6},{6,5},{7,4},{8,11},{9,10},{10,... | collective-permute-start | bytes 147464 | tf_op jit(solution)/shard_map/ppermute | solution.py:543
  (32 other events, 129.1 us)

commit v2 on v1

--- a/solution.py
+++ b/solution.py
@@ -36,9 +36,18 @@
 
 
 def dot3(a, b, dims):
-    ah, al = halves(a)
-    bh, bl = halves(b)
-    return mm(ah, bh, dims) + (mm(ah, bl, dims) + mm(al, bh, dims))
+    return joined3(halves(a), halves(b), dims)
+
+
+def joined3(a, b, dims):
+    (ah, al), (bh, bl) = a, b
+    (left,), (right,) = dims[0]
+    if ah.shape[left] > 128:
+        return mm(ah, bh, dims) + (mm(ah, bl, dims) + mm(al, bh, dims))
+    both = mm(
+        jnp.concatenate([ah, al], axis=left), jnp.concatenate([bh, bh], axis=right), dims
+    )
+    return both + mm(ah, bl, dims)
 
 
 def spread_matrix(share, headdim):
@@ -48,8 +57,13 @@
 
 
 def spread(values, matrix):
-    high, mid, low = thirds(values)
-    return mm(high, matrix, TN) + (mm(mid, matrix, TN) + mm(low, matrix, TN))
+    return mm(
+        jnp.concatenate(thirds(values), axis=0), jnp.concatenate([matrix] * 3, axis=0), TN
+    )
+
+
+def skip_row(hpar, matrix):
+    return spread(jnp.broadcast_to(hpar[:, 2:3], (hpar.shape[0], 8)), matrix)[:1]
 
 
 def head_sums(products, matrix):
@@ -79,12 +93,11 @@
 
 
 def pack_kernel(s, x_ref, step_ref, *refs, share, inner, state, groups):
-    outs, rims, turned = refs[:groups], refs[groups:-1], refs[-1]
+    outs, rims = refs[:groups], refs[groups:]
     me = s[0]
     tokens = x_ref.shape[0]
     part = inner // groups
     width = part + 2 * state
-    turned[...] = step_ref[...].T
     for k in range(groups):
         q = me ^ k
         xs = outs[k]
@@ -96,17 +109,60 @@
             :, pl.ds(pl.multiple_of(inner + (groups + q) * state, state), state)
         ]
         rims[k][...] = xs[tokens - 16 :, :width]
-        raw = turned[pl.ds(pl.multiple_of(q * share, share), share), :]
+        raw = step_ref[pl.ds(pl.multiple_of(q * share, share), share), :]
         xs[:, width:] = jnp.zeros((tokens, tokens), BF16)
         for i, piece in enumerate(thirds(raw)):
             xs[i * share : (i + 1) * share, width:] = piece
 
 
-def pack_grad_kernel(s, g_ref, *outs):
+def pack_grad_kernel(s, g_ref, bias, decay, skip, *refs, groups):
+    outs, hpar, wide, turned = refs[:groups], *refs[groups:]
+    heads = bias.shape[1]
+    share = heads // groups
+    wide[...] = jnp.zeros_like(wide)
+    for i, ref in enumerate((bias, decay, skip)):
+        wide[i : i + 1, :heads] = ref[...]
+    turned[...] = wide[...].T
+    hpar[...] = turned[pl.ds(pl.multiple_of(s[0] * share, share), share), :]
     part = outs[0].shape[1]
     for k, out in enumerate(outs):
         q = s[0] ^ k
         out[...] = g_ref[:, pl.ds(pl.multiple_of(q * part, part), part)]
+
+
+def activate(rows, weight, bias, valid, paired):
+    taps = weight.shape[0]
+    tokens = rows.shape[0] - 8
+    u = jnp.zeros((tokens, rows.shape[1]), F32) + bias
+    for k in range(taps):
+        reach = taps - 1 - k
+        moved = rows[8 - reach : 8 - reach + tokens]
+        if reach:
+            moved = moved * valid[reach]
+        u = u + weight[k : k + 1] * moved
+    sig = 1.0 / (1.0 + jnp.exp(-u))
+    value = u * sig
+    if paired:
+        high, low = halves(value)
+        value = high.astype(F32) + low.astype(F32)
+    return value, sig * (1.0 + u * (1.0 - sig))
+
+
+def convolve_head(s, first, rim, wx, wb, wc, bx, bb, bc, act_ref, dsl_ref, xall_ref, sizes, docs):
+    share, headdim, state = sizes
+    part = share * headdim
+    tokens = act_ref.shape[1]
+    pos = s[1] + first * tokens + lax.broadcasted_iota(jnp.int32, (8, 1), 0)
+    inside = pos - doc_start(pos, s, docs)
+    valid = [(inside >= reach).astype(F32) for reach in range(wx.shape[0])]
+    own = xall_ref[pl.ds(pl.multiple_of(16 + first * tokens, 16), 16), :].astype(F32)
+    rows = jnp.concatenate([rim[8:], own[:8]], axis=0)
+    for lo, size, w_ref, b_ref in (
+        (0, part, wx, bx), (part, state, wb, bb), (part + state, state, wc, bc)
+    ):
+        value, slope = activate(rows[:, lo : lo + size], w_ref[...], b_ref[...], valid, lo == 0)
+        act_ref[first, :8, lo : lo + size] = value
+        dsl_ref[first, :8, lo : lo + size] = slope
 
 
 def convolve_pair(s, first, pieces, rim, wx, wb, wc, bx, bb, bc, act_ref, dsl_ref, xall_ref, ext,
@@ -132,20 +188,11 @@
 
         def convolve(lo, w_ref, b_ref, wlo, paired):
             rows = ext[c * tokens : c * tokens + tokens + 8, lo : lo + 128]
-            u = jnp.zeros((tokens, 128), F32) + b_ref[:, wlo : wlo + 128]
-            for k in range(taps):
-                reach = taps - 1 - k
-                shifted = rows[8 - reach : 8 - reach + tokens]
-                if reach:
-                    shifted = shifted * valid[reach]
-                u = u + w_ref[k : k + 1, wlo : wlo + 128] * shifted
-            sig = 1.0 / (1.0 + jnp.exp(-u))
-            value = u * sig
-            if paired:
-                high, low = halves(value)
-                value = high.astype(F32) + low.astype(F32)
+            value, slope = activate(
+                rows, w_ref[:, wlo : wlo + 128], b_ref[:, wlo : wlo + 128], valid, paired
+            )
             act_ref[chunk, :, lo : lo + 128] = value
-            dsl_ref[chunk, :, lo : lo + 128] = sig * (1.0 + u * (1.0 - sig))
+            dsl_ref[chunk, :, lo : lo + 128] = slope
 
         for lo in range(0, part, 128):
             convolve(lo, wx, bx, lo, True)
@@ -155,21 +202,17 @@
 
 
 def conv_kernel(
-    s, x0, x1, r2, r3, wx, wb, wc, bx, bb, bc, act_ref, dsl_ref, xall_ref, ext, *, sizes, docs
-):
-    rim = r2[...].astype(F32) + r3[...].astype(F32)
+    s, x0, x1, wx, wb, wc, bx, bb, bc, act_ref, dsl_ref, xall_ref, ext, *, sizes, docs
+):
+    rim = jnp.zeros((16, ext.shape[1]), F32)
     convolve_pair(
         s, s[0] & 2, (x0, x1), rim, wx, wb, wc, bx, bb, bc, act_ref, dsl_ref, xall_ref, ext,
         sizes, docs,
     )
 
-    @pl.when((s[0] & 2) == 0)
-    def _():
-        xall_ref[:16, :] = rim.astype(BF16)
-
 
 def conv_state_kernel(
-    s, x0, x1, x2, x3, r0, r1, wx, wb, wc, bx, bb, bc, hpar, act_in, dsl_in, xall_in,
+    s, x0, x1, x2, x3, r0, r1, r2, r3, wx, wb, wc, bx, bb, bc, hpar, act_in, dsl_in, xall_in,
     act_ref, dsl_ref, xall_ref, pay_ref, chain_ref, vec_ref,
     ext, raws, *, share, headdim, state, docs,
 ):
@@ -186,10 +229,12 @@
     inner_rim = xall_ref[2 * tokens : 2 * tokens + 16, :].astype(F32)
     rim = jnp.where(upper_chip, r0[...].astype(F32) + r1[...].astype(F32), inner_rim)
 
-    @pl.when(upper_chip)
-    def _():
-        xall_ref[:16, :] = rim.astype(BF16)
-
+    own_rim = r2[...].astype(F32) + r3[...].astype(F32)
+    xall_ref[:16, :] = jnp.where(upper_chip, rim, own_rim).astype(BF16)
+    convolve_head(
+        s, me & 2, own_rim, wx, wb, wc, bx, bb, bc, act_ref, dsl_ref, xall_ref,
+        (share, headdim, state), docs,
+    )
     convolve_pair(
         s, (me & 2) ^ 2, (x2, x3), rim, wx, wb, wc, bx, bb, bc, act_ref, dsl_ref, xall_ref, ext,
         (share, headdim, state), docs,
@@ -261,7 +306,7 @@
 
 
 def local_kernel(
-    s, act_ref, vec_ref, gall_ref, schain, gchain, *refs, first, share, headdim, state, docs,
+    s, act_ref, vec_ref, gall_ref, schain, gchain, *refs, span, share, headdim, state, docs,
 ):
     y_ref, dx_ref, db_ref, dc_ref, flow_ref, xd_ref, wide, yd, dxd = refs[-9:]
     plane = s[1]
@@ -298,13 +343,16 @@
             for h in (2 * pair, 2 * pair + 1):
                 diff = wide[:, h * tokens : (h + 1) * tokens] - cum[h : h + 1, :]
                 factors.append(jnp.exp(diff + mask) * step[h : h + 1, :])
-            dw = mm(gst, xh, NT) + mm(gst, xl, NT)
+            pieces = jnp.concatenate([xh, xl], axis=1)
+            dw = mm(jnp.concatenate([gst, gst], axis=1), pieces, NT)
             dm = dm + dw[:tokens] * factors[0] + dw[tokens:] * factors[1]
             w = jnp.concatenate([m * factors[0], m * factors[1]], axis=0)
-            wh, wl = halves(w)
-            yst = mm(wh, xh, NN) + (mm(wh, xl, NN) + mm(wl, xh, NN) + mm(wl, xl, NN))
+            w = jnp.concatenate(halves(w), axis=1)
+            yst = mm(w, jnp.concatenate([pieces, pieces], axis=0), NN)
+            yst = yst[:, : 2 * headdim] + yst[:, 2 * headdim :]
             yd[:, lo : lo + 2 * headdim] = jnp.where(left, yst[:tokens], yst[tokens:])
-            dxd[:, lo : lo + 2 * headdim] = mm(wh, gst, TN) + mm(wl, gst, TN)
+            dst = mm(w, gst, TN)
+            dxd[:, lo : lo + 2 * headdim] = dst[:tokens] + dst[tokens:]
         head_in = spread(vec_ref[c, HEAD], matrix)
         tail = spread(vec_ref[c, TAIL], matrix)
         x = act_ref[c, :, :part]
@@ -327,11 +375,11 @@
         db_ref[c] = dot3(dm, cc, TN) + dot3(x * tail, gchain[c], NT)
         return carry
 
-    lax.fori_loop(first, first + 2, chunk, 0)
+    lax.fori_loop(*span, chunk, 0)
 
 
 def out_kernel(
-    s, one, two, act_ref, y_ref, gall_ref, vec_ref, skip, dcl_ref,
+    s, one, two, act_ref, y_ref, gall_ref, vec_ref, hpar, dcl_ref,
     m0, m1, m2, m3, gy_ref, in_ref, dc_ref, *, share, headdim, state,
 ):
     me = s[0]
@@ -340,119 +388,207 @@
     arrived = one[:state, :] + one[state : state + 1, :] * two[:state, :]
     in_ref[...] = arrived
     ih, il = halves(arrived)
+    skip = skip_row(hpar, matrix)
     for k, out in enumerate((m0, m1, m2, m3)):
         c = me ^ k
         reach = spread(vec_ref[c, HP], matrix)
         ch, cl = halves(act_ref[c, :, part + state :])
-        carry = mm(ch, ih, NN) + (mm(ch, il, NN) + mm(cl, ih, NN))
+        carry = joined3((ch, cl), (ih, il), NN)
         y = reach * carry
         g = gall_ref[c].astype(F32)
         gy_ref[c] = head_sums(g * y, matrix)
         y = y + y_ref[c]
-        out[...] = (y + skip[...] * act_ref[c, :, :part]).astype(BF16)
+        out[...] = (y + skip * act_ref[c, :, :part]).astype(BF16)
         gh, gl = halves(g * reach)
         dc_ref[c] = dcl_ref[c] + mm(gh, ih, NT) + (mm(gh, il, NT) + mm(gl, ih, NT))
 
 
-def back_kernel(
-    s, one, two, in_ref, pay, act_ref, dsl_ref, dxl_ref, dbl_ref, dc_ref, gy_ref, flow_ref,
-    xd_ref, gall_ref, vec_ref, skip, hpar, xall_ref, du_ref, par_ref, gs_ref,
-    *, share, headdim, state, docs, taps,
-):
+def input_grads(c, rows, high, low, act_ref, dsl_ref, dxl_ref, dbl_ref, dc_ref, gall_ref, vec_ref,
+                skip, matrix, part, state):
+    x = act_ref[c, :rows, :part]
+    g = gall_ref[c, :rows].astype(F32)
+    tail = spread(vec_ref[c, TP][:, :rows], matrix)
+    bh, bl = halves(act_ref[c, :rows, part : part + state])
+    far = tail * joined3((bh, bl), (high, low), NN)
+    xh, xl = halves(x * tail)
+    db = dbl_ref[c, :rows] + mm(xh, high, NT) + (mm(xh, low, NT) + mm(xl, high, NT))
+    dx = far + dxl_ref[c, :rows] + skip * g
+    return (
+        dx * dsl_ref[c, :rows, :part],
+        db * dsl_ref[c, :rows, part : part + state],
+        dc_ref[c, :rows] * dsl_ref[c, :rows, part + state :],
+        x * far,
+        g * x,
+    )
+
+
+def edge_kernel(
+    s, one, two, act_ref, dsl_ref, dxl_ref, dbl_ref, dc_ref, gall_ref, vec_ref, hpar,
+    edge_ref, adjoint_ref, high_ref, low_ref, *, share, headdim, state,
+):
+    part = share * headdim
+    matrix = spread_matrix(share, headdim)
+    adjoint = one[:state, :] + one[state : state + 1, :] * two[:state, :]
+    adjoint_ref[...] = adjoint
+    high, low = halves(adjoint)
+    high_ref[...] = high
+    low_ref[...] = low
+    grads = input_grads(
+        0, 16, high, low, act_ref, dsl_ref, dxl_ref, dbl_ref, dc_ref, gall_ref, vec_ref,
+        skip_row(hpar, matrix), matrix, part, state,
+    )
+    edge_ref[:, :part] = grads[0][:8]
+    edge_ref[:, part : part + state] = grads[1][:8]
+    edge_ref[:, part + state :] = grads[2][:8]
+
+
+def pair_grads(s, first, high_ref, low_ref, act_ref, dsl_ref, dxl_ref, dbl_ref, dc_ref, gall_ref,
+               vec_ref, hpar, xall_ref, du_ref, par_ref, sizes, docs, taps):
+    share, headdim, state = sizes
+    part = share * headdim
+    width = part + 2 * state
+    tokens = act_ref.shape[1]
     plane = s[1]
-    part = share * headdim
+    matrix = spread_matrix(share, headdim)
+    skip = skip_row(hpar, matrix)
+    high, low = high_ref[...], low_ref[...]
+    away, skips = [], []
+    for i in range(2):
+        c = first + i
+        grads = input_grads(
+            c, tokens, high, low, act_ref, dsl_ref, dxl_ref, dbl_ref, dc_ref, gall_ref, vec_ref,
+            skip, matrix, part, state,
+        )
+        rows = pl.ds(pl.multiple_of(c * tokens, tokens), tokens)
+        du_ref[rows, :part] = grads[0]
+        du_ref[rows, part : part + state] = grads[1]
+        du_ref[rows, part + state : width] = grads[2]
+        away.append(head_sums(grads[3], matrix))
+        skips.append(head_sums(grads[4], matrix))
+    for lo in range(0, width, 128):
+        sums = [jnp.zeros((8, 128), F32) for _ in range(taps + 1)]
+        for i in range(2):
+            c = first + i
+            begin = pl.multiple_of(c * tokens, tokens)
+            rows = xall_ref[pl.ds(begin, tokens + 16), lo : lo + 128].astype(F32)
+            pos = plane + c * tokens + lax.broadcasted_iota(jnp.int32, (tokens, 1), 0)
+            inside = pos - doc_start(pos, s, docs)
+            du = du_ref[pl.ds(begin, tokens), lo : lo + 128]
+            for k in range(taps):
+                reach = taps - 1 - k
+                moved = rows[16 - reach : 16 - reach + tokens]
+                if reach:
+                    moved = moved * (inside >= reach).astype(F32)
+                sums[k] = sums[k] + jnp.sum((du * moved).reshape(tokens // 8, 8, 128), axis=0)
+            sums[taps] = sums[taps] + jnp.sum(du.reshape(tokens // 8, 8, 128), axis=0)
+        for k in range(taps + 1):
+            par_ref[k : k + 1, lo : lo + 128] = jnp.sum(sums[k], axis=0, keepdims=True)
+    return away, skips[0] + skips[1]
+
+
+def back_far_kernel(
+    s, high_ref, low_ref, act_ref, dsl_ref, dxl_ref, dbl_ref, dc_ref, gall_ref, vec_ref, hpar,
+    xall_ref, du_ref, par_ref, aux_ref, *, sizes, docs, taps,
+):
+    share, headdim, state = sizes
+    part = share * headdim
+    width = part + 2 * state
+    tokens = act_ref.shape[1]
+    par_ref[...] = jnp.zeros_like(par_ref)
+    away, skips = pair_grads(
+        s, (s[0] & 2) ^ 2, high_ref, low_ref, act_ref, dsl_ref, dxl_ref, dbl_ref, dc_ref, gall_ref,
+        vec_ref, hpar, xall_ref, du_ref, par_ref, sizes, docs, taps,
+    )
+    aux_ref[0], aux_ref[1], aux_ref[2] = away[0], away[1], skips
+
+    @pl.when((s[0] & 2) == 2)
+    def _():
+        matrix = spread_matrix(share, headdim)
+        grads = input_grads(
+            2, 16, high_ref[...], low_ref[...], act_ref, dsl_ref, dxl_ref, dbl_ref, dc_ref,
+            gall_ref, vec_ref, skip_row(hpar, matrix), matrix, part, state,
+        )
+        du_ref[2 * tokens : 2 * tokens + 8, :part] = grads[0][:8]
+        du_ref[2 * tokens : 2 * tokens + 8, part : part + state] = grads[1][:8]
+        du_ref[2 * tokens : 2 * tokens + 8, part + state :] = grads[2][:8]
+
+
+def back_near_kernel(
+    s, high_ref, low_ref, act_ref, dsl_ref, dxl_ref, dbl_ref, dc_ref, gall_ref, vec_ref, hpar,
+    xall_ref, adjoint_ref, in_ref, pay, gy_ref, flow_ref, xd_ref, par_in, aux, du_in,
+    du_ref, par_ref, g0, g1, g2, g3, away_s, gs_s, *, sizes, docs, taps,
+):
+    share, headdim, state = sizes
+    part = share * headdim
+    width = part + 2 * state
     tokens = act_ref.shape[1]
     chunks = 4
+    me = s[0]
     matrix = spread_matrix(share, headdim)
-    adjoint = one[:state, :] + one[state : state + 1, :] * two[:state, :]
-    inner = jnp.sum(adjoint * in_ref[...], axis=0, keepdims=True) * pay[state : state + 1, :]
+    own, skips = pair_grads(
+        s, me & 2, high_ref, low_ref, act_ref, dsl_ref, dxl_ref, dbl_ref, dc_ref, gall_ref,
+        vec_ref, hpar, xall_ref, du_ref, par_ref, sizes, docs, taps,
+    )
+    par_ref[: taps + 1, :width] = par_ref[: taps + 1, :width] + par_in[: taps + 1, :width]
+    for i in range(2):
+        away_s[(me & 2) + i] = own[i]
+        away_s[((me & 2) ^ 2) + i] = aux[i]
+    inner = jnp.sum(adjoint_ref[...] * in_ref[...], axis=0, keepdims=True)
+    inner = inner * pay[state : state + 1, :]
     through = head_sums(jnp.broadcast_to(inner, (8, part)), matrix)[:, :1]
-    ah, al = halves(adjoint)
     rate = jnp.exp(hpar[:, 1:2])
     start_sums = triangle(tokens, "from")
     end_sums = triangle(tokens, "before")
-    away = []
     g_bias = jnp.zeros((share, 1), F32)
     g_decay = jnp.zeros((share, 1), F32)
-    g_skip = jnp.zeros((share, 1), F32)
-    for c in range(chunks):
-        x = act_ref[c, :, :part]
-        g = gall_ref[c].astype(F32)
-        tail = spread(vec_ref[c, TP], matrix)
-        bh, bl = halves(act_ref[c, :, part : part + state])
-        dx = tail * (mm(bh, ah, NN) + (mm(bh, al, NN) + mm(bl, ah, NN)))
-        away.append(head_sums(x * dx, matrix))
-        dx = dx + dxl_ref[c]
-        xh, xl = halves(x * tail)
-        db = dbl_ref[c] + mm(xh, ah, NT) + (mm(xh, al, NT) + mm(xl, ah, NT))
-        du_ref[c * tokens : (c + 1) * tokens, :part] = (dx + skip[...] * g) * dsl_ref[c, :, :part]
-        du_ref[c * tokens : (c + 1) * tokens, part : part + state] = (
-            db * dsl_ref[c, :, part : part + state]
-        )
-        du_ref[c * tokens : (c + 1) * tokens, part + state :] = (
-            dc_ref[c] * dsl_ref[c, :, part + state :]
-        )
-        g_skip = g_skip + jnp.sum(head_sums(g * x, matrix), axis=1, keepdims=True)
     for c in range(chunks):
         flow = (
-            flow_ref[c] + by_triangle(gy_ref[c], start_sums) + by_triangle(away[c], end_sums)
+            flow_ref[c] + by_triangle(gy_ref[c], start_sums) + by_triangle(away_s[c], end_sums)
         ) + through
         for d in range(chunks):
             if d > c:
                 flow = flow + jnp.sum(gy_ref[d], axis=1, keepdims=True)
             if d < c:
-                flow = flow + jnp.sum(away[d], axis=1, keepdims=True)
+                flow = flow + jnp.sum(away_s[d], axis=1, keepdims=True)
         step = vec_ref[c, STEP]
-        grad_step = ((xd_ref[c] + away[c]) / step - rate * flow) * vec_ref[c, SIG]
-        gs_ref[c] = grad_step
+        grad_step = ((xd_ref[c] + away_s[c]) / step - rate * flow) * vec_ref[c, SIG]
+        gs_s[c] = grad_step
         g_bias = g_bias + jnp.sum(grad_step, axis=1, keepdims=True)
         g_decay = g_decay - rate * jnp.sum(flow * step, axis=1, keepdims=True)
+    for k, out in enumerate((g0, g1, g2, g3)):
+        out[...] = gs_s[me ^ k]
+    g_skip = jnp.sum(skips + aux[2], axis=1, keepdims=True)
     lane = lax.broadcasted_iota(jnp.int32, (share, 128), 1)
     heads = jnp.where(lane == 0, g_bias, jnp.where(lane == 1, g_decay, g_skip))
-    width = part + 2 * state
-    par_ref[...] = jnp.zeros_like(par_ref)
+    par_ref[taps + 1 :, :width] = jnp.zeros((8 - taps - 1, width), F32)
     par_ref[:, width : width + 128] = heads[:8]
     par_ref[:, width + 128 :] = heads[8:]
-    for lo in range(0, width, 128):
-        sums = [jnp.zeros((8, 128), F32) for _ in range(taps + 1)]
-        for c in range(chunks):
-            rows = xall_ref[c * tokens : c * tokens + tokens + 16, lo : lo + 128].astype(F32)
-            pos = plane + c * tokens + lax.broadcasted_iota(jnp.int32, (tokens, 1), 0)
-            inside = pos - doc_start(pos, s, docs)
-            du = du_ref[c * tokens : (c + 1) * tokens, lo : lo + 128]
-            for k in range(taps):
-                reach = taps - 1 - k
-                shifted = rows[16 - reach : 16 - reach + tokens]
-                if reach:
-                    shifted = shifted * (inside >= reach).astype(F32)
-                sums[k] = sums[k] + jnp.sum((du * shifted).reshape(tokens // 8, 8, 128), axis=0)
-            sums[taps] = sums[taps] + jnp.sum(du.reshape(tokens // 8, 8, 128), axis=0)
-        for k in range(taps + 1):
-            par_ref[k : k + 1, lo : lo + 128] = jnp.sum(sums[k], axis=0, keepdims=True)
 
 
 def conv_back_kernel(
-    s, du_ref, rim_ref, wx, wb, wc, gs_ref, o0, o1, o2, o3, ext,
-    *, share, headdim, state, docs, taps,
-):
+    s, du_ref, rim_ref, wx, wb, wc, o0, o1, ext, *, far, sizes, docs, taps
+):
+    share, headdim, state = sizes
     me = s[0]
     plane = s[1]
     part = share * headdim
     width = part + 2 * state
     tokens = o0.shape[0]
-    chunks = 4
-    ext[: chunks * tokens, :] = du_ref[...]
-    ext[chunks * tokens :, :] = rim_ref[...]
-    for k, out in enumerate((o0, o1, o2, o3)):
-        c = me ^ k
-        pos = plane + c * tokens + lax.broadcasted_iota(jnp.int32, (tokens, 1), 0)
+    first = (me & 2) ^ (2 if far else 0)
+    ext[: 2 * tokens, :] = du_ref[pl.ds(pl.multiple_of(first * tokens, tokens), 2 * tokens), :]
+    ext[2 * tokens :, :] = jnp.where(
+        first == 2, rim_ref[...], du_ref[2 * tokens : 2 * tokens + 8, :]
+    )
+    for k, out in enumerate((o0, o1)):
+        place = (me & 1) ^ k
+        pos = plane + (first + place) * tokens + lax.broadcasted_iota(jnp.int32, (tokens, 1), 0)
         valid = []
         for reach in range(1, taps):
             ahead = pos + reach
             valid.append((ahead - doc_start(ahead, s, docs) >= reach).astype(F32))
-        first = pl.multiple_of(c * tokens, tokens)
+        begin = pl.multiple_of(place * tokens, tokens)
         for lo in range(0, width, 128):
-            rows = ext[pl.ds(first, tokens + 8), lo : lo + 128]
+            rows = ext[pl.ds(begin, tokens + 8), lo : lo + 128]
             if lo < part:
                 w = wx[:, lo : lo + 128]
             elif lo < part + state:
@@ -466,9 +602,6 @@
                     rows[reach : reach + tokens] * valid[reach - 1]
                 )
             out[:, lo : lo + 128] = total.astype(BF16)
-        out[:, width:] = jnp.zeros((tokens, tokens), BF16)
-        for i, piece in enumerate(thirds(gs_ref[c])):
-            out[i * share : (i + 1) * share, width:] = piece
 
 
 def join_kernel(s, p0, p1, p2, p3, out_ref):
@@ -478,7 +611,21 @@
         out_ref[:, pl.ds(pl.multiple_of(q * part, part), part)] = ref[...]
 
 
-def join_grad_kernel(s, p0, p1, p2, p3, out_ref, gs_ref, turned, *, share, inner, state, groups):
+def join_small_kernel(s, first, *refs):
+    groups = 4
+    width = first.shape[1]
+    received, steps, outs = refs[: -2 * groups], refs[-2 * groups : -groups], refs[-groups:]
+    total = first[...]
+    for ref in received:
+        total = total + ref[...]
+    for step, out in zip(steps, outs):
+        tokens = step.shape[1]
+        out[:, :width] = total
+        out[:, width : width + tokens] = step[:8, :]
+        out[:, width + tokens :] = step[8:, :]
+
+
+def join_grad_kernel(s, p0, p1, p2, p3, g0, g1, g2, g3, out_ref, gs_ref, *, share, inner, state, groups):
     part = inner // groups
     for k, ref in enumerate((p0, p1, p2, p3)):
         q = s[0] ^ k
@@ -487,13 +634,14 @@
             :, part : part + state
         ]
         out_ref[:, pl.ds(pl.multiple_of(inner + (groups + q) * state, state), state)] = ref[
-            :, part + state : part + 2 * state
+            :, part + state :
         ]
-        block = ref[: 3 * share, part + 2 * state :].astype(F32)
-        turned[pl.ds(pl.multiple_of(q * share, share), share), :] = (
-            block[:share] + block[share : 2 * share] + block[2 * share :]
-        )
-    gs_ref[...] = turned[...].T
+    for k, ref in enumerate((g0, g1, g2, g3)):
+        tokens = gs_ref.shape[1]
+        last = ref.shape[1]
+        first = pl.multiple_of((s[0] ^ k) * share, share)
+        gs_ref[pl.ds(first, 8), :] = ref[:, last - 2 * tokens : last - tokens]
+        gs_ref[pl.ds(first + 8, 8), :] = ref[:, last - tokens :]
 
 
 def join_params_kernel(
@@ -512,7 +660,7 @@
             ref[:rows, part + state : width] * scale
         )
         turned[pl.ds(pl.multiple_of(q * share, 8), 8), :] = ref[:, width : width + 128]
-        turned[pl.ds(pl.multiple_of(q * share + 8, 8), 8), :] = ref[:, width + 128 :]
+        turned[pl.ds(pl.multiple_of(q * share + 8, 8), 8), :] = ref[:, width + 128 : width + 256]
     head_ref[...] = turned[...].T[: head_ref.shape[0], :] * scale
 
 
@@ -533,6 +681,7 @@
             scratch_shapes=[pltpu.VMEM(shape, kind) for shape, kind in scratch],
         ),
         compiler_params=pltpu.CompilerParams(vmem_limit_bytes=LIMIT),
+        cost_estimate=pl.CostEstimate(flops=1, transcendentals=0, bytes_accessed=1),
         name=name,
         input_output_aliases=aliases or {},
     )(table, *operands)
@@ -587,17 +736,11 @@
     sizes = dict(share=share, headdim=headdim, state=state)
     table = jnp.concatenate(
         [
-            jnp.stack([me % groups, (me // groups) * (groups * tokens)]).astype(jnp.int32),
+            jnp.stack([me & (groups - 1), (me & -groups) * tokens]).astype(jnp.int32),
             doc_lengths,
         ]
     )
-    hpar = jnp.pad(
-        jnp.stack([step_bias, decay_log, skip_gain], axis=1), ((0, 0), (0, 128 - 3))
-    )
-    skips = jnp.repeat(skip_gain, headdim)[None, :]
     bias_row = conv_bias[None, :]
-    hpar_spec = pl.BlockSpec((share, 128), lambda i, s: (s[0], 0))
-    skip_spec = pl.BlockSpec((1, part), lambda i, s: (0, s[0]))
     b_first = inner // state
 
     def column_specs(rows):
@@ -611,15 +754,19 @@
     packed = call(
         functools.partial(pack_kernel, **shapes),
         table,
-        [conv_input, step_raw],
+        [conv_input, step_raw.T],
         [None] * 2,
         [((tokens, width + tokens), BF16)] * groups + [((16, width), BF16)] * groups,
-        [((heads, tokens), F32)],
         name="pack",
     )
     xs, edges = packed[:groups], packed[groups:]
-    gs = call(
-        pack_grad_kernel, table, [grad_out], [None], [((tokens, part), BF16)] * groups,
+    *gs, hpar = call(
+        functools.partial(pack_grad_kernel, groups=groups),
+        table,
+        [grad_out, step_bias[None, :], decay_log[None, :], skip_gain[None, :]],
+        [None] * 4,
+        [((tokens, part), BF16)] * groups + [((share, 128), F32)],
+        [((128, 128), F32)] * 2,
         name="pack_grad",
     )
     xr = [xs[0]] + [swapped(xs[k], k) for k in range(1, groups)]
@@ -631,7 +778,6 @@
             if source >= 0 and (source % groups) ^ (i % groups) == k:
                 pairs.append((source, i))
         rims.append(lax.ppermute(edges[k], "ctx", pairs))
-    gr = [gs[0]] + [swapped(gs[k], k) for k in range(1, groups)]
     conv_shapes = [
         ((groups, tokens, width), F32),
         ((groups, tokens, width), F32),
@@ -643,17 +789,19 @@
     act, dsl, xall = call(
         functools.partial(conv_kernel, docs=docs, sizes=(share, headdim, state)),
         table,
-        [xr[0], xr[1], rims[2], rims[3]] + conv_params,
-        [None] * 4 + conv_specs,
+        [xr[0], xr[1]] + conv_params,
+        [None] * 2 + conv_specs,
         conv_shapes,
         [ext_shape],
         name="conv",
     )
+    act, *gs = lax.optimization_barrier((act, *gs))
+    gr = [gs[0]] + [swapped(gs[k], k) for k in range(1, groups)]
     act, dsl, xall, spay, schain, vec = call(
         functools.partial(conv_state_kernel, docs=docs, **sizes),
         table,
-        xr + rims[:2] + conv_params + [hpar, act, dsl, xall],
-        [None] * 6 + conv_specs + [hpar_spec] + [None] * 3,
+        xr + rims + conv_params + [hpar, act, dsl, xall],
+        [None] * 8 + conv_specs + [None] * 4,
         conv_shapes
         + [
             ((state + 8, part), F32),
@@ -662,7 +810,7 @@
         ],
         [ext_shape, ((groups, share, tokens), F32)],
         name="conv_state",
-        aliases={14: 0, 15: 1, 16: 2},
+        aliases={16: 0, 17: 1, 18: 2},
     )
     s_near, covered = near_of(spay, state, 1, planes)
     gall, gpay, gchain = call(
@@ -687,9 +835,9 @@
         ((groups, share, tokens), F32),
     ]
     locals_ = []
-    for first in (0, 2):
+    for span in ((0, 2), (2, 3), (3, 4)):
         locals_ = call(
-            functools.partial(local_kernel, first=first, docs=docs, **sizes),
+            functools.partial(local_kernel, span=span, docs=docs, **sizes),
             table,
             [act, vec, gall, schain, gchain] + list(locals_),
             [None] * (5 + len(locals_)),
@@ -698,16 +846,18 @@
             name="local",
             aliases={6 + i: i for i in range(len(locals_))},
         )
-        if first == 0:
-            s_far = shifted(after(s_near, locals_[4]), GROUPS * covered)
-        else:
-            g_far = shifted(after(g_near, locals_[4]), -GROUPS * covered)
+        if span[1] == 2:
+            s_near, *locals_ = lax.optimization_barrier((s_near, *locals_))
+            s_far = shifted(s_near, GROUPS * covered)
+        elif span[1] == 3:
+            g_near, *locals_ = lax.optimization_barrier((g_near, *locals_))
+            g_far = shifted(g_near, -GROUPS * covered)
     y_local, dx_local, db_local, dc_local, flow, xd = locals_
     *mixed, gy, state_in, dc = call(
         functools.partial(out_kernel, **sizes),
         table,
-        [s_near, s_far, act, y_local, gall, vec, skips, dc_local],
-        [None] * 6 + [skip_spec, None],
+        [s_near, s_far, act, y_local, gall, vec, hpar, dc_local],
+        [None] * 8,
         [((tokens, part), BF16)] * groups
         + [
             ((groups, share, tokens), F32),
@@ -717,41 +867,90 @@
         name="out",
     )
     mr = [mixed[0]] + [swapped(mixed[k], k) for k in range(1, groups)]
-    du, params, grad_steps = call(
-        functools.partial(back_kernel, docs=docs, taps=taps, **sizes),
-        table,
-        [g_near, g_far, state_in, spay, act, dsl, dx_local, db_local, dc, gy, flow, xd, gall, vec,
-         skips, hpar, xall],
-        [None] * 14 + [skip_spec, hpar_spec, None],
+    common = [act, dsl, dx_local, db_local, dc, gall, vec, hpar]
+    edge, adjoint, high, low = call(
+        functools.partial(edge_kernel, **sizes),
+        table,
+        [g_near, g_far] + common,
+        [None] * 10,
         [
-            ((groups * tokens, width), F32),
-            ((8, width + 256), F32),
-            ((groups, share, tokens), F32),
+            ((8, width), F32),
+            ((state, part), F32),
+            ((state, part), BF16),
+            ((state, part), BF16),
         ],
-        name="back",
-    )
-    rim_back = shifted(du[:8], -groups)
+        name="edge",
+    )
+    rim_back = shifted(edge, -groups)
+    triple = (share, headdim, state)
+    settings = dict(sizes=triple, docs=docs, taps=taps)
+    common = [high, low] + common + [xall]
+    du_shape = ((groups * tokens, width), F32)
+    par_shape = ((8, width + 256), F32)
+    du, par_far, aux = call(
+        functools.partial(back_far_kernel, **settings),
+        table,
+        common,
+        [None] * 11,
+        [du_shape, par_shape, ((3, share, tokens), F32)],
+        name="back_far",
+    )
     rim_back, *mr = lax.optimization_barrier((rim_back, *mr))
-    back = call(
-        functools.partial(conv_back_kernel, docs=docs, taps=taps, **sizes),
-        table,
-        [du, rim_back] + [conv_weight] * 3 + [grad_steps],
-        [None] * 2 + column_specs(taps) + [None],
-        [((tokens, width + tokens), BF16)] * groups,
-        [((groups * tokens + 8, width), F32)],
-        name="conv_back",
-    )
-    br = [back[0]] + [swapped(back[k], k) for k in range(1, groups)]
-    params = after(params, back[1])
-    step = groups
-    while step < devices:
-        params = params + swapped(params, step)
-        step *= 2
-    pr = [params] + [swapped(params, k) for k in range(1, groups)]
+    pair_shapes = [((tokens, width), BF16)] * 2
+    ext_back = [((2 * tokens + 8, width), F32)]
+    back_far = call(
+        functools.partial(conv_back_kernel, far=True, **settings),
+        table,
+        [du, rim_back] + [conv_weight] * 3,
+        [None] * 2 + column_specs(taps),
+        pair_shapes,
+        ext_back,
+        name="conv_back_far",
+    )
+    br_far = [swapped(back_far[k - 2], k) for k in (2, 3)]
+    du = after(du, back_far[0])
+    du, params, *grad_steps = call(
+        functools.partial(back_near_kernel, **settings),
+        table,
+        common
+        + [adjoint, state_in, spay, gy, flow, xd, par_far, aux, du],
+        [None] * 20,
+        [du_shape, par_shape] + [((share, tokens), F32)] * groups,
+        [((groups, share, tokens), F32)] * 2,
+        name="back_near",
+        aliases={20: 0},
+    )
     (mixer_out,) = call(
         join_kernel, table, mr, [None] * groups, [((tokens, inner), BF16)], name="join_out",
         vmem=False,
     )
+    du, br_far[0], mixer_out = lax.optimization_barrier((du, br_far[0], mixer_out))
+    back_near = call(
+        functools.partial(conv_back_kernel, far=False, **settings),
+        table,
+        [du, rim_back] + [conv_weight] * 3,
+        [None] * 2 + column_specs(taps),
+        pair_shapes,
+        ext_back,
+        name="conv_back_near",
+    )
+    br = [back_near[0], swapped(back_near[1], 1)] + br_far
+    step = groups
+    received = []
+    while step < devices:
+        ways = 4 if 4 * step <= devices else 2
+        params = functools.reduce(jnp.add, received, params)
+        received = [swapped(params, way * step) for way in range(1, ways)]
+        step *= ways
+    small = call(
+        join_small_kernel,
+        table,
+        [params] + received + list(grad_steps),
+        [None] * (1 + len(received) + groups),
+        [((8, width + 256 + 2 * tokens), F32)] * groups,
+        name="join_small",
+    )
+    pr = [small[0]] + [swapped(small[k], k) for k in range(1, groups)]
     grad_conv, grad_heads = call(
         functools.partial(join_params_kernel, scale=(tokens * devices) ** (-0.5), **shapes),
         table,
@@ -765,14 +964,13 @@
     grad_input, grad_step = call(
         functools.partial(join_grad_kernel, **shapes),
         table,
-        br,
-        [None] * groups,
-        [((tokens, channels), BF16), ((tokens, heads), F32)],
-        [((heads, tokens), F32)],
+        br + pr,
+        [None] * (2 * groups),
+        [((tokens, channels), BF16), ((heads, tokens), F32)],
         name="join_grad",
         vmem=False,
     )
-    return mixer_out, grad_input, grad_step, grad_conv, grad_heads
+    return mixer_out, grad_input, grad_step.T, grad_conv, grad_heads
 
 
 def solution(mesh):

time: 144 us -> 116 us (0.81)
  local copies, waits for them, and re-layouts: 23.2 us -> 5.27 us
  Pallas kernels: 57.9 us -> 47.5 us
  waiting for transfers between devices: 16 us -> 23 us
  starting transfers between devices: 43.6 us -> 38.2 us
    unnamed x78 -> x16, local copies, waits for them, and re-layouts: 21.6 us -> 5.27 us
    pallas_call x13 -> x18, Pallas kernels: 57.9 us -> 47.5 us  [call(): pl.pallas_call(kernel, out_shape=[pltpu.VMEM(shape, kind) if vmem else ja...]
    ppermute x17 -> x18, waiting for transfers between devices: 10.6 us -> 18 us  [swapped(): return lax.ppermute(value, 'ctx', [(i, i ^ bits) for i in range(count)])]
    ppermute x17 -> x18, starting transfers between devices: 26.8 us -> 23.4 us  [swapped(): return lax.ppermute(value, 'ctx', [(i, i ^ bits) for i in range(count)])]
    ppermute x5, starting transfers between devices: 14.2 us -> 12.2 us  [shifted(): return lax.ppermute(value, 'ctx', pairs)]
  transfers between devices with their start and end apart: 26 -> 27, of which waited for: 6 -> 9; matrix products, arithmetic and copies ran while one was open for 1% -> 0% of each run, Pallas kernels for 36% -> 38%
where the time goes in v2:
time: 116 us
  Pallas kernels  47.5 us (41%)
  starting transfers between devices  38.2 us (33%)
  waiting for transfers between devices  23 us (20%)
  local copies, waits for them, and re-layouts  5.27 us (5%)
    pallas_call x18, Pallas kernels, call(): pl.pallas_call(kernel, out_shape=[pltpu.VMEM(shape, kind) if vmem else ja...  47.5 us
    ppermute x18, starting transfers between devices, swapped(): return lax.ppermute(value, 'ctx', [(i, i ^ bits) for i in range(count)])  23.4 us
    ppermute x18, waiting for transfers between devices, swapped(): return lax.ppermute(value, 'ctx', [(i, i ^ bits) for i in range(count)])  18 us
    ppermute x5, starting transfers between devices, shifted(): return lax.ppermute(value, 'ctx', pairs)  12.2 us
    unnamed x16, local copies, waits for them, and re-layouts  5.27 us
    ppermute x5, waiting for transfers between devices, shifted(): return lax.ppermute(value, 'ctx', pairs)  4.98 us
    ppermute x4, starting transfers between devices, body(): rims.append(lax.ppermute(edges[k], 'ctx', pairs))  2.64 us
  transfers between devices with their start and end apart: 27, of which 9 were waited for; matrix products, arithmetic and copies ran while one was open for 0% of the time, Pallas kernels for 38%

profile of v2, /device:TPU:0, one launch (start us, length us, event | category | flops | bytes accessed | tf_op | source)
XLA Modules:
  0.0 115.7 jit_solution(4186480096819743933)
XLA Ops:
  1.4 1.3 %copy-done.1 = bf16[128,5120]{1,0:T(8,128)(2,1)S(1)} copy-done((bf16[128,5120]{1,0:T(8,128)(2,1)S(1)}, bf16[128,5120]{1,0:T(8,128)(2,1)}, u32[]{:S(2)}) %copy-start.1) | copy-done | bytes 1310744
  4.7 2.6 %collective-permute-start.4 = (bf16[128,1408]{1,0:T(8,128)(2,1)S(1)}, bf16[128,1408]{1,0:T(8,128)(2,1)S(1)}, u32[]{:S(2)}, u32[]{:S(2)}) collective-permute-start(bf16[128,1408]{1,0:T(8,128)(2,1)S(1)} %get-tuple-element.119), channel_id=1, source_target_pairs={{0,2},{1,3},{2,0},{3,1},{4,6},{5,7},{6,4},{7,5},{8,10},{9,11},{10,... | collective-permute-start | bytes 1081352 | tf_op jit(solution)/shard_map/ppermute | solution.py:692
  13.9 2.5 %conv.1 = (f32[4,128,1280]{2,1,0:T(8,128)S(1)}, f32[4,128,1280]{2,1,0:T(8,128)S(1)}, bf16[528,1280]{1,0:T(8,128)(2,1)S(1)}) custom-call(s32[6]{0:T(128)S(1)} %pad_add_fusion.s, bf16[128,1408]{1,0:T(8,128)(2,1)S(1)} %get-tuple-element.108.x0, bf16[128,1408]{1,0:T(8,128)(2,1)S(1)} %collective-permute-done.x1, f32[4,5120]{1,0:T(4,128)S(1)} %copy-done, ...), custom_call_target="tpu_custom_call" | custom-call | flops 1 | bytes 1 | tf_op jit(solution)/shard_map/conv/pallas_call | solution.py:670
  16.4 6.9 %collective-permute-start.1 = (bf16[128,1024]{1,0:T(8,128)(2,1)S(1)}, bf16[128,1024]{1,0:T(8,128)(2,1)S(1)}, u32[]{:S(2)}, u32[]{:S(2)}) collective-permute-start(bf16[128,1024]{1,0:T(8,128)(2,1)S(1)} %get-tuple-element.116), channel_id=1, source_target_pairs={{0,1},{1,0},{2,3},{3,2},{4,5},{5,4},{6,7},{7,6},{8,9},{9,8},{10,11... | collective-permute-start | bytes 786440 | tf_op jit(solution)/shard_map/ppermute | solution.py:692
  23.6 2.1 %collective-permute-start.3 = (bf16[128,1024]{1,0:T(8,128)(2,1)S(1)}, bf16[128,1024]{1,0:T(8,128)(2,1)S(1)}, u32[]{:S(2)}, u32[]{:S(2)}) collective-permute-start(bf16[128,1024]{1,0:T(8,128)(2,1)S(1)} %get-tuple-element.118), channel_id=1, source_target_pairs={{0,3},{1,2},{2,1},{3,0},{4,7},{5,6},{6,5},{7,4},{8,11},{9,10},{10,... | collective-permute-start | bytes 786440 | tf_op jit(solution)/shard_map/ppermute | solution.py:692
  25.7 4.6 %conv_state.1 = (f32[4,128,1280]{2,1,0:T(8,128)S(1)}, f32[4,128,1280]{2,1,0:T(8,128)S(1)}, bf16[528,1280]{1,0:T(8,128)(2,1)S(1)}, f32[136,1024]{1,0:T(8,128)S(1)...) custom-call(s32[6]{0:T(128)S(1)} %pad_add_fusion.s, ...), custom_call_target="tpu_custom_call", output_to_operand_aliasing={{0}: (16, {}), {1}: (17, {}), {2}: (18, {})} | custom-call | flops 1 | bytes 1 | tf_op jit(solution)/shard_map/conv_state/pallas_call | solution.py:670
  30.3 3.5 %collective-permute-start.11 = (f32[136,1024]{1,0:T(8,128)S(1)}, f32[136,1024]{1,0:T(8,128)S(1)}, u32[]{:S(2)}, u32[]{:S(2)}) collective-permute-start(f32[136,1024]{1,0:T(8,128)S(1)} %get-tuple-element.131.pay_in.pay), channel_id=1, source_target_pairs={{0,4},{1,5},{2,6},{3,7},{4,8},{5,9},{6,10},{7,11},{8,12},{9,13},{1... | collective-permute-start | bytes 1671176 | tf_op jit(solution)/shard_map/ppermute | solution.py:698
  33.8 4.2 %collective-permute-done.3.g3 = bf16[128,1024]{1,0:T(8,128)(2,1)S(1)} collective-permute-done((bf16[128,1024]{1,0:T(8,128)(2,1)S(1)}, bf16[128,1024]{1,0:T(8,128)(2,1)S(1)}, u32[]{:S(2)}, u32[]{:S(2)}) %collective-permute-start.3) | collective-permute-done | bytes 262176 | tf_op jit(solution)/shard_map/ppermute | solution.py:692
  38.1 2.4 %grad_state.1 = (bf16[4,128,1024]{2,1,0:T(8,128)(2,1)S(1)}, f32[136,1024]{1,0:T(8,128)S(1)}, f32[4,128,1024]{2,1,0:T(8,128)S(1)}) custom-call(s32[6]{0:T(128)S(1)} %pad_add_fusion.s, bf16[128,1024]{1,0:T(8,128)(2,1)S(1)} %get-tuple-element.115.g0, bf16[128,1024]{1,0:T(8,128)(2,1)S(1)} %collective-permute-done.1.g1, ...), custom_call_target="tpu_custom_call" | custom-call | flops 1 | bytes 1 | tf_op jit(solution)/shard_map/grad_state/pallas_call | solution.py:670
  40.5 1.3 %collective-permute-start.10 = (f32[136,1024]{1,0:T(8,128)S(1)}, f32[136,1024]{1,0:T(8,128)S(1)}, u32[]{:S(2)}, u32[]{:S(2)}) collective-permute-start(f32[136,1024]{1,0:T(8,128)S(1)} %get-tuple-element.132), channel_id=1, source_target_pairs={{4,0},{5,1},{6,2},{7,3},{8,4},{9,5},{10,6},{11,7},{12,8},{13,9},{1... | collective-permute-start | bytes 1671176 | tf_op jit(solution)/shard_map/ppermute | solution.py:698
  41.8 7.4 %local.3 = (f32[4,128,1024]{2,1,0:T(8,128)S(1)}, f32[4,128,1024]{2,1,0:T(8,128)S(1)}, f32[4,128,128]{2,1,0:T(8,128)S(1)}, f32[4,128,128]{2,1,0:T(8,128)S(1)}, f3...) custom-call(s32[6]{0:T(128)S(1)} %pad_add_fusion.s, f32[4,128,1280]{2,1,0:T(8,128)S(1)} %get-tuple-element.129.act_ref, ...), custom_call_target="tpu_custom_call" | custom-call | flops 1 | bytes 1 | tf_op jit(solution)/shard_map/local/pallas_call | solution.py:670
  49.2 4.8 %collective-permute-start.13 = (f32[136,1024]{1,0:T(8,128)S(1)}, f32[136,1024]{1,0:T(8,128)S(1)}, u32[]{:S(2)}, u32[]{:S(2)}) collective-permute-start(f32[136,1024]{1,0:T(8,128)S(1)} %collective-permute-done.11.one), channel_id=1, source_target_pairs={{0,4},{1,5},{2,6},{3,7},{4,8},{5,9},{6,10},{7,11},{8,12},{9,13},{1... | collective-permute-start | bytes 1671176 | tf_op jit(solution)/shard_map/ppermute | solution.py:698
  53.9 3.9 %local.4 = (f32[4,128,1024]{2,1,0:T(8,128)S(1)}, f32[4,128,1024]{2,1,0:T(8,128)S(1)}, f32[4,128,128]{2,1,0:T(8,128)S(1)}, f32[4,128,128]{2,1,0:T(8,128)S(1)}, f3...) custom-call(s32[6]{0:T(128)S(1)} %pad_add_fusion.s, ...), custom_call_target="tpu_custom_call", output_to_operand_aliasing={{0}: (6, {}), {1}: (7, {}), {2}: (8, {}), {3}: (9, {}), {4}... | custom-call | flops 1 | bytes 1 | tf_op jit(solution)/shard_map/local/pallas_call | solution.py:670
  59.2 3.9 %local.5 = (f32[4,128,1024]{2,1,0:T(8,128)S(1)}, f32[4,128,1024]{2,1,0:T(8,128)S(1)}, f32[4,128,128]{2,1,0:T(8,128)S(1)}, f32[4,128,128]{2,1,0:T(8,128)S(1)}, f3...) custom-call(s32[6]{0:T(128)S(1)} %pad_add_fusion.s, ...), custom_call_target="tpu_custom_call", output_to_operand_aliasing={{0}: (6, {}), {1}: (7, {}), {2}: (8, {}), {3}: (9, {}), {4}... | custom-call | flops 1 | bytes 1 | tf_op jit(solution)/shard_map/local/pallas_call | solution.py:670
  63.1 2.4 %collective-permute-done.13.two = f32[136,1024]{1,0:T(8,128)S(1)} collective-permute-done((f32[136,1024]{1,0:T(8,128)S(1)}, f32[136,1024]{1,0:T(8,128)S(1)}, u32[]{:S(2)}, u32[]{:S(2)}) %collective-permute-start.13) | collective-permute-done | bytes 557088 | tf_op jit(solution)/shard_map/ppermute | solution.py:698
  65.6 3.8 %out.1 = (bf16[128,1024]{1,0:T(8,128)(2,1)S(1)}, bf16[128,1024]{1,0:T(8,128)(2,1)S(1)}, bf16[128,1024]{1,0:T(8,128)(2,1)S(1)}, bf16[128,1024]{1,0:T(8,128)(2,1)S...) custom-call(s32[6]{0:T(128)S(1)} %pad_add_fusion.s, ...), custom_call_target="tpu_custom_call" | custom-call | flops 1 | bytes 1 | tf_op jit(solution)/shard_map/out/pallas_call | solution.py:670
  69.5 1.8 %collective-permute-start.17 = (bf16[128,1024]{1,0:T(8,128)(2,1)S(1)}, bf16[128,1024]{1,0:T(8,128)(2,1)S(1)}, u32[]{:S(2)}, u32[]{:S(2)}) collective-permute-start(bf16[128,1024]{1,0:T(8,128)(2,1)S(1)} %get-tuple-element.183), channel_id=1, source_target_pairs={{0,3},{1,2},{2,1},{3,0},{4,7},{5,6},{6,5},{7,4},{8,11},{9,10},{10,... | collective-permute-start | bytes 786440 | tf_op jit(solution)/shard_map/ppermute | solution.py:692
  71.3 2.5 %collective-permute-done.12.two = f32[136,1024]{1,0:T(8,128)S(1)} collective-permute-done((f32[136,1024]{1,0:T(8,128)S(1)}, f32[136,1024]{1,0:T(8,128)S(1)}, u32[]{:S(2)}, u32[]{:S(2)}) %collective-permute-start.12) | collective-permute-done | bytes 557088 | tf_op jit(solution)/shard_map/ppermute | solution.py:698
  75.0 1.3 %collective-permute-start.14 = (f32[8,1280]{1,0:T(8,128)S(1)}, f32[8,1280]{1,0:T(8,128)S(1)}, u32[]{:S(2)}, u32[]{:S(2)}) collective-permute-start(f32[8,1280]{1,0:T(8,128)S(1)} %get-tuple-element.179), channel_id=1, source_target_pairs={{4,0},{5,1},{6,2},{7,3},{8,4},{9,5},{10,6},{11,7},{12,8},{13,9},{1... | collective-permute-start | bytes 122888 | tf_op jit(solution)/shard_map/ppermute | solution.py:698
  76.3 3.9 %back_far.1 = (f32[512,1280]{1,0:T(8,128)S(1)}, f32[8,1536]{1,0:T(8,128)S(1)}, f32[3,16,128]{2,1,0:T(8,128)S(1)}) custom-call(s32[6]{0:T(128)S(1)} %pad_add_fusion.s, bf16[128,1024]{1,0:T(8,128)(2,1)S(1)} %get-tuple-element.168.high_ref, bf16[128,1024]{1,0:T(8,128)(2,1)S(1)} %get-tuple-element.169.low_ref, f32[4,128,1280]{2,1,0:T(8,128)S(1)} %get-tuple-element.129.act_ref, ...), custom_call_target="tpu_custom_call" | custom-call | flops 1 | bytes 1 | tf_op jit(solution)/shard_map/back_far/pallas_call | solution.py:670
  80.2 3.1 %collective-permute-done.17.p3 = bf16[128,1024]{1,0:T(8,128)(2,1)S(1)} collective-permute-done((bf16[128,1024]{1,0:T(8,128)(2,1)S(1)}, bf16[128,1024]{1,0:T(8,128)(2,1)S(1)}, u32[]{:S(2)}, u32[]{:S(2)}) %collective-permute-start.17) | collective-permute-done | bytes 262176 | tf_op jit(solution)/shard_map/ppermute | solution.py:692
  83.3 1.6 %conv_back_far.1 = (bf16[128,1280]{1,0:T(8,128)(2,1)S(1)}, bf16[128,1280]{1,0:T(8,128)(2,1)S(1)}) custom-call(s32[6]{0:T(128)S(1)} %pad_add_fusion.s, f32[512,1280]{1,0:T(8,128)S(1)} %get-tuple-element.186.du_ref.du_in, f32[8,1280]{1,0:T(8,128)S(1)} %collective-permute-done.14.rim_ref, f32[4,5120]{1,0:T(4,128)S(1)} %copy-done, f32[4,5120]{1,0:T(4,128)S(1)} %copy-done, ...), custom_call_target="tpu_custom_call" | custom-call | flops 1 | bytes 1 | tf_op jit(solution)/shard_map/conv_back_far/pallas_call | solution.py:670
  86.6 1.6 %join_out.1 = bf16[128,4096]{1,0:T(8,128)(2,1)} custom-call(s32[6]{0:T(128)S(1)} %pad_add_fusion.s, bf16[128,1024]{1,0:T(8,128)(2,1)S(1)} %get-tuple-element.188.p0, bf16[128,1024]{1,0:T(8,128)(2,1)S(1)} %collective-permute-done.15.p1, bf16[128,1024]{1,0:T(8,128)(2,1)S(1)} %collective-permute-done.16.p2, bf16[128,1024]{1,0:T(8,128)(2,1)S(1)} %collective-permute-done.17.p3), custom_call_target="tpu_custom_call" | custom-call | flops 1 | bytes 1 | tf_op jit(solution)/shard_map/join_out/pallas_call | solution.py:670
  88.2 4.5 %back_near.1 = (f32[512,1280]{1,0:T(8,128)S(1)}, f32[8,1536]{1,0:T(8,128)S(1)}, f32[16,128]{1,0:T(8,128)S(1)}, f32[16,128]{1,0:T(8,128)S(1)}, f32[16,128]{1,0:T(8,128)S(1)}, /*index=5*/f32[16,128]{1,0:T(8,128)S(1)}) custom-call(s32[6]{0:T(128)S(1)} %pad_add_fusion.s, ...), custom_call_target="tpu_custom_call", output_to_operand_aliasing={{0}: (20, {})} | custom-call | flops 1 | bytes 1 | tf_op jit(solution)/shard_map/back_near/pallas_call | solution.py:670
  92.6 2.9 %collective-permute-done.18.p2 = bf16[128,1280]{1,0:T(8,128)(2,1)S(1)} collective-permute-done((bf16[128,1280]{1,0:T(8,128)(2,1)S(1)}, bf16[128,1280]{1,0:T(8,128)(2,1)S(1)}, u32[]{:S(2)}, u32[]{:S(2)}) %collective-permute-start.18) | collective-permute-done | bytes 327712 | tf_op jit(solution)/shard_map/ppermute | solution.py:692
  95.5 1.6 %conv_back_near.1 = (bf16[128,1280]{1,0:T(8,128)(2,1)S(1)}, bf16[128,1280]{1,0:T(8,128)(2,1)S(1)}) custom-call(s32[6]{0:T(128)S(1)} %pad_add_fusion.s, f32[512,1280]{1,0:T(8,128)S(1)} %get-tuple-element.193.du_ref, f32[8,1280]{1,0:T(8,128)S(1)} %collective-permute-done.14.rim_ref, f32[4,5120]{1,0:T(4,128)S(1)} %copy-done, f32[4,5120]{1,0:T(4,128)S(1)} %copy-done, ...), custom_call_target="tpu_custom_call" | custom-call | flops 1 | bytes 1 | tf_op jit(solution)/shard_map/conv_back_near/pallas_call | solution.py:670
  97.2 4.7 %collective-permute-start.23 = (f32[8,1536]{1,0:T(8,128)S(1)}, f32[8,1536]{1,0:T(8,128)S(1)}, u32[]{:S(2)}, u32[]{:S(2)}) collective-permute-start(f32[8,1536]{1,0:T(8,128)S(1)} %get-tuple-element.198.first), channel_id=1, source_target_pairs={{0,12},{1,13},{2,14},{3,15},{4,8},{5,9},{6,10},{7,11},{8,4},{9,5},... | collective-permute-start | bytes 147464 | tf_op jit(solution)/shard_map/ppermute | solution.py:692
  102.5 1.8 %collective-permute-done.23.refs_2_ = f32[8,1536]{1,0:T(8,128)S(1)} collective-permute-done((f32[8,1536]{1,0:T(8,128)S(1)}, f32[8,1536]{1,0:T(8,128)S(1)}, u32[]{:S(2)}, u32[]{:S(2)}) %collective-permute-start.23) | collective-permute-done | bytes 49184 | tf_op jit(solution)/shard_map/ppermute | solution.py:692
  104.3 2.7 %collective-permute-done.22.refs_1_ = f32[8,1536]{1,0:T(8,128)S(1)} collective-permute-done((f32[8,1536]{1,0:T(8,128)S(1)}, f32[8,1536]{1,0:T(8,128)S(1)}, u32[]{:S(2)}, u32[]{:S(2)}) %collective-permute-start.22) | collective-permute-done | bytes 49184 | tf_op jit(solution)/shard_map/ppermute | solution.py:692
  108.2 1.3 %collective-permute-start.26 = (f32[8,1792]{1,0:T(8,128)S(1)}, f32[8,1792]{1,0:T(8,128)S(1)}, u32[]{:S(2)}, u32[]{:S(2)}) collective-permute-start(f32[8,1792]{1,0:T(8,128)S(1)} %get-tuple-element.206), channel_id=1, source_target_pairs={{0,3},{1,2},{2,1},{3,0},{4,7},{5,6},{6,5},{7,4},{8,11},{9,10},{10,... | collective-permute-start | bytes 172040 | tf_op jit(solution)/shard_map/ppermute | solution.py:692
  109.5 2.9 %collective-permute-done.25.g2.p2 = f32[8,1792]{1,0:T(8,128)S(1)} collective-permute-done((f32[8,1792]{1,0:T(8,128)S(1)}, f32[8,1792]{1,0:T(8,128)S(1)}, u32[]{:S(2)}, u32[]{:S(2)}) %collective-permute-start.25) | collective-permute-done | bytes 57376 | tf_op jit(solution)/shard_map/ppermute | solution.py:692
  114.0 1.7 %join_grad.1 = (bf16[128,5120]{1,0:T(8,128)(2,1)}, f32[64,128]{1,0:T(8,128)}) custom-call(s32[6]{0:T(128)S(1)} %pad_add_fusion.s, bf16[128,1280]{1,0:T(8,128)(2,1)S(1)} %get-tuple-element.194.p0, bf16[128,1280]{1,0:T(8,128)(2,1)S(1)} %collective-permute-done.19.p1, bf16[128,1280]{1,0:T(8,128)(2,1)S(1)} %collective-permute-done.18.p2, ...), custom_call_target="tpu_custom_call" | custom-call | flops 1 | bytes 1 | tf_op jit(solution)/shard_map/join_grad/pallas_call | solution.py:670
  (57 shorter events, 17.4 us)
Async XLA Ops:
  0.6 13.3 %copy-start = (f32[4,5120]{1,0:T(4,128)S(1)}, f32[4,5120]{1,0:T(4,128)}, u32[]{:S(2)}) copy-start(f32[4,5120]{1,0:T(4,128)} %wc.7) | copy-start | bytes 245764
  1.4 1.3 %copy-start.1 = (bf16[128,5120]{1,0:T(8,128)(2,1)S(1)}, bf16[128,5120]{1,0:T(8,128)(2,1)}, u32[]{:S(2)}) copy-start(bf16[128,5120]{1,0:T(8,128)(2,1)} %x_ref.1) | copy-start | bytes 3932164
  2.7 0.8 copy-start.4
  3.5 10.4 %copy-start.3 = (f32[5120]{0:T(1024)S(1)}, f32[5120]{0:T(1024)}, u32[]{:S(2)}) copy-start(f32[5120]{0:T(1024)} %param.15) | copy-start | bytes 61444
  4.2 5.2 %collective-permute-start = (bf16[128,1408]{1,0:T(8,128)(2,1)S(1)}, bf16[128,1408]{1,0:T(8,128)(2,1)S(1)}, u32[]{:S(2)}, u32[]{:S(2)}) collective-permute-start(bf16[128,1408]{1,0:T(8,128)(2,1)S(1)} %get-tuple-element.109), channel_id=1, source_target_pairs={{0,1},{1,0},{2,3},{3,2},{4,5},{5,4},{6,7},{7,6},{8,9},{9,8},{10,11... | collective-permute-start | bytes 1081352 | tf_op jit(solution)/shard_map/ppermute | solution.py:692
  4.7 21.0 %collective-permute-start.4 = (bf16[128,1408]{1,0:T(8,128)(2,1)S(1)}, bf16[128,1408]{1,0:T(8,128)(2,1)S(1)}, u32[]{:S(2)}, u32[]{:S(2)}) collective-permute-start(bf16[128,1408]{1,0:T(8,128)(2,1)S(1)} %get-tuple-element.119), channel_id=1, source_target_pairs={{0,2},{1,3},{2,0},{3,1},{4,6},{5,7},{6,4},{7,5},{8,10},{9,11},{10,... | collective-permute-start | bytes 1081352 | tf_op jit(solution)/shard_map/ppermute | solution.py:692
  7.3 18.4 %collective-permute-start.5 = (bf16[128,1408]{1,0:T(8,128)(2,1)S(1)}, bf16[128,1408]{1,0:T(8,128)(2,1)S(1)}, u32[]{:S(2)}, u32[]{:S(2)}) collective-permute-start(bf16[128,1408]{1,0:T(8,128)(2,1)S(1)} %get-tuple-element.120), channel_id=1, source_target_pairs={{0,3},{1,2},{2,1},{3,0},{4,7},{5,6},{6,5},{7,4},{8,11},{9,10},{10,... | collective-permute-start | bytes 1081352 | tf_op jit(solution)/shard_map/ppermute | solution.py:692
  7.4 1.3 %collective-permute-start.6 = (bf16[16,1280]{1,0:T(8,128)(2,1)S(1)}, bf16[16,1280]{1,0:T(8,128)(2,1)S(1)}, u32[]{:S(2)}, u32[]{:S(2)}) collective-permute-start(bf16[16,1280]{1,0:T(8,128)(2,1)S(1)} %get-tuple-element.121), channel_id=1, source_target_pairs={{3,7},{7,11},{11,15},{19,23},{23,27},{27,31}} | collective-permute-start | bytes 122888 | tf_op jit(solution)/shard_map/ppermute | solution.py:780
  8.0 8.4 %collective-permute-start.7 = (bf16[16,1280]{1,0:T(8,128)(2,1)S(1)}, bf16[16,1280]{1,0:T(8,128)(2,1)S(1)}, u32[]{:S(2)}, u32[]{:S(2)}) collective-permute-start(bf16[16,1280]{1,0:T(8,128)(2,1)S(1)} %get-tuple-element.122), channel_id=1, source_target_pairs={{3,6},{7,10},{11,14},{19,22},{23,26},{27,30}} | collective-permute-start | bytes 122888 | tf_op jit(solution)/shard_map/ppermute | solution.py:780
  8.7 14.6 %collective-permute-start.8 = (bf16[16,1280]{1,0:T(8,128)(2,1)S(1)}, bf16[16,1280]{1,0:T(8,128)(2,1)S(1)}, u32[]{:S(2)}, u32[]{:S(2)}) collective-permute-start(bf16[16,1280]{1,0:T(8,128)(2,1)S(1)} %get-tuple-element.123), channel_id=1, source_target_pairs={{1,3},{3,5},{5,7},{7,9},{9,11},{11,13},{13,15},{17,19},{19,21},{21... | collective-permute-start | bytes 122888 | tf_op jit(solution)/shard_map/ppermute | solution.py:780
  9.4 14.2 %collective-permute-start.9 = (bf16[16,1280]{1,0:T(8,128)(2,1)S(1)}, bf16[16,1280]{1,0:T(8,128)(2,1)S(1)}, u32[]{:S(2)}, u32[]{:S(2)}) collective-permute-start(bf16[16,1280]{1,0:T(8,128)(2,1)S(1)} %get-tuple-element.124), channel_id=1, source_target_pairs={{1,2},{3,4},{5,6},{7,8},{9,10},{11,12},{13,14},{17,18},{19,20},{21... | collective-permute-start | bytes 122888 | tf_op jit(solution)/shard_map/ppermute | solution.py:780
  10.1 1.2 %copy-start.2 = (bf16[128,4096]{1,0:T(8,128)(2,1)S(1)}, bf16[128,4096]{1,0:T(8,128)(2,1)}, u32[]{:S(2)}) copy-start(bf16[128,4096]{1,0:T(8,128)(2,1)} %g_ref.1) | copy-start | bytes 3145732
  16.4 17.4 %collective-permute-start.1 = (bf16[128,1024]{1,0:T(8,128)(2,1)S(1)}, bf16[128,1024]{1,0:T(8,128)(2,1)S(1)}, u32[]{:S(2)}, u32[]{:S(2)}) collective-permute-start(bf16[128,1024]{1,0:T(8,128)(2,1)S(1)} %get-tuple-element.116), channel_id=1, source_target_pairs={{0,1},{1,0},{2,3},{3,2},{4,5},{5,4},{6,7},{7,6},{8,9},{9,8},{10,11... | collective-permute-start | bytes 786440 | tf_op jit(solution)/shard_map/ppermute | solution.py:692
  23.3 10.5 %collective-permute-start.2 = (bf16[128,1024]{1,0:T(8,128)(2,1)S(1)}, bf16[128,1024]{1,0:T(8,128)(2,1)S(1)}, u32[]{:S(2)}, u32[]{:S(2)}) collective-permute-start(bf16[128,1024]{1,0:T(8,128)(2,1)S(1)} %get-tuple-element.117), channel_id=1, source_target_pairs={{0,2},{1,3},{2,0},{3,1},{4,6},{5,7},{6,4},{7,5},{8,10},{9,11},{10,... | collective-permute-start | bytes 786440 | tf_op jit(solution)/shard_map/ppermute | solution.py:692
  23.6 14.5 %collective-permute-start.3 = (bf16[128,1024]{1,0:T(8,128)(2,1)S(1)}, bf16[128,1024]{1,0:T(8,128)(2,1)S(1)}, u32[]{:S(2)}, u32[]{:S(2)}) collective-permute-start(bf16[128,1024]{1,0:T(8,128)(2,1)S(1)} %get-tuple-element.118), channel_id=1, source_target_pairs={{0,3},{1,2},{2,1},{3,0},{4,7},{5,6},{6,5},{7,4},{8,11},{9,10},{10,... | collective-permute-start | bytes 786440 | tf_op jit(solution)/shard_map/ppermute | solution.py:692
  30.3 18.9 %collective-permute-start.11 = (f32[136,1024]{1,0:T(8,128)S(1)}, f32[136,1024]{1,0:T(8,128)S(1)}, u32[]{:S(2)}, u32[]{:S(2)}) collective-permute-start(f32[136,1024]{1,0:T(8,128)S(1)} %get-tuple-element.131.pay_in.pay), channel_id=1, source_target_pairs={{0,4},{1,5},{2,6},{3,7},{4,8},{5,9},{6,10},{7,11},{8,12},{9,13},{1... | collective-permute-start | bytes 1671176 | tf_op jit(solution)/shard_map/ppermute | solution.py:698
  40.5 17.4 %collective-permute-start.10 = (f32[136,1024]{1,0:T(8,128)S(1)}, f32[136,1024]{1,0:T(8,128)S(1)}, u32[]{:S(2)}, u32[]{:S(2)}) collective-permute-start(f32[136,1024]{1,0:T(8,128)S(1)} %get-tuple-element.132), channel_id=1, source_target_pairs={{4,0},{5,1},{6,2},{7,3},{8,4},{9,5},{10,6},{11,7},{12,8},{13,9},{1... | collective-permute-start | bytes 1671176 | tf_op jit(solution)/shard_map/ppermute | solution.py:698
  49.2 16.4 %collective-permute-start.13 = (f32[136,1024]{1,0:T(8,128)S(1)}, f32[136,1024]{1,0:T(8,128)S(1)}, u32[]{:S(2)}, u32[]{:S(2)}) collective-permute-start(f32[136,1024]{1,0:T(8,128)S(1)} %collective-permute-done.11.one), channel_id=1, source_target_pairs={{0,4},{1,5},{2,6},{3,7},{4,8},{5,9},{6,10},{7,11},{8,12},{9,13},{1... | collective-permute-start | bytes 1671176 | tf_op jit(solution)/shard_map/ppermute | solution.py:698
  57.9 16.0 %collective-permute-start.12 = (f32[136,1024]{1,0:T(8,128)S(1)}, f32[136,1024]{1,0:T(8,128)S(1)}, u32[]{:S(2)}, u32[]{:S(2)}) collective-permute-start(f32[136,1024]{1,0:T(8,128)S(1)} %collective-permute-done.10.one), channel_id=1, source_target_pairs={{4,0},{5,1},{6,2},{7,3},{8,4},{9,5},{10,6},{11,7},{12,8},{13,9},{1... | collective-permute-start | bytes 1671176 | tf_op jit(solution)/shard_map/ppermute | solution.py:698
  69.4 10.8 %collective-permute-start.15 = (bf16[128,1024]{1,0:T(8,128)(2,1)S(1)}, bf16[128,1024]{1,0:T(8,128)(2,1)S(1)}, u32[]{:S(2)}, u32[]{:S(2)}) collective-permute-start(bf16[128,1024]{1,0:T(8,128)(2,1)S(1)} %get-tuple-element.181), channel_id=1, source_target_pairs={{0,1},{1,0},{2,3},{3,2},{4,5},{5,4},{6,7},{7,6},{8,9},{9,8},{10,11... | collective-permute-start | bytes 786440 | tf_op jit(solution)/shard_map/ppermute | solution.py:692
  69.4 10.8 %collective-permute-start.16 = (bf16[128,1024]{1,0:T(8,128)(2,1)S(1)}, bf16[128,1024]{1,0:T(8,128)(2,1)S(1)}, u32[]{:S(2)}, u32[]{:S(2)}) collective-permute-start(bf16[128,1024]{1,0:T(8,128)(2,1)S(1)} %get-tuple-element.182), channel_id=1, source_target_pairs={{0,2},{1,3},{2,0},{3,1},{4,6},{5,7},{6,4},{7,5},{8,10},{9,11},{10,... | collective-permute-start | bytes 786440 | tf_op jit(solution)/shard_map/ppermute | solution.py:692
  69.5 13.8 %collective-permute-start.17 = (bf16[128,1024]{1,0:T(8,128)(2,1)S(1)}, bf16[128,1024]{1,0:T(8,128)(2,1)S(1)}, u32[]{:S(2)}, u32[]{:S(2)}) collective-permute-start(bf16[128,1024]{1,0:T(8,128)(2,1)S(1)} %get-tuple-element.183), channel_id=1, source_target_pairs={{0,3},{1,2},{2,1},{3,0},{4,7},{5,6},{6,5},{7,4},{8,11},{9,10},{10,... | collective-permute-start | bytes 786440 | tf_op jit(solution)/shard_map/ppermute | solution.py:692
  75.0 8.3 %collective-permute-start.14 = (f32[8,1280]{1,0:T(8,128)S(1)}, f32[8,1280]{1,0:T(8,128)S(1)}, u32[]{:S(2)}, u32[]{:S(2)}) collective-permute-start(f32[8,1280]{1,0:T(8,128)S(1)} %get-tuple-element.179), channel_id=1, source_target_pairs={{4,0},{5,1},{6,2},{7,3},{8,4},{9,5},{10,6},{11,7},{12,8},{13,9},{1... | collective-permute-start | bytes 122888 | tf_op jit(solution)/shard_map/ppermute | solution.py:698
  84.9 10.6 %collective-permute-start.18 = (bf16[128,1280]{1,0:T(8,128)(2,1)S(1)}, bf16[128,1280]{1,0:T(8,128)(2,1)S(1)}, u32[]{:S(2)}, u32[]{:S(2)}) collective-permute-start(bf16[128,1280]{1,0:T(8,128)(2,1)S(1)} %get-tuple-element.185), channel_id=1, source_target_pairs={{0,2},{1,3},{2,0},{3,1},{4,6},{5,7},{6,4},{7,5},{8,10},{9,11},{10,... | collective-permute-start | bytes 983048 | tf_op jit(solution)/shard_map/ppermute | solution.py:692
  85.4 28.6 %collective-permute-start.20 = (bf16[128,1280]{1,0:T(8,128)(2,1)S(1)}, bf16[128,1280]{1,0:T(8,128)(2,1)S(1)}, u32[]{:S(2)}, u32[]{:S(2)}) collective-permute-start(bf16[128,1280]{1,0:T(8,128)(2,1)S(1)} %get-tuple-element.197), channel_id=1, source_target_pairs={{0,3},{1,2},{2,1},{3,0},{4,7},{5,6},{6,5},{7,4},{8,11},{9,10},{10,... | collective-permute-start | bytes 983048 | tf_op jit(solution)/shard_map/ppermute | solution.py:692
  97.1 16.9 %collective-permute-start.19 = (bf16[128,1280]{1,0:T(8,128)(2,1)S(1)}, bf16[128,1280]{1,0:T(8,128)(2,1)S(1)}, u32[]{:S(2)}, u32[]{:S(2)}) collective-permute-start(bf16[128,1280]{1,0:T(8,128)(2,1)S(1)} %get-tuple-element.195), channel_id=1, source_target_pairs={{0,1},{1,0},{2,3},{3,2},{4,5},{5,4},{6,7},{7,6},{8,9},{9,8},{10,11... | collective-permute-start | bytes 983048 | tf_op jit(solution)/shard_map/ppermute | solution.py:692
  97.2 7.1 %collective-permute-start.23 = (f32[8,1536]{1,0:T(8,128)S(1)}, f32[8,1536]{1,0:T(8,128)S(1)}, u32[]{:S(2)}, u32[]{:S(2)}) collective-permute-start(f32[8,1536]{1,0:T(8,128)S(1)} %get-tuple-element.198.first), channel_id=1, source_target_pairs={{0,12},{1,13},{2,14},{3,15},{4,8},{5,9},{6,10},{7,11},{8,4},{9,5},... | collective-permute-start | bytes 147464 | tf_op jit(solution)/shard_map/ppermute | solution.py:692
  101.8 5.1 %collective-permute-start.22 = (f32[8,1536]{1,0:T(8,128)S(1)}, f32[8,1536]{1,0:T(8,128)S(1)}, u32[]{:S(2)}, u32[]{:S(2)}) collective-permute-start(f32[8,1536]{1,0:T(8,128)S(1)} %get-tuple-element.198.first), channel_id=1, source_target_pairs={{0,8},{1,9},{2,10},{3,11},{4,12},{5,13},{6,14},{7,15},{8,0},{9,1},... | collective-permute-start | bytes 147464 | tf_op jit(solution)/shard_map/ppermute | solution.py:692
  101.8 5.1 %collective-permute-start.21 = (f32[8,1536]{1,0:T(8,128)S(1)}, f32[8,1536]{1,0:T(8,128)S(1)}, u32[]{:S(2)}, u32[]{:S(2)}) collective-permute-start(f32[8,1536]{1,0:T(8,128)S(1)} %get-tuple-element.198.first), channel_id=1, source_target_pairs={{0,4},{1,5},{2,6},{3,7},{4,0},{5,1},{6,2},{7,3},{8,12},{9,13},{10,... | collective-permute-start | bytes 147464 | tf_op jit(solution)/shard_map/ppermute | solution.py:692
  107.6 1.9 %collective-permute-start.24 = (f32[8,1792]{1,0:T(8,128)S(1)}, f32[8,1792]{1,0:T(8,128)S(1)}, u32[]{:S(2)}, u32[]{:S(2)}) collective-permute-start(f32[8,1792]{1,0:T(8,128)S(1)} %get-tuple-element.204), channel_id=1, source_target_pairs={{0,1},{1,0},{2,3},{3,2},{4,5},{5,4},{6,7},{7,6},{8,9},{9,8},{10,11... | collective-permute-start | bytes 172040 | tf_op jit(solution)/shard_map/ppermute | solution.py:692
  107.6 4.8 %collective-permute-start.25 = (f32[8,1792]{1,0:T(8,128)S(1)}, f32[8,1792]{1,0:T(8,128)S(1)}, u32[]{:S(2)}, u32[]{:S(2)}) collective-permute-start(f32[8,1792]{1,0:T(8,128)S(1)} %get-tuple-element.205), channel_id=1, source_target_pairs={{0,2},{1,3},{2,0},{3,1},{4,6},{5,7},{6,4},{7,5},{8,10},{9,11},{10,... | collective-permute-start | bytes 172040 | tf_op jit(solution)/shard_map/ppermute | solution.py:692
  108.2 4.6 %collective-permute-start.26 = (f32[8,1792]{1,0:T(8,128)S(1)}, f32[8,1792]{1,0:T(8,128)S(1)}, u32[]{:S(2)}, u32[]{:S(2)}) collective-permute-start(f32[8,1792]{1,0:T(8,128)S(1)} %get-tuple-element.206), channel_id=1, source_target_pairs={{0,3},{1,2},{2,1},{3,0},{4,7},{5,6},{6,5},{7,4},{8,11},{9,10},{10,... | collective-permute-start | bytes 172040 | tf_op jit(solution)/shard_map/ppermute | solution.py:692
  (3 other events, 2.0 us)

commit v3 on v2

--- a/solution.py
+++ b/solution.py
@@ -501,17 +501,6 @@
     )
     aux_ref[0], aux_ref[1], aux_ref[2] = away[0], away[1], skips
 
-    @pl.when((s[0] & 2) == 2)
-    def _():
-        matrix = spread_matrix(share, headdim)
-        grads = input_grads(
-            2, 16, high_ref[...], low_ref[...], act_ref, dsl_ref, dxl_ref, dbl_ref, dc_ref,
-            gall_ref, vec_ref, skip_row(hpar, matrix), matrix, part, state,
-        )
-        du_ref[2 * tokens : 2 * tokens + 8, :part] = grads[0][:8]
-        du_ref[2 * tokens : 2 * tokens + 8, part : part + state] = grads[1][:8]
-        du_ref[2 * tokens : 2 * tokens + 8, part + state :] = grads[2][:8]
-
 
 def back_near_kernel(
     s, high_ref, low_ref, act_ref, dsl_ref, dxl_ref, dbl_ref, dc_ref, gall_ref, vec_ref, hpar,
@@ -835,7 +824,7 @@
         ((groups, share, tokens), F32),
     ]
     locals_ = []
-    for span in ((0, 2), (2, 3), (3, 4)):
+    for span in ((0, 1), (1, 2), (2, 4)):
         locals_ = call(
             functools.partial(local_kernel, span=span, docs=docs, **sizes),
             table,
@@ -846,10 +835,10 @@
             name="local",
             aliases={6 + i: i for i in range(len(locals_))},
         )
-        if span[1] == 2:
+        if span[1] == 1:
             s_near, *locals_ = lax.optimization_barrier((s_near, *locals_))
             s_far = shifted(s_near, GROUPS * covered)
-        elif span[1] == 3:
+        elif span[1] == 2:
             g_near, *locals_ = lax.optimization_barrier((g_near, *locals_))
             g_far = shifted(g_near, -GROUPS * covered)
     y_local, dx_local, db_local, dc_local, flow, xd = locals_
@@ -895,20 +884,6 @@
         [du_shape, par_shape, ((3, share, tokens), F32)],
         name="back_far",
     )
-    rim_back, *mr = lax.optimization_barrier((rim_back, *mr))
-    pair_shapes = [((tokens, width), BF16)] * 2
-    ext_back = [((2 * tokens + 8, width), F32)]
-    back_far = call(
-        functools.partial(conv_back_kernel, far=True, **settings),
-        table,
-        [du, rim_back] + [conv_weight] * 3,
-        [None] * 2 + column_specs(taps),
-        pair_shapes,
-        ext_back,
-        name="conv_back_far",
-    )
-    br_far = [swapped(back_far[k - 2], k) for k in (2, 3)]
-    du = after(du, back_far[0])
     du, params, *grad_steps = call(
         functools.partial(back_near_kernel, **settings),
         table,
@@ -920,21 +895,23 @@
         name="back_near",
         aliases={20: 0},
     )
-    (mixer_out,) = call(
-        join_kernel, table, mr, [None] * groups, [((tokens, inner), BF16)], name="join_out",
-        vmem=False,
-    )
-    du, br_far[0], mixer_out = lax.optimization_barrier((du, br_far[0], mixer_out))
-    back_near = call(
-        functools.partial(conv_back_kernel, far=False, **settings),
+    rim_back, *mr = lax.optimization_barrier((rim_back, *mr))
+    pair_shapes = [((tokens, width), BF16)] * 2
+    ext_back = [((2 * tokens + 8, width), F32)]
+    back_far = call(
+        functools.partial(conv_back_kernel, far=True, **settings),
         table,
         [du, rim_back] + [conv_weight] * 3,
         [None] * 2 + column_specs(taps),
         pair_shapes,
         ext_back,
-        name="conv_back_near",
-    )
-    br = [back_near[0], swapped(back_near[1], 1)] + br_far
+        name="conv_back_far",
+    )
+    br_far = [swapped(back_far[k - 2], k) for k in (2, 3)]
+    (mixer_out,) = call(
+        join_kernel, table, mr, [None] * groups, [((tokens, inner), BF16)], name="join_out",
+        vmem=False,
+    )
     step = groups
     received = []
     while step < devices:
@@ -950,6 +927,19 @@
         [((8, width + 256 + 2 * tokens), F32)] * groups,
         name="join_small",
     )
+    du, br_far[0], mixer_out, *small = lax.optimization_barrier(
+        (du, br_far[0], mixer_out, *small)
+    )
+    back_near = call(
+        functools.partial(conv_back_kernel, far=False, **settings),
+        table,
+        [du, rim_back] + [conv_weight] * 3,
+        [None] * 2 + column_specs(taps),
+        pair_shapes,
+        ext_back,
+        name="conv_back_near",
+    )
+    br = [back_near[0], swapped(back_near[1], 1)] + br_far
     pr = [small[0]] + [swapped(small[k], k) for k in range(1, groups)]
     grad_conv, grad_heads = call(
         functools.partial(join_params_kernel, scale=(tokens * devices) ** (-0.5), **shapes),

time: 116 us -> 108 us (0.931)
  waiting for transfers between devices: 23 us -> 15.3 us
    ppermute x18, waiting for transfers between devices: 18 us -> 10.9 us  [swapped(): return lax.ppermute(value, 'ctx', [(i, i ^ bits) for i in range(count)])]
  transfers between devices with their start and end apart: 27 -> 27, of which waited for: 9 -> 7; matrix products, arithmetic and copies ran while one was open for 0% -> 0% of each run, Pallas kernels for 38% -> 40%
where the time goes in v3:
time: 108 us; the launch traced here: 107 us
  Pallas kernels  47.3 us (44%)
  starting transfers between devices  37.7 us (35%)
  waiting for transfers between devices  15.3 us (14%)
  local copies, waits for them, and re-layouts  5.27 us (5%)
    pallas_call x18, Pallas kernels, call(): pl.pallas_call(kernel, out_shape=[pltpu.VMEM(shape, kind) if vmem else ja...  47.3 us
    ppermute x18, starting transfers between devices, swapped(): return lax.ppermute(value, 'ctx', [(i, i ^ bits) for i in range(count)])  22.9 us
    ppermute x5, starting transfers between devices, shifted(): return lax.ppermute(value, 'ctx', pairs)  12.2 us
    ppermute x18, waiting for transfers between devices, swapped(): return lax.ppermute(value, 'ctx', [(i, i ^ bits) for i in range(count)])  10.9 us
    unnamed x16, local copies, waits for them, and re-layouts  5.27 us
    ppermute x5, waiting for transfers between devices, shifted(): return lax.ppermute(value, 'ctx', pairs)  4.36 us
    ppermute x4, starting transfers between devices, body(): rims.append(lax.ppermute(edges[k], 'ctx', pairs))  2.64 us
  transfers between devices with their start and end apart: 27, of which 7 were waited for; matrix products, arithmetic and copies ran while one was open for 0% of the time, Pallas kernels for 40%

profile of v3, /device:TPU:0, one launch (start us, length us, event | category | flops | bytes accessed | tf_op | source)
XLA Modules:
  0.0 107.4 jit_solution(15406341588321605204)
XLA Ops:
  1.4 1.3 %copy-done.1 = bf16[128,5120]{1,0:T(8,128)(2,1)S(1)} copy-done((bf16[128,5120]{1,0:T(8,128)(2,1)S(1)}, bf16[128,5120]{1,0:T(8,128)(2,1)}, u32[]{:S(2)}) %copy-start.1) | copy-done | bytes 1310744
  4.7 2.6 %collective-permute-start.4 = (bf16[128,1408]{1,0:T(8,128)(2,1)S(1)}, bf16[128,1408]{1,0:T(8,128)(2,1)S(1)}, u32[]{:S(2)}, u32[]{:S(2)}) collective-permute-start(bf16[128,1408]{1,0:T(8,128)(2,1)S(1)} %get-tuple-element.122), channel_id=1, source_target_pairs={{0,2},{1,3},{2,0},{3,1},{4,6},{5,7},{6,4},{7,5},{8,10},{9,11},{10,... | collective-permute-start | bytes 1081352 | tf_op jit(solution)/shard_map/ppermute | solution.py:681
  10.1 1.2 %copy-done.2 = bf16[128,4096]{1,0:T(8,128)(2,1)S(1)} copy-done((bf16[128,4096]{1,0:T(8,128)(2,1)S(1)}, bf16[128,4096]{1,0:T(8,128)(2,1)}, u32[]{:S(2)}) %copy-start.2) | copy-done | bytes 1048600
  13.9 2.5 %conv.1 = (f32[4,128,1280]{2,1,0:T(8,128)S(1)}, f32[4,128,1280]{2,1,0:T(8,128)S(1)}, bf16[528,1280]{1,0:T(8,128)(2,1)S(1)}) custom-call(s32[6]{0:T(128)S(1)} %pad_add_fusion.s, bf16[128,1408]{1,0:T(8,128)(2,1)S(1)} %get-tuple-element.111.x0, bf16[128,1408]{1,0:T(8,128)(2,1)S(1)} %collective-permute-done.x1, f32[4,5120]{1,0:T(4,128)S(1)} %copy-done, ...), custom_call_target="tpu_custom_call" | custom-call | flops 1 | bytes 1 | tf_op jit(solution)/shard_map/conv/pallas_call | solution.py:659
  16.4 6.9 %collective-permute-start.1 = (bf16[128,1024]{1,0:T(8,128)(2,1)S(1)}, bf16[128,1024]{1,0:T(8,128)(2,1)S(1)}, u32[]{:S(2)}, u32[]{:S(2)}) collective-permute-start(bf16[128,1024]{1,0:T(8,128)(2,1)S(1)} %get-tuple-element.119), channel_id=1, source_target_pairs={{0,1},{1,0},{2,3},{3,2},{4,5},{5,4},{6,7},{7,6},{8,9},{9,8},{10,11... | collective-permute-start | bytes 786440 | tf_op jit(solution)/shard_map/ppermute | solution.py:681
  23.6 2.1 %collective-permute-start.3 = (bf16[128,1024]{1,0:T(8,128)(2,1)S(1)}, bf16[128,1024]{1,0:T(8,128)(2,1)S(1)}, u32[]{:S(2)}, u32[]{:S(2)}) collective-permute-start(bf16[128,1024]{1,0:T(8,128)(2,1)S(1)} %get-tuple-element.121), channel_id=1, source_target_pairs={{0,3},{1,2},{2,1},{3,0},{4,7},{5,6},{6,5},{7,4},{8,11},{9,10},{10,... | collective-permute-start | bytes 786440 | tf_op jit(solution)/shard_map/ppermute | solution.py:681
  25.7 4.6 %conv_state.1 = (f32[4,128,1280]{2,1,0:T(8,128)S(1)}, f32[4,128,1280]{2,1,0:T(8,128)S(1)}, bf16[528,1280]{1,0:T(8,128)(2,1)S(1)}, f32[136,1024]{1,0:T(8,128)S(1)...) custom-call(s32[6]{0:T(128)S(1)} %pad_add_fusion.s, ...), custom_call_target="tpu_custom_call", output_to_operand_aliasing={{0}: (16, {}), {1}: (17, {}), {2}: (18, {})} | custom-call | flops 1 | bytes 1 | tf_op jit(solution)/shard_map/conv_state/pallas_call | solution.py:659
  30.3 3.5 %collective-permute-start.11 = (f32[136,1024]{1,0:T(8,128)S(1)}, f32[136,1024]{1,0:T(8,128)S(1)}, u32[]{:S(2)}, u32[]{:S(2)}) collective-permute-start(f32[136,1024]{1,0:T(8,128)S(1)} %get-tuple-element.134.pay_in.pay), channel_id=1, source_target_pairs={{0,4},{1,5},{2,6},{3,7},{4,8},{5,9},{6,10},{7,11},{8,12},{9,13},{1... | collective-permute-start | bytes 1671176 | tf_op jit(solution)/shard_map/ppermute | solution.py:687
  33.8 4.3 %collective-permute-done.3.g3 = bf16[128,1024]{1,0:T(8,128)(2,1)S(1)} collective-permute-done((bf16[128,1024]{1,0:T(8,128)(2,1)S(1)}, bf16[128,1024]{1,0:T(8,128)(2,1)S(1)}, u32[]{:S(2)}, u32[]{:S(2)}) %collective-permute-start.3) | collective-permute-done | bytes 262176 | tf_op jit(solution)/shard_map/ppermute | solution.py:681
  38.1 2.4 %grad_state.1 = (bf16[4,128,1024]{2,1,0:T(8,128)(2,1)S(1)}, f32[136,1024]{1,0:T(8,128)S(1)}, f32[4,128,1024]{2,1,0:T(8,128)S(1)}) custom-call(s32[6]{0:T(128)S(1)} %pad_add_fusion.s, bf16[128,1024]{1,0:T(8,128)(2,1)S(1)} %get-tuple-element.118.g0, bf16[128,1024]{1,0:T(8,128)(2,1)S(1)} %collective-permute-done.1.g1, ...), custom_call_target="tpu_custom_call" | custom-call | flops 1 | bytes 1 | tf_op jit(solution)/shard_map/grad_state/pallas_call | solution.py:659
  40.5 1.3 %collective-permute-start.10 = (f32[136,1024]{1,0:T(8,128)S(1)}, f32[136,1024]{1,0:T(8,128)S(1)}, u32[]{:S(2)}, u32[]{:S(2)}) collective-permute-start(f32[136,1024]{1,0:T(8,128)S(1)} %get-tuple-element.135), channel_id=1, source_target_pairs={{4,0},{5,1},{6,2},{7,3},{8,4},{9,5},{10,6},{11,7},{12,8},{13,9},{1... | collective-permute-start | bytes 1671176 | tf_op jit(solution)/shard_map/ppermute | solution.py:687
  41.8 3.9 %local.3 = (f32[4,128,1024]{2,1,0:T(8,128)S(1)}, f32[4,128,1024]{2,1,0:T(8,128)S(1)}, f32[4,128,128]{2,1,0:T(8,128)S(1)}, f32[4,128,128]{2,1,0:T(8,128)S(1)}, f3...) custom-call(s32[6]{0:T(128)S(1)} %pad_add_fusion.s, f32[4,128,1280]{2,1,0:T(8,128)S(1)} %get-tuple-element.132.act_ref, ...), custom_call_target="tpu_custom_call" | custom-call | flops 1 | bytes 1 | tf_op jit(solution)/shard_map/local/pallas_call | solution.py:659
  46.6 4.6 %collective-permute-start.13 = (f32[136,1024]{1,0:T(8,128)S(1)}, f32[136,1024]{1,0:T(8,128)S(1)}, u32[]{:S(2)}, u32[]{:S(2)}) collective-permute-start(f32[136,1024]{1,0:T(8,128)S(1)} %collective-permute-done.11.one), channel_id=1, source_target_pairs={{0,4},{1,5},{2,6},{3,7},{4,8},{5,9},{6,10},{7,11},{8,12},{9,13},{1... | collective-permute-start | bytes 1671176 | tf_op jit(solution)/shard_map/ppermute | solution.py:687
  51.2 3.9 %local.4 = (f32[4,128,1024]{2,1,0:T(8,128)S(1)}, f32[4,128,1024]{2,1,0:T(8,128)S(1)}, f32[4,128,128]{2,1,0:T(8,128)S(1)}, f32[4,128,128]{2,1,0:T(8,128)S(1)}, f3...) custom-call(s32[6]{0:T(128)S(1)} %pad_add_fusion.s, ...), custom_call_target="tpu_custom_call", output_to_operand_aliasing={{0}: (6, {}), {1}: (7, {}), {2}: (8, {}), {3}: (9, {}), {4}... | custom-call | flops 1 | bytes 1 | tf_op jit(solution)/shard_map/local/pallas_call | solution.py:659
  55.2 1.8 %collective-permute-done.10.one = f32[136,1024]{1,0:T(8,128)S(1)} collective-permute-done((f32[136,1024]{1,0:T(8,128)S(1)}, f32[136,1024]{1,0:T(8,128)S(1)}, u32[]{:S(2)}, u32[]{:S(2)}) %collective-permute-start.10) | collective-permute-done | bytes 557088 | tf_op jit(solution)/shard_map/ppermute | solution.py:687
  57.0 1.3 %collective-permute-start.12 = (f32[136,1024]{1,0:T(8,128)S(1)}, f32[136,1024]{1,0:T(8,128)S(1)}, u32[]{:S(2)}, u32[]{:S(2)}) collective-permute-start(f32[136,1024]{1,0:T(8,128)S(1)} %collective-permute-done.10.one), channel_id=1, source_target_pairs={{4,0},{5,1},{6,2},{7,3},{8,4},{9,5},{10,6},{11,7},{12,8},{13,9},{1... | collective-permute-start | bytes 1671176 | tf_op jit(solution)/shard_map/ppermute | solution.py:687
  58.3 7.4 %local.5 = (f32[4,128,1024]{2,1,0:T(8,128)S(1)}, f32[4,128,1024]{2,1,0:T(8,128)S(1)}, f32[4,128,128]{2,1,0:T(8,128)S(1)}, f32[4,128,128]{2,1,0:T(8,128)S(1)}, f3...) custom-call(s32[6]{0:T(128)S(1)} %pad_add_fusion.s, ...), custom_call_target="tpu_custom_call", output_to_operand_aliasing={{0}: (6, {}), {1}: (7, {}), {2}: (8, {}), {3}: (9, {}), {4}... | custom-call | flops 1 | bytes 1 | tf_op jit(solution)/shard_map/local/pallas_call | solution.py:659
  65.7 3.8 %out.1 = (bf16[128,1024]{1,0:T(8,128)(2,1)S(1)}, bf16[128,1024]{1,0:T(8,128)(2,1)S(1)}, bf16[128,1024]{1,0:T(8,128)(2,1)S(1)}, bf16[128,1024]{1,0:T(8,128)(2,1)S...) custom-call(s32[6]{0:T(128)S(1)} %pad_add_fusion.s, ...), custom_call_target="tpu_custom_call" | custom-call | flops 1 | bytes 1 | tf_op jit(solution)/shard_map/out/pallas_call | solution.py:659
  69.6 1.8 %collective-permute-start.17 = (bf16[128,1024]{1,0:T(8,128)(2,1)S(1)}, bf16[128,1024]{1,0:T(8,128)(2,1)S(1)}, u32[]{:S(2)}, u32[]{:S(2)}) collective-permute-start(bf16[128,1024]{1,0:T(8,128)(2,1)S(1)} %get-tuple-element.187), channel_id=1, source_target_pairs={{0,3},{1,2},{2,1},{3,0},{4,7},{5,6},{6,5},{7,4},{8,11},{9,10},{10,... | collective-permute-start | bytes 786440 | tf_op jit(solution)/shard_map/ppermute | solution.py:681
  71.4 1.6 %collective-permute-done.12.two = f32[136,1024]{1,0:T(8,128)S(1)} collective-permute-done((f32[136,1024]{1,0:T(8,128)S(1)}, f32[136,1024]{1,0:T(8,128)S(1)}, u32[]{:S(2)}, u32[]{:S(2)}) %collective-permute-start.12) | collective-permute-done | bytes 557088 | tf_op jit(solution)/shard_map/ppermute | solution.py:687
  74.2 1.5 %collective-permute-start.14 = (f32[8,1280]{1,0:T(8,128)S(1)}, f32[8,1280]{1,0:T(8,128)S(1)}, u32[]{:S(2)}, u32[]{:S(2)}) collective-permute-start(f32[8,1280]{1,0:T(8,128)S(1)} %get-tuple-element.183), channel_id=1, source_target_pairs={{4,0},{5,1},{6,2},{7,3},{8,4},{9,5},{10,6},{11,7},{12,8},{13,9},{1... | collective-permute-start | bytes 122888 | tf_op jit(solution)/shard_map/ppermute | solution.py:687
  75.8 3.6 %back_far.1 = (f32[512,1280]{1,0:T(8,128)S(1)}, f32[8,1536]{1,0:T(8,128)S(1)}, f32[3,16,128]{2,1,0:T(8,128)S(1)}) custom-call(s32[6]{0:T(128)S(1)} %pad_add_fusion.s, bf16[128,1024]{1,0:T(8,128)(2,1)S(1)} %get-tuple-element.171.high_ref, bf16[128,1024]{1,0:T(8,128)(2,1)S(1)} %get-tuple-element.172.low_ref, f32[4,128,1280]{2,1,0:T(8,128)S(1)} %get-tuple-element.132.act_ref, ...), custom_call_target="tpu_custom_call" | custom-call | flops 1 | bytes 1 | tf_op jit(solution)/shard_map/back_far/pallas_call | solution.py:659
  79.4 4.5 %back_near.1 = (f32[512,1280]{1,0:T(8,128)S(1)}, f32[8,1536]{1,0:T(8,128)S(1)}, f32[16,128]{1,0:T(8,128)S(1)}, f32[16,128]{1,0:T(8,128)S(1)}, f32[16,128]{1,0:T(8,128)S(1)}, /*index=5*/f32[16,128]{1,0:T(8,128)S(1)}) custom-call(s32[6]{0:T(128)S(1)} %pad_add_fusion.s, ...), custom_call_target="tpu_custom_call", output_to_operand_aliasing={{0}: (20, {})} | custom-call | flops 1 | bytes 1 | tf_op jit(solution)/shard_map/back_near/pallas_call | solution.py:659
  83.9 1.6 %conv_back_far.1 = (bf16[128,1280]{1,0:T(8,128)(2,1)S(1)}, bf16[128,1280]{1,0:T(8,128)(2,1)S(1)}) custom-call(s32[6]{0:T(128)S(1)} %pad_add_fusion.s, f32[512,1280]{1,0:T(8,128)S(1)} %get-tuple-element.204.du_ref, f32[8,1280]{1,0:T(8,128)S(1)} %collective-permute-done.14.rim_ref, f32[4,5120]{1,0:T(4,128)S(1)} %copy-done, f32[4,5120]{1,0:T(4,128)S(1)} %copy-done, ...), custom_call_target="tpu_custom_call" | custom-call | flops 1 | bytes 1 | tf_op jit(solution)/shard_map/conv_back_far/pallas_call | solution.py:659
  85.6 4.9 %collective-permute-start.21 = (f32[8,1536]{1,0:T(8,128)S(1)}, f32[8,1536]{1,0:T(8,128)S(1)}, u32[]{:S(2)}, u32[]{:S(2)}) collective-permute-start(f32[8,1536]{1,0:T(8,128)S(1)} %get-tuple-element.194.first), channel_id=1, source_target_pairs={{0,12},{1,13},{2,14},{3,15},{4,8},{5,9},{6,10},{7,11},{8,4},{9,5},... | collective-permute-start | bytes 147464 | tf_op jit(solution)/shard_map/ppermute | solution.py:681
  91.5 1.6 %join_out.1 = bf16[128,4096]{1,0:T(8,128)(2,1)} custom-call(s32[6]{0:T(128)S(1)} %pad_add_fusion.s, bf16[128,1024]{1,0:T(8,128)(2,1)S(1)} %get-tuple-element.190.p0, bf16[128,1024]{1,0:T(8,128)(2,1)S(1)} %collective-permute-done.15.p1, bf16[128,1024]{1,0:T(8,128)(2,1)S(1)} %collective-permute-done.16.p2, bf16[128,1024]{1,0:T(8,128)(2,1)S(1)} %collective-permute-done.17.p3), custom_call_target="tpu_custom_call" | custom-call | flops 1 | bytes 1 | tf_op jit(solution)/shard_map/join_out/pallas_call | solution.py:659
  93.1 2.4 %collective-permute-done.20.refs_1_ = f32[8,1536]{1,0:T(8,128)S(1)} collective-permute-done((f32[8,1536]{1,0:T(8,128)S(1)}, f32[8,1536]{1,0:T(8,128)S(1)}, u32[]{:S(2)}, u32[]{:S(2)}) %collective-permute-start.20) | collective-permute-done | bytes 49184 | tf_op jit(solution)/shard_map/ppermute | solution.py:681
  96.0 1.6 %conv_back_near.1 = (bf16[128,1280]{1,0:T(8,128)(2,1)S(1)}, bf16[128,1280]{1,0:T(8,128)(2,1)S(1)}) custom-call(s32[6]{0:T(128)S(1)} %pad_add_fusion.s, f32[512,1280]{1,0:T(8,128)S(1)} %get-tuple-element.204.du_ref, f32[8,1280]{1,0:T(8,128)S(1)} %collective-permute-done.14.rim_ref, f32[4,5120]{1,0:T(4,128)S(1)} %copy-done, f32[4,5120]{1,0:T(4,128)S(1)} %copy-done, ...), custom_call_target="tpu_custom_call" | custom-call | flops 1 | bytes 1 | tf_op jit(solution)/shard_map/conv_back_near/pallas_call | solution.py:659
  98.2 1.9 %collective-permute-start.25 = (f32[8,1792]{1,0:T(8,128)S(1)}, f32[8,1792]{1,0:T(8,128)S(1)}, u32[]{:S(2)}, u32[]{:S(2)}) collective-permute-start(f32[8,1792]{1,0:T(8,128)S(1)} %get-tuple-element.211), channel_id=1, source_target_pairs={{0,2},{1,3},{2,0},{3,1},{4,6},{5,7},{6,4},{7,5},{8,10},{9,11},{10,... | collective-permute-start | bytes 172040 | tf_op jit(solution)/shard_map/ppermute | solution.py:681
  100.1 3.1 %collective-permute-done.25.g2.p2 = f32[8,1792]{1,0:T(8,128)S(1)} collective-permute-done((f32[8,1792]{1,0:T(8,128)S(1)}, f32[8,1792]{1,0:T(8,128)S(1)}, u32[]{:S(2)}, u32[]{:S(2)}) %collective-permute-start.25) | collective-permute-done | bytes 57376 | tf_op jit(solution)/shard_map/ppermute | solution.py:681
  104.4 1.2 %join_params.1 = (f32[5,5120]{1,0:T(8,128)}, f32[3,64]{1,0:T(4,128)}) custom-call(s32[6]{0:T(128)S(1)} %pad_add_fusion.s, f32[8,1792]{1,0:T(8,128)S(1)} %get-tuple-element.209.g0.p0, f32[8,1792]{1,0:T(8,128)S(1)} %collective-permute-done.24.g1.p1, f32[8,1792]{1,0:T(8,128)S(1)} %collective-permute-done.25.g2.p2, f32[8,1792]{1,0:T(8,128)S(1)} %collective-permute-done.26.g3.p3), custom_call_target="tpu_custom_call" | custom-call | flops 1 | bytes 1 | tf_op jit(solution)/shard_map/join_params/pallas_call | solution.py:659
  105.6 1.7 %join_grad.1 = (bf16[128,5120]{1,0:T(8,128)(2,1)}, f32[64,128]{1,0:T(8,128)}) custom-call(s32[6]{0:T(128)S(1)} %pad_add_fusion.s, bf16[128,1280]{1,0:T(8,128)(2,1)S(1)} %get-tuple-element.205.p0, bf16[128,1280]{1,0:T(8,128)(2,1)S(1)} %collective-permute-done.22.p1, bf16[128,1280]{1,0:T(8,128)(2,1)S(1)} %collective-permute-done.18.p2, ...), custom_call_target="tpu_custom_call" | custom-call | flops 1 | bytes 1 | tf_op jit(solution)/shard_map/join_grad/pallas_call | solution.py:659
  (57 shorter events, 14.0 us)
Async XLA Ops:
  0.6 13.3 %copy-start = (f32[4,5120]{1,0:T(4,128)S(1)}, f32[4,5120]{1,0:T(4,128)}, u32[]{:S(2)}) copy-start(f32[4,5120]{1,0:T(4,128)} %wc.7) | copy-start | bytes 245764
  1.4 1.3 %copy-start.1 = (bf16[128,5120]{1,0:T(8,128)(2,1)S(1)}, bf16[128,5120]{1,0:T(8,128)(2,1)}, u32[]{:S(2)}) copy-start(bf16[128,5120]{1,0:T(8,128)(2,1)} %x_ref.1) | copy-start | bytes 3932164
  2.7 0.8 copy-start.4
  3.5 10.4 %copy-start.3 = (f32[5120]{0:T(1024)S(1)}, f32[5120]{0:T(1024)}, u32[]{:S(2)}) copy-start(f32[5120]{0:T(1024)} %param.15) | copy-start | bytes 61444
  4.2 5.2 %collective-permute-start = (bf16[128,1408]{1,0:T(8,128)(2,1)S(1)}, bf16[128,1408]{1,0:T(8,128)(2,1)S(1)}, u32[]{:S(2)}, u32[]{:S(2)}) collective-permute-start(bf16[128,1408]{1,0:T(8,128)(2,1)S(1)} %get-tuple-element.112), channel_id=1, source_target_pairs={{0,1},{1,0},{2,3},{3,2},{4,5},{5,4},{6,7},{7,6},{8,9},{9,8},{10,11... | collective-permute-start | bytes 1081352 | tf_op jit(solution)/shard_map/ppermute | solution.py:681
  4.7 21.0 %collective-permute-start.4 = (bf16[128,1408]{1,0:T(8,128)(2,1)S(1)}, bf16[128,1408]{1,0:T(8,128)(2,1)S(1)}, u32[]{:S(2)}, u32[]{:S(2)}) collective-permute-start(bf16[128,1408]{1,0:T(8,128)(2,1)S(1)} %get-tuple-element.122), channel_id=1, source_target_pairs={{0,2},{1,3},{2,0},{3,1},{4,6},{5,7},{6,4},{7,5},{8,10},{9,11},{10,... | collective-permute-start | bytes 1081352 | tf_op jit(solution)/shard_map/ppermute | solution.py:681
  7.3 18.4 %collective-permute-start.5 = (bf16[128,1408]{1,0:T(8,128)(2,1)S(1)}, bf16[128,1408]{1,0:T(8,128)(2,1)S(1)}, u32[]{:S(2)}, u32[]{:S(2)}) collective-permute-start(bf16[128,1408]{1,0:T(8,128)(2,1)S(1)} %get-tuple-element.123), channel_id=1, source_target_pairs={{0,3},{1,2},{2,1},{3,0},{4,7},{5,6},{6,5},{7,4},{8,11},{9,10},{10,... | collective-permute-start | bytes 1081352 | tf_op jit(solution)/shard_map/ppermute | solution.py:681
  7.4 1.3 %collective-permute-start.6 = (bf16[16,1280]{1,0:T(8,128)(2,1)S(1)}, bf16[16,1280]{1,0:T(8,128)(2,1)S(1)}, u32[]{:S(2)}, u32[]{:S(2)}) collective-permute-start(bf16[16,1280]{1,0:T(8,128)(2,1)S(1)} %get-tuple-element.124), channel_id=1, source_target_pairs={{3,7},{7,11},{11,15},{19,23},{23,27},{27,31}} | collective-permute-start | bytes 122888 | tf_op jit(solution)/shard_map/ppermute | solution.py:769
  8.0 8.4 %collective-permute-start.7 = (bf16[16,1280]{1,0:T(8,128)(2,1)S(1)}, bf16[16,1280]{1,0:T(8,128)(2,1)S(1)}, u32[]{:S(2)}, u32[]{:S(2)}) collective-permute-start(bf16[16,1280]{1,0:T(8,128)(2,1)S(1)} %get-tuple-element.125), channel_id=1, source_target_pairs={{3,6},{7,10},{11,14},{19,22},{23,26},{27,30}} | collective-permute-start | bytes 122888 | tf_op jit(solution)/shard_map/ppermute | solution.py:769
  8.7 14.6 %collective-permute-start.8 = (bf16[16,1280]{1,0:T(8,128)(2,1)S(1)}, bf16[16,1280]{1,0:T(8,128)(2,1)S(1)}, u32[]{:S(2)}, u32[]{:S(2)}) collective-permute-start(bf16[16,1280]{1,0:T(8,128)(2,1)S(1)} %get-tuple-element.126), channel_id=1, source_target_pairs={{1,3},{3,5},{5,7},{7,9},{9,11},{11,13},{13,15},{17,19},{19,21},{21... | collective-permute-start | bytes 122888 | tf_op jit(solution)/shard_map/ppermute | solution.py:769
  9.4 14.2 %collective-permute-start.9 = (bf16[16,1280]{1,0:T(8,128)(2,1)S(1)}, bf16[16,1280]{1,0:T(8,128)(2,1)S(1)}, u32[]{:S(2)}, u32[]{:S(2)}) collective-permute-start(bf16[16,1280]{1,0:T(8,128)(2,1)S(1)} %get-tuple-element.127), channel_id=1, source_target_pairs={{1,2},{3,4},{5,6},{7,8},{9,10},{11,12},{13,14},{17,18},{19,20},{21... | collective-permute-start | bytes 122888 | tf_op jit(solution)/shard_map/ppermute | solution.py:769
  10.1 1.2 %copy-start.2 = (bf16[128,4096]{1,0:T(8,128)(2,1)S(1)}, bf16[128,4096]{1,0:T(8,128)(2,1)}, u32[]{:S(2)}) copy-start(bf16[128,4096]{1,0:T(8,128)(2,1)} %g_ref.1) | copy-start | bytes 3145732
  16.4 17.4 %collective-permute-start.1 = (bf16[128,1024]{1,0:T(8,128)(2,1)S(1)}, bf16[128,1024]{1,0:T(8,128)(2,1)S(1)}, u32[]{:S(2)}, u32[]{:S(2)}) collective-permute-start(bf16[128,1024]{1,0:T(8,128)(2,1)S(1)} %get-tuple-element.119), channel_id=1, source_target_pairs={{0,1},{1,0},{2,3},{3,2},{4,5},{5,4},{6,7},{7,6},{8,9},{9,8},{10,11... | collective-permute-start | bytes 786440 | tf_op jit(solution)/shard_map/ppermute | solution.py:681
  23.3 10.5 %collective-permute-start.2 = (bf16[128,1024]{1,0:T(8,128)(2,1)S(1)}, bf16[128,1024]{1,0:T(8,128)(2,1)S(1)}, u32[]{:S(2)}, u32[]{:S(2)}) collective-permute-start(bf16[128,1024]{1,0:T(8,128)(2,1)S(1)} %get-tuple-element.120), channel_id=1, source_target_pairs={{0,2},{1,3},{2,0},{3,1},{4,6},{5,7},{6,4},{7,5},{8,10},{9,11},{10,... | collective-permute-start | bytes 786440 | tf_op jit(solution)/shard_map/ppermute | solution.py:681
  23.6 14.5 %collective-permute-start.3 = (bf16[128,1024]{1,0:T(8,128)(2,1)S(1)}, bf16[128,1024]{1,0:T(8,128)(2,1)S(1)}, u32[]{:S(2)}, u32[]{:S(2)}) collective-permute-start(bf16[128,1024]{1,0:T(8,128)(2,1)S(1)} %get-tuple-element.121), channel_id=1, source_target_pairs={{0,3},{1,2},{2,1},{3,0},{4,7},{5,6},{6,5},{7,4},{8,11},{9,10},{10,... | collective-permute-start | bytes 786440 | tf_op jit(solution)/shard_map/ppermute | solution.py:681
  30.3 16.3 %collective-permute-start.11 = (f32[136,1024]{1,0:T(8,128)S(1)}, f32[136,1024]{1,0:T(8,128)S(1)}, u32[]{:S(2)}, u32[]{:S(2)}) collective-permute-start(f32[136,1024]{1,0:T(8,128)S(1)} %get-tuple-element.134.pay_in.pay), channel_id=1, source_target_pairs={{0,4},{1,5},{2,6},{3,7},{4,8},{5,9},{6,10},{7,11},{8,12},{9,13},{1... | collective-permute-start | bytes 1671176 | tf_op jit(solution)/shard_map/ppermute | solution.py:687
  40.5 16.5 %collective-permute-start.10 = (f32[136,1024]{1,0:T(8,128)S(1)}, f32[136,1024]{1,0:T(8,128)S(1)}, u32[]{:S(2)}, u32[]{:S(2)}) collective-permute-start(f32[136,1024]{1,0:T(8,128)S(1)} %get-tuple-element.135), channel_id=1, source_target_pairs={{4,0},{5,1},{6,2},{7,3},{8,4},{9,5},{10,6},{11,7},{12,8},{13,9},{1... | collective-permute-start | bytes 1671176 | tf_op jit(solution)/shard_map/ppermute | solution.py:687
  46.6 19.0 %collective-permute-start.13 = (f32[136,1024]{1,0:T(8,128)S(1)}, f32[136,1024]{1,0:T(8,128)S(1)}, u32[]{:S(2)}, u32[]{:S(2)}) collective-permute-start(f32[136,1024]{1,0:T(8,128)S(1)} %collective-permute-done.11.one), channel_id=1, source_target_pairs={{0,4},{1,5},{2,6},{3,7},{4,8},{5,9},{6,10},{7,11},{8,12},{9,13},{1... | collective-permute-start | bytes 1671176 | tf_op jit(solution)/shard_map/ppermute | solution.py:687
  57.0 16.1 %collective-permute-start.12 = (f32[136,1024]{1,0:T(8,128)S(1)}, f32[136,1024]{1,0:T(8,128)S(1)}, u32[]{:S(2)}, u32[]{:S(2)}) collective-permute-start(f32[136,1024]{1,0:T(8,128)S(1)} %collective-permute-done.10.one), channel_id=1, source_target_pairs={{4,0},{5,1},{6,2},{7,3},{8,4},{9,5},{10,6},{11,7},{12,8},{13,9},{1... | collective-permute-start | bytes 1671176 | tf_op jit(solution)/shard_map/ppermute | solution.py:687
  69.5 14.4 %collective-permute-start.15 = (bf16[128,1024]{1,0:T(8,128)(2,1)S(1)}, bf16[128,1024]{1,0:T(8,128)(2,1)S(1)}, u32[]{:S(2)}, u32[]{:S(2)}) collective-permute-start(bf16[128,1024]{1,0:T(8,128)(2,1)S(1)} %get-tuple-element.185), channel_id=1, source_target_pairs={{0,1},{1,0},{2,3},{3,2},{4,5},{5,4},{6,7},{7,6},{8,9},{9,8},{10,11... | collective-permute-start | bytes 786440 | tf_op jit(solution)/shard_map/ppermute | solution.py:681
  69.6 14.3 %collective-permute-start.16 = (bf16[128,1024]{1,0:T(8,128)(2,1)S(1)}, bf16[128,1024]{1,0:T(8,128)(2,1)S(1)}, u32[]{:S(2)}, u32[]{:S(2)}) collective-permute-start(bf16[128,1024]{1,0:T(8,128)(2,1)S(1)} %get-tuple-element.186), channel_id=1, source_target_pairs={{0,2},{1,3},{2,0},{3,1},{4,6},{5,7},{6,4},{7,5},{8,10},{9,11},{10,... | collective-permute-start | bytes 786440 | tf_op jit(solution)/shard_map/ppermute | solution.py:681
  69.6 14.2 %collective-permute-start.17 = (bf16[128,1024]{1,0:T(8,128)(2,1)S(1)}, bf16[128,1024]{1,0:T(8,128)(2,1)S(1)}, u32[]{:S(2)}, u32[]{:S(2)}) collective-permute-start(bf16[128,1024]{1,0:T(8,128)(2,1)S(1)} %get-tuple-element.187), channel_id=1, source_target_pairs={{0,3},{1,2},{2,1},{3,0},{4,7},{5,6},{6,5},{7,4},{8,11},{9,10},{10,... | collective-permute-start | bytes 786440 | tf_op jit(solution)/shard_map/ppermute | solution.py:681
  74.2 9.7 %collective-permute-start.14 = (f32[8,1280]{1,0:T(8,128)S(1)}, f32[8,1280]{1,0:T(8,128)S(1)}, u32[]{:S(2)}, u32[]{:S(2)}) collective-permute-start(f32[8,1280]{1,0:T(8,128)S(1)} %get-tuple-element.183), channel_id=1, source_target_pairs={{4,0},{5,1},{6,2},{7,3},{8,4},{9,5},{10,6},{11,7},{12,8},{13,9},{1... | collective-permute-start | bytes 122888 | tf_op jit(solution)/shard_map/ppermute | solution.py:687
  85.5 10.5 %collective-permute-start.18 = (bf16[128,1280]{1,0:T(8,128)(2,1)S(1)}, bf16[128,1280]{1,0:T(8,128)(2,1)S(1)}, u32[]{:S(2)}, u32[]{:S(2)}) collective-permute-start(bf16[128,1280]{1,0:T(8,128)(2,1)S(1)} %get-tuple-element.189), channel_id=1, source_target_pairs={{0,2},{1,3},{2,0},{3,1},{4,6},{5,7},{6,4},{7,5},{8,10},{9,11},{10,... | collective-permute-start | bytes 983048 | tf_op jit(solution)/shard_map/ppermute | solution.py:681
  85.6 7.5 %collective-permute-start.21 = (f32[8,1536]{1,0:T(8,128)S(1)}, f32[8,1536]{1,0:T(8,128)S(1)}, u32[]{:S(2)}, u32[]{:S(2)}) collective-permute-start(f32[8,1536]{1,0:T(8,128)S(1)} %get-tuple-element.194.first), channel_id=1, source_target_pairs={{0,12},{1,13},{2,14},{3,15},{4,8},{5,9},{6,10},{7,11},{8,4},{9,5},... | collective-permute-start | bytes 147464 | tf_op jit(solution)/shard_map/ppermute | solution.py:681
  90.4 5.0 %collective-permute-start.20 = (f32[8,1536]{1,0:T(8,128)S(1)}, f32[8,1536]{1,0:T(8,128)S(1)}, u32[]{:S(2)}, u32[]{:S(2)}) collective-permute-start(f32[8,1536]{1,0:T(8,128)S(1)} %get-tuple-element.194.first), channel_id=1, source_target_pairs={{0,8},{1,9},{2,10},{3,11},{4,12},{5,13},{6,14},{7,15},{8,0},{9,1},... | collective-permute-start | bytes 147464 | tf_op jit(solution)/shard_map/ppermute | solution.py:681
  90.4 5.0 %collective-permute-start.19 = (f32[8,1536]{1,0:T(8,128)S(1)}, f32[8,1536]{1,0:T(8,128)S(1)}, u32[]{:S(2)}, u32[]{:S(2)}) collective-permute-start(f32[8,1536]{1,0:T(8,128)S(1)} %get-tuple-element.194.first), channel_id=1, source_target_pairs={{0,4},{1,5},{2,6},{3,7},{4,0},{5,1},{6,2},{7,3},{8,12},{9,13},{10,... | collective-permute-start | bytes 147464 | tf_op jit(solution)/shard_map/ppermute | solution.py:681
  91.1 14.6 %collective-permute-start.23 = (bf16[128,1280]{1,0:T(8,128)(2,1)S(1)}, bf16[128,1280]{1,0:T(8,128)(2,1)S(1)}, u32[]{:S(2)}, u32[]{:S(2)}) collective-permute-start(bf16[128,1280]{1,0:T(8,128)(2,1)S(1)} %get-tuple-element.208), channel_id=1, source_target_pairs={{0,3},{1,2},{2,1},{3,0},{4,7},{5,6},{6,5},{7,4},{8,11},{9,10},{10,... | collective-permute-start | bytes 983048 | tf_op jit(solution)/shard_map/ppermute | solution.py:681
  97.6 8.0 %collective-permute-start.22 = (bf16[128,1280]{1,0:T(8,128)(2,1)S(1)}, bf16[128,1280]{1,0:T(8,128)(2,1)S(1)}, u32[]{:S(2)}, u32[]{:S(2)}) collective-permute-start(bf16[128,1280]{1,0:T(8,128)(2,1)S(1)} %get-tuple-element.206), channel_id=1, source_target_pairs={{0,1},{1,0},{2,3},{3,2},{4,5},{5,4},{6,7},{7,6},{8,9},{9,8},{10,11... | collective-permute-start | bytes 983048 | tf_op jit(solution)/shard_map/ppermute | solution.py:681
  97.7 2.5 %collective-permute-start.24 = (f32[8,1792]{1,0:T(8,128)S(1)}, f32[8,1792]{1,0:T(8,128)S(1)}, u32[]{:S(2)}, u32[]{:S(2)}) collective-permute-start(f32[8,1792]{1,0:T(8,128)S(1)} %get-tuple-element.210), channel_id=1, source_target_pairs={{0,1},{1,0},{2,3},{3,2},{4,5},{5,4},{6,7},{7,6},{8,9},{9,8},{10,11... | collective-permute-start | bytes 172040 | tf_op jit(solution)/shard_map/ppermute | solution.py:681
  98.2 5.1 %collective-permute-start.25 = (f32[8,1792]{1,0:T(8,128)S(1)}, f32[8,1792]{1,0:T(8,128)S(1)}, u32[]{:S(2)}, u32[]{:S(2)}) collective-permute-start(f32[8,1792]{1,0:T(8,128)S(1)} %get-tuple-element.211), channel_id=1, source_target_pairs={{0,2},{1,3},{2,0},{3,1},{4,6},{5,7},{6,4},{7,5},{8,10},{9,11},{10,... | collective-permute-start | bytes 172040 | tf_op jit(solution)/shard_map/ppermute | solution.py:681
  100.1 4.3 %collective-permute-start.26 = (f32[8,1792]{1,0:T(8,128)S(1)}, f32[8,1792]{1,0:T(8,128)S(1)}, u32[]{:S(2)}, u32[]{:S(2)}) collective-permute-start(f32[8,1792]{1,0:T(8,128)S(1)} %get-tuple-element.212), channel_id=1, source_target_pairs={{0,3},{1,2},{2,1},{3,0},{4,7},{5,6},{6,5},{7,4},{8,11},{9,10},{10,... | collective-permute-start | bytes 172040 | tf_op jit(solution)/shard_map/ppermute | solution.py:681
  (3 other events, 2.0 us)

commit v4 on v3

--- a/solution.py
+++ b/solution.py
@@ -101,18 +101,21 @@
     for k in range(groups):
         q = me ^ k
         xs = outs[k]
-        xs[:, :part] = x_ref[:, pl.ds(pl.multiple_of(q * part, part), part)]
-        xs[:, part : part + state] = x_ref[
+        xs[:tokens, :part] = x_ref[:, pl.ds(pl.multiple_of(q * part, part), part)]
+        xs[:tokens, part : part + state] = x_ref[
             :, pl.ds(pl.multiple_of(inner + q * state, state), state)
         ]
-        xs[:, part + state : width] = x_ref[
+        xs[:tokens, part + state :] = x_ref[
             :, pl.ds(pl.multiple_of(inner + (groups + q) * state, state), state)
         ]
-        rims[k][...] = xs[tokens - 16 :, :width]
-        raw = step_ref[pl.ds(pl.multiple_of(q * share, share), share), :]
-        xs[:, width:] = jnp.zeros((tokens, tokens), BF16)
-        for i, piece in enumerate(thirds(raw)):
-            xs[i * share : (i + 1) * share, width:] = piece
+        rims[k][...] = xs[tokens - 16 : tokens, :]
+        xs[tokens:, :] = jnp.zeros((8, width), BF16)
+        place = 0
+        for row in range(0, share, 8):
+            raw = step_ref[pl.ds(pl.multiple_of(q * share + row, 8), 8), :]
+            for piece in thirds(raw):
+                xs[tokens:, place : place + tokens] = piece
+                place += tokens
 
 
 def pack_grad_kernel(s, g_ref, bias, decay, skip, *refs, groups):
@@ -171,12 +174,12 @@
     share, headdim, state = sizes
     part = share * headdim
     width = part + 2 * state
-    tokens = pieces[0].shape[0]
+    tokens = act_ref.shape[1]
     taps = wx.shape[0]
     ext[:8, :] = rim[8:]
     for k, ref in enumerate(pieces):
         place = (me & 1) ^ k
-        value = ref[:, :width]
+        value = ref[:tokens, :]
         ext[pl.ds(pl.multiple_of(8 + place * tokens, 8), tokens), :] = value.astype(F32)
         xall_ref[pl.ds(pl.multiple_of(16 + (first + place) * tokens, 16), tokens), :] = value
 
@@ -220,11 +223,17 @@
     plane = s[1]
     part = share * headdim
     width = part + 2 * state
-    tokens = x0.shape[0]
+    tokens = act_ref.shape[1]
     chunks = 4
     for k, ref in enumerate((x0, x1, x2, x3)):
-        block = ref[: 3 * share, width:].astype(F32)
-        raws[me ^ k] = block[:share] + block[share : 2 * share] + block[2 * share :]
+        block = ref[tokens:, :].astype(F32)
+        for i in range(share // 8):
+            lo = 3 * i * tokens
+            raws[me ^ k, 8 * i : 8 * i + 8] = (
+                block[:, lo : lo + tokens]
+                + block[:, lo + tokens : lo + 2 * tokens]
+                + block[:, lo + 2 * tokens : lo + 3 * tokens]
+            )
     upper_chip = (me & 2) == 2
     inner_rim = xall_ref[2 * tokens : 2 * tokens + 16, :].astype(F32)
     rim = jnp.where(upper_chip, r0[...].astype(F32) + r1[...].astype(F32), inner_rim)
@@ -305,64 +314,81 @@
     pay_ref[state:, :] = pay_in[state:, :]
 
 
+def within_chunk(s, c, g_ref, act_ref, vec_ref, y_ref, dx_ref, db_ref, dc_ref, wide, sizes, docs):
+    share, headdim, state = sizes
+    part = share * headdim
+    tokens = act_ref.shape[1]
+    lanes = lax.broadcasted_iota(jnp.int32, (tokens, 2 * headdim), 1)
+    left = lanes < headdim
+    base = s[1] + c * tokens
+    tpos = base + lax.broadcasted_iota(jnp.int32, (tokens, tokens), 0)
+    spos = base + lax.broadcasted_iota(jnp.int32, (tokens, tokens), 1)
+    tstart = doc_start(tpos, s, docs)
+    mask = jnp.where((spos <= tpos) & (spos >= tstart), 0.0, NEG)
+    b = act_ref[c, :, part : part + state]
+    cc = act_ref[c, :, part + state :]
+    m = dot3(cc, b, NT)
+    cum = vec_ref[c, CUM]
+    step = vec_ref[c, STEP]
+    wide[...] = spread(cum, spread_matrix(share, tokens))
+    dm = jnp.zeros((tokens, tokens), F32)
+    for pair in range(share // 2):
+        lo = pair * 2 * headdim
+        xp = act_ref[c, :, lo : lo + 2 * headdim]
+        gp = g_ref[:, lo : lo + 2 * headdim]
+        zero = jnp.zeros_like(gp)
+        gst = jnp.concatenate([jnp.where(left, gp, zero), jnp.where(left, zero, gp)], axis=0)
+        factors = []
+        for h in (2 * pair, 2 * pair + 1):
+            diff = wide[:, h * tokens : (h + 1) * tokens] - cum[h : h + 1, :]
+            factors.append(jnp.exp(diff + mask) * step[h : h + 1, :])
+        pieces = jnp.concatenate(halves(xp), axis=1)
+        dw = mm(jnp.concatenate([gst, gst], axis=1), pieces, NT)
+        dm = dm + dw[:tokens] * factors[0] + dw[tokens:] * factors[1]
+        w = jnp.concatenate([m * factors[0], m * factors[1]], axis=0)
+        w = jnp.concatenate(halves(w), axis=1)
+        yst = mm(w, jnp.concatenate([pieces, pieces], axis=0), NN)
+        yst = yst[:, : 2 * headdim] + yst[:, 2 * headdim :]
+        y_ref[c, :, lo : lo + 2 * headdim] = jnp.where(left, yst[:tokens], yst[tokens:])
+        dst = mm(w, gst, TN)
+        dx_ref[c, :, lo : lo + 2 * headdim] = dst[:tokens] + dst[tokens:]
+    dc_ref[c] = dot3(dm, b, NN)
+    db_ref[c] = dot3(dm, cc, TN)
+
+
+def within_kernel(
+    s, act_ref, vec_ref, g_ref, y_ref, dx_ref, db_ref, dc_ref, wide, *, sizes, docs
+):
+    within_chunk(
+        s, s[0], g_ref, act_ref, vec_ref, y_ref, dx_ref, db_ref, dc_ref, wide, sizes, docs
+    )
+
+
 def local_kernel(
-    s, act_ref, vec_ref, gall_ref, schain, gchain, *refs, span, share, headdim, state, docs,
-):
-    y_ref, dx_ref, db_ref, dc_ref, flow_ref, xd_ref, wide, yd, dxd = refs[-9:]
-    plane = s[1]
+    s, act_ref, vec_ref, gall_ref, schain, gchain, *refs, span, sizes, docs,
+):
+    y_ref, dx_ref, db_ref, dc_ref, flow_ref, xd_ref, wide = refs[-7:]
+    share, headdim, state = sizes
     part = share * headdim
     tokens = act_ref.shape[1]
     matrix = spread_matrix(share, headdim)
-    lanes = lax.broadcasted_iota(jnp.int32, (tokens, 2 * headdim), 1)
-    left = lanes < headdim
-    to_lanes = spread_matrix(share, tokens)
     start_sums = triangle(tokens, "from")
     end_sums = triangle(tokens, "before")
 
-    def chunk(c, carry):
-        base = plane + c * tokens
-        tpos = base + lax.broadcasted_iota(jnp.int32, (tokens, tokens), 0)
-        spos = base + lax.broadcasted_iota(jnp.int32, (tokens, tokens), 1)
-        tstart = doc_start(tpos, s, docs)
-        mask = jnp.where((spos <= tpos) & (spos >= tstart), 0.0, NEG)
+    def across(c):
         b = act_ref[c, :, part : part + state]
         cc = act_ref[c, :, part + state :]
-        m = dot3(cc, b, NT)
-        cum = vec_ref[c, CUM]
-        step = vec_ref[c, STEP]
-        wide[...] = spread(cum, to_lanes)
-        dm = jnp.zeros((tokens, tokens), F32)
-        for pair in range(share // 2):
-            lo = pair * 2 * headdim
-            xp = act_ref[c, :, lo : lo + 2 * headdim]
-            gp = gall_ref[c, :, lo : lo + 2 * headdim]
-            zero = jnp.zeros_like(gp)
-            gst = jnp.concatenate([jnp.where(left, gp, zero), jnp.where(left, zero, gp)], axis=0)
-            xh, xl = halves(xp)
-            factors = []
-            for h in (2 * pair, 2 * pair + 1):
-                diff = wide[:, h * tokens : (h + 1) * tokens] - cum[h : h + 1, :]
-                factors.append(jnp.exp(diff + mask) * step[h : h + 1, :])
-            pieces = jnp.concatenate([xh, xl], axis=1)
-            dw = mm(jnp.concatenate([gst, gst], axis=1), pieces, NT)
-            dm = dm + dw[:tokens] * factors[0] + dw[tokens:] * factors[1]
-            w = jnp.concatenate([m * factors[0], m * factors[1]], axis=0)
-            w = jnp.concatenate(halves(w), axis=1)
-            yst = mm(w, jnp.concatenate([pieces, pieces], axis=0), NN)
-            yst = yst[:, : 2 * headdim] + yst[:, 2 * headdim :]
-            yd[:, lo : lo + 2 * headdim] = jnp.where(left, yst[:tokens], yst[tokens:])
-            dst = mm(w, gst, TN)
-            dxd[:, lo : lo + 2 * headdim] = dst[:tokens] + dst[tokens:]
         head_in = spread(vec_ref[c, HEAD], matrix)
         tail = spread(vec_ref[c, TAIL], matrix)
         x = act_ref[c, :, :part]
         g = gall_ref[c].astype(F32)
-        y = yd[...] + head_in * dot3(cc, schain[c], NN)
+        y = y_ref[c] + head_in * dot3(cc, schain[c], NN)
         y_ref[c] = y
         dx_tail = tail * dot3(b, gchain[c], NN)
-        near = head_sums(x * dxd[...], matrix)
+        dx_near = dx_ref[c]
+        near = head_sums(x * dx_near, matrix)
         away = head_sums(x * dx_tail, matrix)
-        dx_ref[c] = dxd[...] + dx_tail
+        dx_ref[c] = dx_near + dx_tail
         xd_ref[c] = near + away
         inner = jnp.sum(schain[c] * gchain[c], axis=0, keepdims=True)
         through = head_sums(jnp.broadcast_to(inner, (8, part)), matrix)[:, :1]
@@ -371,11 +397,21 @@
             + by_triangle(away, end_sums)
             + through * vec_ref[c, WHOLE]
         )
-        dc_ref[c] = dot3(dm, b, NN) + dot3(g * head_in, schain[c], NT)
-        db_ref[c] = dot3(dm, cc, TN) + dot3(x * tail, gchain[c], NT)
+        dc_ref[c] = dc_ref[c] + dot3(g * head_in, schain[c], NT)
+        db_ref[c] = db_ref[c] + dot3(x * tail, gchain[c], NT)
+
+    def chunk(k, carry):
+        c = s[0] ^ k
+        within_chunk(
+            s, c, gall_ref.at[c], act_ref, vec_ref, y_ref, dx_ref, db_ref, dc_ref, wide, sizes,
+            docs,
+        )
+        across(c)
         return carry
 
-    lax.fori_loop(*span, chunk, 0)
+    if span[0] == 0:
+        across(s[0])
+    lax.fori_loop(max(span[0], 1), span[1], chunk, 0)
 
 
 def out_kernel(
@@ -593,11 +629,16 @@
             out[:, lo : lo + 128] = total.astype(BF16)
 
 
-def join_kernel(s, p0, p1, p2, p3, out_ref):
+def join_kernel(s, p0, p1, p2, p3, out_ref, done):
     part = p0.shape[1]
+    copies = []
     for k, ref in enumerate((p0, p1, p2, p3)):
-        q = s[0] ^ k
-        out_ref[:, pl.ds(pl.multiple_of(q * part, part), part)] = ref[...]
+        columns = pl.ds(pl.multiple_of((s[0] ^ k) * part, part), part)
+        copies.append(pltpu.make_async_copy(ref, out_ref.at[:, columns], done.at[k]))
+    for copy in copies:
+        copy.start()
+    for copy in copies:
+        copy.wait()
 
 
 def join_small_kernel(s, first, *refs):
@@ -614,32 +655,31 @@
         out[:, width + tokens :] = step[8:, :]
 
 
-def join_grad_kernel(s, p0, p1, p2, p3, g0, g1, g2, g3, out_ref, gs_ref, *, share, inner, state, groups):
+def join_grads_kernel(
+    s, p0, p1, p2, p3, g0, g1, g2, g3, out_ref, gs_ref, conv_ref, head_ref, turned, done,
+    *, share, inner, state, groups, scale,
+):
     part = inner // groups
+    width = part + 2 * state
+    copies = []
     for k, ref in enumerate((p0, p1, p2, p3)):
         q = s[0] ^ k
-        out_ref[:, pl.ds(pl.multiple_of(q * part, part), part)] = ref[:, :part]
-        out_ref[:, pl.ds(pl.multiple_of(inner + q * state, state), state)] = ref[
-            :, part : part + state
-        ]
-        out_ref[:, pl.ds(pl.multiple_of(inner + (groups + q) * state, state), state)] = ref[
-            :, part + state :
-        ]
+        for i, (size, lo, first) in enumerate((
+            (part, 0, q * part),
+            (state, part, inner + q * state),
+            (state, part + state, inner + (groups + q) * state),
+        )):
+            columns = pl.ds(pl.multiple_of(first, size), size)
+            copies.append(
+                pltpu.make_async_copy(
+                    ref.at[:, lo : lo + size], out_ref.at[:, columns], done.at[3 * k + i]
+                )
+            )
+    for copy in copies:
+        copy.start()
+    rows = conv_ref.shape[0]
+    tokens = gs_ref.shape[1]
     for k, ref in enumerate((g0, g1, g2, g3)):
-        tokens = gs_ref.shape[1]
-        last = ref.shape[1]
-        first = pl.multiple_of((s[0] ^ k) * share, share)
-        gs_ref[pl.ds(first, 8), :] = ref[:, last - 2 * tokens : last - tokens]
-        gs_ref[pl.ds(first + 8, 8), :] = ref[:, last - tokens :]
-
-
-def join_params_kernel(
-    s, p0, p1, p2, p3, conv_ref, head_ref, turned, *, share, inner, state, groups, scale
-):
-    part = inner // groups
-    width = part + 2 * state
-    rows = conv_ref.shape[0]
-    for k, ref in enumerate((p0, p1, p2, p3)):
         q = s[0] ^ k
         conv_ref[:, pl.ds(pl.multiple_of(q * part, part), part)] = ref[:rows, :part] * scale
         conv_ref[:, pl.ds(pl.multiple_of(inner + q * state, state), state)] = (
@@ -648,12 +688,19 @@
         conv_ref[:, pl.ds(pl.multiple_of(inner + (groups + q) * state, state), state)] = (
             ref[:rows, part + state : width] * scale
         )
-        turned[pl.ds(pl.multiple_of(q * share, 8), 8), :] = ref[:, width : width + 128]
-        turned[pl.ds(pl.multiple_of(q * share + 8, 8), 8), :] = ref[:, width + 128 : width + 256]
+        first = pl.multiple_of(q * share, share)
+        turned[pl.ds(first, 8), :] = ref[:, width : width + 128]
+        turned[pl.ds(first + 8, 8), :] = ref[:, width + 128 : width + 256]
+        last = width + 256
+        gs_ref[pl.ds(first, 8), :] = ref[:, last : last + tokens]
+        gs_ref[pl.ds(first + 8, 8), :] = ref[:, last + tokens :]
     head_ref[...] = turned[...].T[: head_ref.shape[0], :] * scale
-
-
-def call(kernel, table, operands, specs, outs, scratch=(), name=None, vmem=True, aliases=None):
+    for copy in copies:
+        copy.wait()
+
+
+def call(kernel, table, operands, specs, outs, scratch=(), name=None, vmem=True, aliases=None,
+         far=()):
     here = pl.BlockSpec(memory_space=pltpu.VMEM)
     in_specs = [here if spec is None else spec for spec in specs]
     return pl.pallas_call(
@@ -666,8 +713,12 @@
             num_scalar_prefetch=1,
             grid=(1,),
             in_specs=in_specs,
-            out_specs=[here] * len(outs),
-            scratch_shapes=[pltpu.VMEM(shape, kind) for shape, kind in scratch],
+            out_specs=[
+                pl.BlockSpec(memory_space=pl.ANY) if i in far else here for i in range(len(outs))
+            ],
+            scratch_shapes=[
+                pltpu.VMEM(*entry) if isinstance(entry, tuple) else entry for entry in scratch
+            ],
         ),
         compiler_params=pltpu.CompilerParams(vmem_limit_bytes=LIMIT),
         cost_estimate=pl.CostEstimate(flops=1, transcendentals=0, bytes_accessed=1),
@@ -745,7 +796,7 @@
         table,
         [conv_input, step_raw.T],
         [None] * 2,
-        [((tokens, width + tokens), BF16)] * groups + [((16, width), BF16)] * groups,
+        [((tokens + 8, width), BF16)] * groups + [((16, width), BF16)] * groups,
         name="pack",
     )
     xs, edges = packed[:groups], packed[groups:]
@@ -802,6 +853,25 @@
         aliases={16: 0, 17: 1, 18: 2},
     )
     s_near, covered = near_of(spay, state, 1, planes)
+    local_shapes = [
+        ((groups, tokens, part), F32),
+        ((groups, tokens, part), F32),
+        ((groups, tokens, state), F32),
+        ((groups, tokens, state), F32),
+        ((groups, share, tokens), F32),
+        ((groups, share, tokens), F32),
+    ]
+    triple = (share, headdim, state)
+    locals_ = call(
+        functools.partial(within_kernel, docs=docs, sizes=triple),
+        table,
+        [act, vec, gs[0]],
+        [None] * 3,
+        local_shapes[:4],
+        [((tokens, share * tokens), F32)],
+        name="within",
+    )
+    *gr, _ = lax.optimization_barrier((*gr, locals_[0]))
     gall, gpay, gchain = call(
         functools.partial(grad_state_kernel, **sizes),
         table,
@@ -815,30 +885,21 @@
         name="grad_state",
     )
     g_near, _ = near_of(gpay, state, -1, planes)
-    local_shapes = [
-        ((groups, tokens, part), F32),
-        ((groups, tokens, part), F32),
-        ((groups, tokens, state), F32),
-        ((groups, tokens, state), F32),
-        ((groups, share, tokens), F32),
-        ((groups, share, tokens), F32),
-    ]
-    locals_ = []
-    for span in ((0, 1), (1, 2), (2, 4)):
+    for span in ((0, 2), (2, 3), (3, 4)):
         locals_ = call(
-            functools.partial(local_kernel, span=span, docs=docs, **sizes),
+            functools.partial(local_kernel, span=span, docs=docs, sizes=triple),
             table,
             [act, vec, gall, schain, gchain] + list(locals_),
             [None] * (5 + len(locals_)),
             local_shapes,
-            [((tokens, share * tokens), F32)] + [((tokens, part), F32)] * 2,
+            [((tokens, share * tokens), F32)],
             name="local",
             aliases={6 + i: i for i in range(len(locals_))},
         )
-        if span[1] == 1:
+        if span[1] == 2:
             s_near, *locals_ = lax.optimization_barrier((s_near, *locals_))
             s_far = shifted(s_near, GROUPS * covered)
-        elif span[1] == 2:
+        elif span[1] == 3:
             g_near, *locals_ = lax.optimization_barrier((g_near, *locals_))
             g_far = shifted(g_near, -GROUPS * covered)
     y_local, dx_local, db_local, dc_local, flow, xd = locals_
@@ -871,7 +932,6 @@
         name="edge",
     )
     rim_back = shifted(edge, -groups)
-    triple = (share, headdim, state)
     settings = dict(sizes=triple, docs=docs, taps=taps)
     common = [high, low] + common + [xall]
     du_shape = ((groups * tokens, width), F32)
@@ -909,15 +969,15 @@
     )
     br_far = [swapped(back_far[k - 2], k) for k in (2, 3)]
     (mixer_out,) = call(
-        join_kernel, table, mr, [None] * groups, [((tokens, inner), BF16)], name="join_out",
-        vmem=False,
+        join_kernel, table, mr, [None] * groups, [((tokens, inner), BF16)],
+        [pltpu.SemaphoreType.DMA((groups,))], name="join_out", vmem=False, far=(0,),
     )
     step = groups
     received = []
     while step < devices:
         ways = 4 if 4 * step <= devices else 2
         params = functools.reduce(jnp.add, received, params)
-        received = [swapped(params, way * step) for way in range(1, ways)]
+        received = [swapped(params, way * step) for way in range(ways - 1, 0, -1)]
         step *= ways
     small = call(
         join_small_kernel,
@@ -941,24 +1001,21 @@
     )
     br = [back_near[0], swapped(back_near[1], 1)] + br_far
     pr = [small[0]] + [swapped(small[k], k) for k in range(1, groups)]
-    grad_conv, grad_heads = call(
-        functools.partial(join_params_kernel, scale=(tokens * devices) ** (-0.5), **shapes),
-        table,
-        pr,
-        [None] * groups,
-        [((taps + 1, channels), F32), ((3, heads), F32)],
-        [((heads, 128), F32)],
-        name="join_params",
-        vmem=False,
-    )
-    grad_input, grad_step = call(
-        functools.partial(join_grad_kernel, **shapes),
+    grad_input, grad_step, grad_conv, grad_heads = call(
+        functools.partial(join_grads_kernel, scale=(tokens * devices) ** (-0.5), **shapes),
         table,
         br + pr,
         [None] * (2 * groups),
-        [((tokens, channels), BF16), ((heads, tokens), F32)],
-        name="join_grad",
+        [
+            ((tokens, channels), BF16),
+            ((heads, tokens), F32),
+            ((taps + 1, channels), F32),
+            ((3, heads), F32),
+        ],
+        [((heads, 128), F32), pltpu.SemaphoreType.DMA((3 * groups,))],
+        name="join_grads",
         vmem=False,
+        far=(0,),
     )
     return mixer_out, grad_input, grad_step.T, grad_conv, grad_heads
 

time: 108 us -> 107 us (level)
    ppermute x18, waiting for transfers between devices: 10.9 us -> 8.76 us  [swapped(): return lax.ppermute(value, 'ctx', [(i, i ^ bits) for i in range(count)])]
    ppermute x5, waiting for transfers between devices: 4.36 us -> 6.49 us  [shifted(): return lax.ppermute(value, 'ctx', pairs)]
  transfers between devices with their start and end apart: 27 -> 27, of which waited for: 7 -> 9; matrix products, arithmetic and copies ran while one was open for 0% -> 0% of each run, Pallas kernels for 40% -> 40%
where the time goes in v4:
time: 107 us
  Pallas kernels  47.3 us (44%)
  starting transfers between devices  37.1 us (35%)
  waiting for transfers between devices  15.3 us (14%)
  local copies, waits for them, and re-layouts  5.27 us (5%)
  between operations  1.13 us (1%)
    pallas_call x18, Pallas kernels, call(): pl.pallas_call(kernel, out_shape=[pltpu.VMEM(shape, kind) if vmem else ja...  47.3 us
    ppermute x18, starting transfers between devices, swapped(): return lax.ppermute(value, 'ctx', [(i, i ^ bits) for i in range(count)])  22 us
    ppermute x5, starting transfers between devices, shifted(): return lax.ppermute(value, 'ctx', pairs)  12.5 us
    ppermute x18, waiting for transfers between devices, swapped(): return lax.ppermute(value, 'ctx', [(i, i ^ bits) for i in range(count)])  8.76 us
    ppermute x5, waiting for transfers between devices, shifted(): return lax.ppermute(value, 'ctx', pairs)  6.49 us
    unnamed x16, local copies, waits for them, and re-layouts  5.27 us
    ppermute x4, starting transfers between devices, body(): rims.append(lax.ppermute(edges[k], 'ctx', pairs))  2.64 us
  transfers between devices with their start and end apart: 27, of which 9 were waited for; matrix products, arithmetic and copies ran while one was open for 0% of the time, Pallas kernels for 40%

profile of v4, /device:TPU:0, one launch (start us, length us, event | category | flops | bytes accessed | tf_op | source)
XLA Modules:
  0.0 106.8 jit_solution(6443036036758394885)
XLA Ops:
  1.4 1.3 %copy-done.1 = bf16[128,5120]{1,0:T(8,128)(2,1)S(1)} copy-done((bf16[128,5120]{1,0:T(8,128)(2,1)S(1)}, bf16[128,5120]{1,0:T(8,128)(2,1)}, u32[]{:S(2)}) %copy-start.1) | copy-done | bytes 1310744
  4.7 2.6 %collective-permute-start.4 = (bf16[136,1280]{1,0:T(8,128)(2,1)S(1)}, bf16[136,1280]{1,0:T(8,128)(2,1)S(1)}, u32[]{:S(2)}, u32[]{:S(2)}) collective-permute-start(bf16[136,1280]{1,0:T(8,128)(2,1)S(1)} %get-tuple-element.130), channel_id=1, source_target_pairs={{0,2},{1,3},{2,0},{3,1},{4,6},{5,7},{6,4},{7,5},{8,10},{9,11},{10,... | collective-permute-start | bytes 1044488 | tf_op jit(solution)/shard_map/ppermute | solution.py:732
  10.1 1.2 %copy-done.2 = bf16[128,4096]{1,0:T(8,128)(2,1)S(1)} copy-done((bf16[128,4096]{1,0:T(8,128)(2,1)S(1)}, bf16[128,4096]{1,0:T(8,128)(2,1)}, u32[]{:S(2)}) %copy-start.2) | copy-done | bytes 1048600
  13.9 2.5 %conv.1 = (f32[4,128,1280]{2,1,0:T(8,128)S(1)}, f32[4,128,1280]{2,1,0:T(8,128)S(1)}, bf16[528,1280]{1,0:T(8,128)(2,1)S(1)}) custom-call(s32[6]{0:T(128)S(1)} %pad_add_fusion.s, bf16[136,1280]{1,0:T(8,128)(2,1)S(1)} %get-tuple-element.119.x0, bf16[136,1280]{1,0:T(8,128)(2,1)S(1)} %collective-permute-done.x1, f32[4,5120]{1,0:T(4,128)S(1)} %copy-done, ...), custom_call_target="tpu_custom_call" | custom-call | flops 1 | bytes 1 | tf_op jit(solution)/shard_map/conv/pallas_call | solution.py:706
  16.4 6.9 %collective-permute-start.1 = (bf16[128,1024]{1,0:T(8,128)(2,1)S(1)}, bf16[128,1024]{1,0:T(8,128)(2,1)S(1)}, u32[]{:S(2)}, u32[]{:S(2)}) collective-permute-start(bf16[128,1024]{1,0:T(8,128)(2,1)S(1)} %get-tuple-element.127), channel_id=1, source_target_pairs={{0,1},{1,0},{2,3},{3,2},{4,5},{5,4},{6,7},{7,6},{8,9},{9,8},{10,11... | collective-permute-start | bytes 786440 | tf_op jit(solution)/shard_map/ppermute | solution.py:732
  23.6 1.6 %collective-permute-start.3 = (bf16[128,1024]{1,0:T(8,128)(2,1)S(1)}, bf16[128,1024]{1,0:T(8,128)(2,1)S(1)}, u32[]{:S(2)}, u32[]{:S(2)}) collective-permute-start(bf16[128,1024]{1,0:T(8,128)(2,1)S(1)} %get-tuple-element.129), channel_id=1, source_target_pairs={{0,3},{1,2},{2,1},{3,0},{4,7},{5,6},{6,5},{7,4},{8,11},{9,10},{10,... | collective-permute-start | bytes 786440 | tf_op jit(solution)/shard_map/ppermute | solution.py:732
  25.1 4.6 %conv_state.1 = (f32[4,128,1280]{2,1,0:T(8,128)S(1)}, f32[4,128,1280]{2,1,0:T(8,128)S(1)}, bf16[528,1280]{1,0:T(8,128)(2,1)S(1)}, f32[136,1024]{1,0:T(8,128)S(1)...) custom-call(s32[6]{0:T(128)S(1)} %pad_add_fusion.s, ...), custom_call_target="tpu_custom_call", output_to_operand_aliasing={{0}: (16, {}), {1}: (17, {}), {2}: (18, {})} | custom-call | flops 1 | bytes 1 | tf_op jit(solution)/shard_map/conv_state/pallas_call | solution.py:706
  29.8 3.6 %collective-permute-start.11 = (f32[136,1024]{1,0:T(8,128)S(1)}, f32[136,1024]{1,0:T(8,128)S(1)}, u32[]{:S(2)}, u32[]{:S(2)}) collective-permute-start(f32[136,1024]{1,0:T(8,128)S(1)} %get-tuple-element.147.pay_in.pay), channel_id=1, source_target_pairs={{0,4},{1,5},{2,6},{3,7},{4,8},{5,9},{6,10},{7,11},{8,12},{9,13},{1... | collective-permute-start | bytes 1671176 | tf_op jit(solution)/shard_map/ppermute | solution.py:738
  33.4 2.0 %within.1 = (f32[4,128,1024]{2,1,0:T(8,128)S(1)}, f32[4,128,1024]{2,1,0:T(8,128)S(1)}, f32[4,128,128]{2,1,0:T(8,128)S(1)}, f32[4,128,128]{2,1,0:T(8,128)S(1)}) custom-call(s32[6]{0:T(128)S(1)} %pad_add_fusion.s, f32[4,128,1280]{2,1,0:T(8,128)S(1)} %get-tuple-element.140.act_ref, f32[4,8,16,128]{3,2,1,0:T(8,128)S(1)} %get-tuple-element.141.vec_ref, ...), custom_call_target="tpu_custom_call" | custom-call | flops 1 | bytes 1 | tf_op jit(solution)/shard_map/within/pallas_call | solution.py:706
  35.4 1.7 %collective-permute-done.3.g3 = bf16[128,1024]{1,0:T(8,128)(2,1)S(1)} collective-permute-done((bf16[128,1024]{1,0:T(8,128)(2,1)S(1)}, bf16[128,1024]{1,0:T(8,128)(2,1)S(1)}, u32[]{:S(2)}, u32[]{:S(2)}) %collective-permute-start.3) | collective-permute-done | bytes 262176 | tf_op jit(solution)/shard_map/ppermute | solution.py:732
  37.2 2.4 %grad_state.1 = (bf16[4,128,1024]{2,1,0:T(8,128)(2,1)S(1)}, f32[136,1024]{1,0:T(8,128)S(1)}, f32[4,128,1024]{2,1,0:T(8,128)S(1)}) custom-call(s32[6]{0:T(128)S(1)} %pad_add_fusion.s, bf16[128,1024]{1,0:T(8,128)(2,1)S(1)} %get-tuple-element.143.g_ref.g0, bf16[128,1024]{1,0:T(8,128)(2,1)S(1)} %collective-permute-done.1.g1, ...), custom_call_target="tpu_custom_call" | custom-call | flops 1 | bytes 1 | tf_op jit(solution)/shard_map/grad_state/pallas_call | solution.py:706
  39.6 1.5 %collective-permute-start.10 = (f32[136,1024]{1,0:T(8,128)S(1)}, f32[136,1024]{1,0:T(8,128)S(1)}, u32[]{:S(2)}, u32[]{:S(2)}) collective-permute-start(f32[136,1024]{1,0:T(8,128)S(1)} %get-tuple-element.148), channel_id=1, source_target_pairs={{4,0},{5,1},{6,2},{7,3},{8,4},{9,5},{10,6},{11,7},{12,8},{13,9},{1... | collective-permute-start | bytes 1671176 | tf_op jit(solution)/shard_map/ppermute | solution.py:738
  41.0 5.9 %local.3 = (f32[4,128,1024]{2,1,0:T(8,128)S(1)}, f32[4,128,1024]{2,1,0:T(8,128)S(1)}, f32[4,128,128]{2,1,0:T(8,128)S(1)}, f32[4,128,128]{2,1,0:T(8,128)S(1)}, f3...) custom-call(s32[6]{0:T(128)S(1)} %pad_add_fusion.s, ...), custom_call_target="tpu_custom_call", output_to_operand_aliasing={{0}: (6, {}), {1}: (7, {}), {2}: (8, {}), {3}: (9, {})} | custom-call | flops 1 | bytes 1 | tf_op jit(solution)/shard_map/local/pallas_call | solution.py:706
  46.9 4.6 %collective-permute-start.13 = (f32[136,1024]{1,0:T(8,128)S(1)}, f32[136,1024]{1,0:T(8,128)S(1)}, u32[]{:S(2)}, u32[]{:S(2)}) collective-permute-start(f32[136,1024]{1,0:T(8,128)S(1)} %collective-permute-done.11.one), channel_id=1, source_target_pairs={{0,4},{1,5},{2,6},{3,7},{4,8},{5,9},{6,10},{7,11},{8,12},{9,13},{1... | collective-permute-start | bytes 1671176 | tf_op jit(solution)/shard_map/ppermute | solution.py:738
  51.5 4.0 %local.4 = (f32[4,128,1024]{2,1,0:T(8,128)S(1)}, f32[4,128,1024]{2,1,0:T(8,128)S(1)}, f32[4,128,128]{2,1,0:T(8,128)S(1)}, f32[4,128,128]{2,1,0:T(8,128)S(1)}, f3...) custom-call(s32[6]{0:T(128)S(1)} %pad_add_fusion.s, ...), custom_call_target="tpu_custom_call", output_to_operand_aliasing={{0}: (6, {}), {1}: (7, {}), {2}: (8, {}), {3}: (9, {}), {4}... | custom-call | flops 1 | bytes 1 | tf_op jit(solution)/shard_map/local/pallas_call | solution.py:706
  56.5 1.3 %collective-permute-start.12 = (f32[136,1024]{1,0:T(8,128)S(1)}, f32[136,1024]{1,0:T(8,128)S(1)}, u32[]{:S(2)}, u32[]{:S(2)}) collective-permute-start(f32[136,1024]{1,0:T(8,128)S(1)} %collective-permute-done.10.one), channel_id=1, source_target_pairs={{4,0},{5,1},{6,2},{7,3},{8,4},{9,5},{10,6},{11,7},{12,8},{13,9},{1... | collective-permute-start | bytes 1671176 | tf_op jit(solution)/shard_map/ppermute | solution.py:738
  57.8 4.0 %local.5 = (f32[4,128,1024]{2,1,0:T(8,128)S(1)}, f32[4,128,1024]{2,1,0:T(8,128)S(1)}, f32[4,128,128]{2,1,0:T(8,128)S(1)}, f32[4,128,128]{2,1,0:T(8,128)S(1)}, f3...) custom-call(s32[6]{0:T(128)S(1)} %pad_add_fusion.s, ...), custom_call_target="tpu_custom_call", output_to_operand_aliasing={{0}: (6, {}), {1}: (7, {}), {2}: (8, {}), {3}: (9, {}), {4}... | custom-call | flops 1 | bytes 1 | tf_op jit(solution)/shard_map/local/pallas_call | solution.py:706
  61.8 2.0 %collective-permute-done.13.two = f32[136,1024]{1,0:T(8,128)S(1)} collective-permute-done((f32[136,1024]{1,0:T(8,128)S(1)}, f32[136,1024]{1,0:T(8,128)S(1)}, u32[]{:S(2)}, u32[]{:S(2)}) %collective-permute-start.13) | collective-permute-done | bytes 557088 | tf_op jit(solution)/shard_map/ppermute | solution.py:738
  63.7 3.8 %out.1 = (bf16[128,1024]{1,0:T(8,128)(2,1)S(1)}, bf16[128,1024]{1,0:T(8,128)(2,1)S(1)}, bf16[128,1024]{1,0:T(8,128)(2,1)S(1)}, bf16[128,1024]{1,0:T(8,128)(2,1)S...) custom-call(s32[6]{0:T(128)S(1)} %pad_add_fusion.s, ...), custom_call_target="tpu_custom_call" | custom-call | flops 1 | bytes 1 | tf_op jit(solution)/shard_map/out/pallas_call | solution.py:706
  69.5 3.5 %collective-permute-done.12.two = f32[136,1024]{1,0:T(8,128)S(1)} collective-permute-done((f32[136,1024]{1,0:T(8,128)S(1)}, f32[136,1024]{1,0:T(8,128)S(1)}, u32[]{:S(2)}, u32[]{:S(2)}) %collective-permute-start.12) | collective-permute-done | bytes 557088 | tf_op jit(solution)/shard_map/ppermute | solution.py:738
  74.2 1.5 %collective-permute-start.14 = (f32[8,1280]{1,0:T(8,128)S(1)}, f32[8,1280]{1,0:T(8,128)S(1)}, u32[]{:S(2)}, u32[]{:S(2)}) collective-permute-start(f32[8,1280]{1,0:T(8,128)S(1)} %get-tuple-element.199), channel_id=1, source_target_pairs={{4,0},{5,1},{6,2},{7,3},{8,4},{9,5},{10,6},{11,7},{12,8},{13,9},{1... | collective-permute-start | bytes 122888 | tf_op jit(solution)/shard_map/ppermute | solution.py:738
  75.7 3.6 %back_far.1 = (f32[512,1280]{1,0:T(8,128)S(1)}, f32[8,1536]{1,0:T(8,128)S(1)}, f32[3,16,128]{2,1,0:T(8,128)S(1)}) custom-call(s32[6]{0:T(128)S(1)} %pad_add_fusion.s, bf16[128,1024]{1,0:T(8,128)(2,1)S(1)} %get-tuple-element.187.high_ref, bf16[128,1024]{1,0:T(8,128)(2,1)S(1)} %get-tuple-element.188.low_ref, f32[4,128,1280]{2,1,0:T(8,128)S(1)} %get-tuple-element.140.act_ref, ...), custom_call_target="tpu_custom_call" | custom-call | flops 1 | bytes 1 | tf_op jit(solution)/shard_map/back_far/pallas_call | solution.py:706
  79.4 4.5 %back_near.1 = (f32[512,1280]{1,0:T(8,128)S(1)}, f32[8,1536]{1,0:T(8,128)S(1)}, f32[16,128]{1,0:T(8,128)S(1)}, f32[16,128]{1,0:T(8,128)S(1)}, f32[16,128]{1,0:T(8,128)S(1)}, /*index=5*/f32[16,128]{1,0:T(8,128)S(1)}) custom-call(s32[6]{0:T(128)S(1)} %pad_add_fusion.s, ...), custom_call_target="tpu_custom_call", output_to_operand_aliasing={{0}: (20, {})} | custom-call | flops 1 | bytes 1 | tf_op jit(solution)/shard_map/back_near/pallas_call | solution.py:706
  83.9 1.6 %conv_back_far.1 = (bf16[128,1280]{1,0:T(8,128)(2,1)S(1)}, bf16[128,1280]{1,0:T(8,128)(2,1)S(1)}) custom-call(s32[6]{0:T(128)S(1)} %pad_add_fusion.s, f32[512,1280]{1,0:T(8,128)S(1)} %get-tuple-element.220.du_ref, f32[8,1280]{1,0:T(8,128)S(1)} %collective-permute-done.14.rim_ref, f32[4,5120]{1,0:T(4,128)S(1)} %copy-done, f32[4,5120]{1,0:T(4,128)S(1)} %copy-done, ...), custom_call_target="tpu_custom_call" | custom-call | flops 1 | bytes 1 | tf_op jit(solution)/shard_map/conv_back_far/pallas_call | solution.py:706
  85.5 4.9 %collective-permute-start.19 = (f32[8,1536]{1,0:T(8,128)S(1)}, f32[8,1536]{1,0:T(8,128)S(1)}, u32[]{:S(2)}, u32[]{:S(2)}) collective-permute-start(f32[8,1536]{1,0:T(8,128)S(1)} %get-tuple-element.210.first), channel_id=1, source_target_pairs={{0,12},{1,13},{2,14},{3,15},{4,8},{5,9},{6,10},{7,11},{8,4},{9,5},... | collective-permute-start | bytes 147464 | tf_op jit(solution)/shard_map/ppermute | solution.py:732
  91.0 1.5 %join_out.1 = bf16[128,4096]{1,0:T(8,128)(2,1)} custom-call(s32[6]{0:T(128)S(1)} %pad_add_fusion.s, bf16[128,1024]{1,0:T(8,128)(2,1)S(1)} %get-tuple-element.206.p0, bf16[128,1024]{1,0:T(8,128)(2,1)S(1)} %collective-permute-done.15.p1, bf16[128,1024]{1,0:T(8,128)(2,1)S(1)} %collective-permute-done.16.p2, bf16[128,1024]{1,0:T(8,128)(2,1)S(1)} %collective-permute-done.17.p3), custom_call_target="tpu_custom_call" | custom-call | flops 1 | bytes 1 | tf_op jit(solution)/shard_map/join_out/pallas_call | solution.py:706
  92.8 2.6 %collective-permute-done.20.refs_1_ = f32[8,1536]{1,0:T(8,128)S(1)} collective-permute-done((f32[8,1536]{1,0:T(8,128)S(1)}, f32[8,1536]{1,0:T(8,128)S(1)}, u32[]{:S(2)}, u32[]{:S(2)}) %collective-permute-start.20) | collective-permute-done | bytes 49184 | tf_op jit(solution)/shard_map/ppermute | solution.py:732
  96.0 1.6 %conv_back_near.1 = (bf16[128,1280]{1,0:T(8,128)(2,1)S(1)}, bf16[128,1280]{1,0:T(8,128)(2,1)S(1)}) custom-call(s32[6]{0:T(128)S(1)} %pad_add_fusion.s, f32[512,1280]{1,0:T(8,128)S(1)} %get-tuple-element.220.du_ref, f32[8,1280]{1,0:T(8,128)S(1)} %collective-permute-done.14.rim_ref, f32[4,5120]{1,0:T(4,128)S(1)} %copy-done, f32[4,5120]{1,0:T(4,128)S(1)} %copy-done, ...), custom_call_target="tpu_custom_call" | custom-call | flops 1 | bytes 1 | tf_op jit(solution)/shard_map/conv_back_near/pallas_call | solution.py:706
  98.1 1.9 %collective-permute-start.25 = (f32[8,1792]{1,0:T(8,128)S(1)}, f32[8,1792]{1,0:T(8,128)S(1)}, u32[]{:S(2)}, u32[]{:S(2)}) collective-permute-start(f32[8,1792]{1,0:T(8,128)S(1)} %get-tuple-element.227), channel_id=1, source_target_pairs={{0,2},{1,3},{2,0},{3,1},{4,6},{5,7},{6,4},{7,5},{8,10},{9,11},{10,... | collective-permute-start | bytes 172040 | tf_op jit(solution)/shard_map/ppermute | solution.py:732
  101.1 1.5 %collective-permute-done.25.g2 = f32[8,1792]{1,0:T(8,128)S(1)} collective-permute-done((f32[8,1792]{1,0:T(8,128)S(1)}, f32[8,1792]{1,0:T(8,128)S(1)}, u32[]{:S(2)}, u32[]{:S(2)}) %collective-permute-start.25) | collective-permute-done | bytes 57376 | tf_op jit(solution)/shard_map/ppermute | solution.py:732
  102.6 1.6 %collective-permute-done.26.g3 = f32[8,1792]{1,0:T(8,128)S(1)} collective-permute-done((f32[8,1792]{1,0:T(8,128)S(1)}, f32[8,1792]{1,0:T(8,128)S(1)}, u32[]{:S(2)}, u32[]{:S(2)}) %collective-permute-start.26) | collective-permute-done | bytes 57376 | tf_op jit(solution)/shard_map/ppermute | solution.py:732
  104.3 2.4 %join_grads.1 = (bf16[128,5120]{1,0:T(8,128)(2,1)}, f32[64,128]{1,0:T(8,128)}, f32[5,5120]{1,0:T(8,128)}, f32[3,64]{1,0:T(4,128)}) custom-call(s32[6]{0:T(128)S(1)} %pad_add_fusion.s, bf16[128,1280]{1,0:T(8,128)(2,1)S(1)} %get-tuple-element.221.p0, bf16[128,1280]{1,0:T(8,128)(2,1)S(1)} %collective-permute-done.22.p1, ...), custom_call_target="tpu_custom_call" | custom-call | flops 1 | bytes 1 | tf_op jit(solution)/shard_map/join_grads/pallas_call | solution.py:706
  (57 shorter events, 15.6 us)
Async XLA Ops:
  0.6 13.3 %copy-start = (f32[4,5120]{1,0:T(4,128)S(1)}, f32[4,5120]{1,0:T(4,128)}, u32[]{:S(2)}) copy-start(f32[4,5120]{1,0:T(4,128)} %wc.7) | copy-start | bytes 245764
  1.4 1.3 %copy-start.1 = (bf16[128,5120]{1,0:T(8,128)(2,1)S(1)}, bf16[128,5120]{1,0:T(8,128)(2,1)}, u32[]{:S(2)}) copy-start(bf16[128,5120]{1,0:T(8,128)(2,1)} %x_ref.1) | copy-start | bytes 3932164
  2.7 0.8 copy-start.4
  3.5 10.4 %copy-start.3 = (f32[5120]{0:T(1024)S(1)}, f32[5120]{0:T(1024)}, u32[]{:S(2)}) copy-start(f32[5120]{0:T(1024)} %param.15) | copy-start | bytes 61444
  4.2 5.2 %collective-permute-start = (bf16[136,1280]{1,0:T(8,128)(2,1)S(1)}, bf16[136,1280]{1,0:T(8,128)(2,1)S(1)}, u32[]{:S(2)}, u32[]{:S(2)}) collective-permute-start(bf16[136,1280]{1,0:T(8,128)(2,1)S(1)} %get-tuple-element.120), channel_id=1, source_target_pairs={{0,1},{1,0},{2,3},{3,2},{4,5},{5,4},{6,7},{7,6},{8,9},{9,8},{10,11... | collective-permute-start | bytes 1044488 | tf_op jit(solution)/shard_map/ppermute | solution.py:732
  4.7 20.4 %collective-permute-start.4 = (bf16[136,1280]{1,0:T(8,128)(2,1)S(1)}, bf16[136,1280]{1,0:T(8,128)(2,1)S(1)}, u32[]{:S(2)}, u32[]{:S(2)}) collective-permute-start(bf16[136,1280]{1,0:T(8,128)(2,1)S(1)} %get-tuple-element.130), channel_id=1, source_target_pairs={{0,2},{1,3},{2,0},{3,1},{4,6},{5,7},{6,4},{7,5},{8,10},{9,11},{10,... | collective-permute-start | bytes 1044488 | tf_op jit(solution)/shard_map/ppermute | solution.py:732
  7.3 17.8 %collective-permute-start.5 = (bf16[136,1280]{1,0:T(8,128)(2,1)S(1)}, bf16[136,1280]{1,0:T(8,128)(2,1)S(1)}, u32[]{:S(2)}, u32[]{:S(2)}) collective-permute-start(bf16[136,1280]{1,0:T(8,128)(2,1)S(1)} %get-tuple-element.131), channel_id=1, source_target_pairs={{0,3},{1,2},{2,1},{3,0},{4,7},{5,6},{6,5},{7,4},{8,11},{9,10},{10,... | collective-permute-start | bytes 1044488 | tf_op jit(solution)/shard_map/ppermute | solution.py:732
  7.4 1.3 %collective-permute-start.6 = (bf16[16,1280]{1,0:T(8,128)(2,1)S(1)}, bf16[16,1280]{1,0:T(8,128)(2,1)S(1)}, u32[]{:S(2)}, u32[]{:S(2)}) collective-permute-start(bf16[16,1280]{1,0:T(8,128)(2,1)S(1)} %get-tuple-element.132), channel_id=1, source_target_pairs={{3,7},{7,11},{11,15},{19,23},{23,27},{27,31}} | collective-permute-start | bytes 122888 | tf_op jit(solution)/shard_map/ppermute | solution.py:820
  8.0 8.4 %collective-permute-start.7 = (bf16[16,1280]{1,0:T(8,128)(2,1)S(1)}, bf16[16,1280]{1,0:T(8,128)(2,1)S(1)}, u32[]{:S(2)}, u32[]{:S(2)}) collective-permute-start(bf16[16,1280]{1,0:T(8,128)(2,1)S(1)} %get-tuple-element.133), channel_id=1, source_target_pairs={{3,6},{7,10},{11,14},{19,22},{23,26},{27,30}} | collective-permute-start | bytes 122888 | tf_op jit(solution)/shard_map/ppermute | solution.py:820
  8.7 14.6 %collective-permute-start.8 = (bf16[16,1280]{1,0:T(8,128)(2,1)S(1)}, bf16[16,1280]{1,0:T(8,128)(2,1)S(1)}, u32[]{:S(2)}, u32[]{:S(2)}) collective-permute-start(bf16[16,1280]{1,0:T(8,128)(2,1)S(1)} %get-tuple-element.134), channel_id=1, source_target_pairs={{1,3},{3,5},{5,7},{7,9},{9,11},{11,13},{13,15},{17,19},{19,21},{21... | collective-permute-start | bytes 122888 | tf_op jit(solution)/shard_map/ppermute | solution.py:820
  9.4 14.2 %collective-permute-start.9 = (bf16[16,1280]{1,0:T(8,128)(2,1)S(1)}, bf16[16,1280]{1,0:T(8,128)(2,1)S(1)}, u32[]{:S(2)}, u32[]{:S(2)}) collective-permute-start(bf16[16,1280]{1,0:T(8,128)(2,1)S(1)} %get-tuple-element.135), channel_id=1, source_target_pairs={{1,2},{3,4},{5,6},{7,8},{9,10},{11,12},{13,14},{17,18},{19,20},{21... | collective-permute-start | bytes 122888 | tf_op jit(solution)/shard_map/ppermute | solution.py:820
  10.1 1.2 %copy-start.2 = (bf16[128,4096]{1,0:T(8,128)(2,1)S(1)}, bf16[128,4096]{1,0:T(8,128)(2,1)}, u32[]{:S(2)}) copy-start(bf16[128,4096]{1,0:T(8,128)(2,1)} %g_ref.1) | copy-start | bytes 3145732
  16.4 19.0 %collective-permute-start.1 = (bf16[128,1024]{1,0:T(8,128)(2,1)S(1)}, bf16[128,1024]{1,0:T(8,128)(2,1)S(1)}, u32[]{:S(2)}, u32[]{:S(2)}) collective-permute-start(bf16[128,1024]{1,0:T(8,128)(2,1)S(1)} %get-tuple-element.127), channel_id=1, source_target_pairs={{0,1},{1,0},{2,3},{3,2},{4,5},{5,4},{6,7},{7,6},{8,9},{9,8},{10,11... | collective-permute-start | bytes 786440 | tf_op jit(solution)/shard_map/ppermute | solution.py:732
  23.3 12.1 %collective-permute-start.2 = (bf16[128,1024]{1,0:T(8,128)(2,1)S(1)}, bf16[128,1024]{1,0:T(8,128)(2,1)S(1)}, u32[]{:S(2)}, u32[]{:S(2)}) collective-permute-start(bf16[128,1024]{1,0:T(8,128)(2,1)S(1)} %get-tuple-element.128), channel_id=1, source_target_pairs={{0,2},{1,3},{2,0},{3,1},{4,6},{5,7},{6,4},{7,5},{8,10},{9,11},{10,... | collective-permute-start | bytes 786440 | tf_op jit(solution)/shard_map/ppermute | solution.py:732
  23.6 13.6 %collective-permute-start.3 = (bf16[128,1024]{1,0:T(8,128)(2,1)S(1)}, bf16[128,1024]{1,0:T(8,128)(2,1)S(1)}, u32[]{:S(2)}, u32[]{:S(2)}) collective-permute-start(bf16[128,1024]{1,0:T(8,128)(2,1)S(1)} %get-tuple-element.129), channel_id=1, source_target_pairs={{0,3},{1,2},{2,1},{3,0},{4,7},{5,6},{6,5},{7,4},{8,11},{9,10},{10,... | collective-permute-start | bytes 786440 | tf_op jit(solution)/shard_map/ppermute | solution.py:732
  29.8 17.2 %collective-permute-start.11 = (f32[136,1024]{1,0:T(8,128)S(1)}, f32[136,1024]{1,0:T(8,128)S(1)}, u32[]{:S(2)}, u32[]{:S(2)}) collective-permute-start(f32[136,1024]{1,0:T(8,128)S(1)} %get-tuple-element.147.pay_in.pay), channel_id=1, source_target_pairs={{0,4},{1,5},{2,6},{3,7},{4,8},{5,9},{6,10},{7,11},{8,12},{9,13},{1... | collective-permute-start | bytes 1671176 | tf_op jit(solution)/shard_map/ppermute | solution.py:738
  39.6 16.9 %collective-permute-start.10 = (f32[136,1024]{1,0:T(8,128)S(1)}, f32[136,1024]{1,0:T(8,128)S(1)}, u32[]{:S(2)}, u32[]{:S(2)}) collective-permute-start(f32[136,1024]{1,0:T(8,128)S(1)} %get-tuple-element.148), channel_id=1, source_target_pairs={{4,0},{5,1},{6,2},{7,3},{8,4},{9,5},{10,6},{11,7},{12,8},{13,9},{1... | collective-permute-start | bytes 1671176 | tf_op jit(solution)/shard_map/ppermute | solution.py:738
  46.9 16.8 %collective-permute-start.13 = (f32[136,1024]{1,0:T(8,128)S(1)}, f32[136,1024]{1,0:T(8,128)S(1)}, u32[]{:S(2)}, u32[]{:S(2)}) collective-permute-start(f32[136,1024]{1,0:T(8,128)S(1)} %collective-permute-done.11.one), channel_id=1, source_target_pairs={{0,4},{1,5},{2,6},{3,7},{4,8},{5,9},{6,10},{7,11},{8,12},{9,13},{1... | collective-permute-start | bytes 1671176 | tf_op jit(solution)/shard_map/ppermute | solution.py:738
  56.5 16.5 %collective-permute-start.12 = (f32[136,1024]{1,0:T(8,128)S(1)}, f32[136,1024]{1,0:T(8,128)S(1)}, u32[]{:S(2)}, u32[]{:S(2)}) collective-permute-start(f32[136,1024]{1,0:T(8,128)S(1)} %collective-permute-done.10.one), channel_id=1, source_target_pairs={{4,0},{5,1},{6,2},{7,3},{8,4},{9,5},{10,6},{11,7},{12,8},{13,9},{1... | collective-permute-start | bytes 1671176 | tf_op jit(solution)/shard_map/ppermute | solution.py:738
  67.5 16.3 %collective-permute-start.15 = (bf16[128,1024]{1,0:T(8,128)(2,1)S(1)}, bf16[128,1024]{1,0:T(8,128)(2,1)S(1)}, u32[]{:S(2)}, u32[]{:S(2)}) collective-permute-start(bf16[128,1024]{1,0:T(8,128)(2,1)S(1)} %get-tuple-element.201), channel_id=1, source_target_pairs={{0,1},{1,0},{2,3},{3,2},{4,5},{5,4},{6,7},{7,6},{8,9},{9,8},{10,11... | collective-permute-start | bytes 786440 | tf_op jit(solution)/shard_map/ppermute | solution.py:732
  67.6 16.2 %collective-permute-start.16 = (bf16[128,1024]{1,0:T(8,128)(2,1)S(1)}, bf16[128,1024]{1,0:T(8,128)(2,1)S(1)}, u32[]{:S(2)}, u32[]{:S(2)}) collective-permute-start(bf16[128,1024]{1,0:T(8,128)(2,1)S(1)} %get-tuple-element.202), channel_id=1, source_target_pairs={{0,2},{1,3},{2,0},{3,1},{4,6},{5,7},{6,4},{7,5},{8,10},{9,11},{10,... | collective-permute-start | bytes 786440 | tf_op jit(solution)/shard_map/ppermute | solution.py:732
  68.5 15.4 %collective-permute-start.17 = (bf16[128,1024]{1,0:T(8,128)(2,1)S(1)}, bf16[128,1024]{1,0:T(8,128)(2,1)S(1)}, u32[]{:S(2)}, u32[]{:S(2)}) collective-permute-start(bf16[128,1024]{1,0:T(8,128)(2,1)S(1)} %get-tuple-element.203), channel_id=1, source_target_pairs={{0,3},{1,2},{2,1},{3,0},{4,7},{5,6},{6,5},{7,4},{8,11},{9,10},{10,... | collective-permute-start | bytes 786440 | tf_op jit(solution)/shard_map/ppermute | solution.py:732
  74.2 9.7 %collective-permute-start.14 = (f32[8,1280]{1,0:T(8,128)S(1)}, f32[8,1280]{1,0:T(8,128)S(1)}, u32[]{:S(2)}, u32[]{:S(2)}) collective-permute-start(f32[8,1280]{1,0:T(8,128)S(1)} %get-tuple-element.199), channel_id=1, source_target_pairs={{4,0},{5,1},{6,2},{7,3},{8,4},{9,5},{10,6},{11,7},{12,8},{13,9},{1... | collective-permute-start | bytes 122888 | tf_op jit(solution)/shard_map/ppermute | solution.py:738
  85.4 10.5 %collective-permute-start.18 = (bf16[128,1280]{1,0:T(8,128)(2,1)S(1)}, bf16[128,1280]{1,0:T(8,128)(2,1)S(1)}, u32[]{:S(2)}, u32[]{:S(2)}) collective-permute-start(bf16[128,1280]{1,0:T(8,128)(2,1)S(1)} %get-tuple-element.205), channel_id=1, source_target_pairs={{0,2},{1,3},{2,0},{3,1},{4,6},{5,7},{6,4},{7,5},{8,10},{9,11},{10,... | collective-permute-start | bytes 983048 | tf_op jit(solution)/shard_map/ppermute | solution.py:732
  85.5 7.3 %collective-permute-start.19 = (f32[8,1536]{1,0:T(8,128)S(1)}, f32[8,1536]{1,0:T(8,128)S(1)}, u32[]{:S(2)}, u32[]{:S(2)}) collective-permute-start(f32[8,1536]{1,0:T(8,128)S(1)} %get-tuple-element.210.first), channel_id=1, source_target_pairs={{0,12},{1,13},{2,14},{3,15},{4,8},{5,9},{6,10},{7,11},{8,4},{9,5},... | collective-permute-start | bytes 147464 | tf_op jit(solution)/shard_map/ppermute | solution.py:732
  90.4 5.0 %collective-permute-start.20 = (f32[8,1536]{1,0:T(8,128)S(1)}, f32[8,1536]{1,0:T(8,128)S(1)}, u32[]{:S(2)}, u32[]{:S(2)}) collective-permute-start(f32[8,1536]{1,0:T(8,128)S(1)} %get-tuple-element.210.first), channel_id=1, source_target_pairs={{0,8},{1,9},{2,10},{3,11},{4,12},{5,13},{6,14},{7,15},{8,0},{9,1},... | collective-permute-start | bytes 147464 | tf_op jit(solution)/shard_map/ppermute | solution.py:732
  90.4 5.0 %collective-permute-start.21 = (f32[8,1536]{1,0:T(8,128)S(1)}, f32[8,1536]{1,0:T(8,128)S(1)}, u32[]{:S(2)}, u32[]{:S(2)}) collective-permute-start(f32[8,1536]{1,0:T(8,128)S(1)} %get-tuple-element.210.first), channel_id=1, source_target_pairs={{0,4},{1,5},{2,6},{3,7},{4,0},{5,1},{6,2},{7,3},{8,12},{9,13},{10,... | collective-permute-start | bytes 147464 | tf_op jit(solution)/shard_map/ppermute | solution.py:732
  91.0 10.1 %collective-permute-start.23 = (bf16[128,1280]{1,0:T(8,128)(2,1)S(1)}, bf16[128,1280]{1,0:T(8,128)(2,1)S(1)}, u32[]{:S(2)}, u32[]{:S(2)}) collective-permute-start(bf16[128,1280]{1,0:T(8,128)(2,1)S(1)} %get-tuple-element.224), channel_id=1, source_target_pairs={{0,3},{1,2},{2,1},{3,0},{4,7},{5,6},{6,5},{7,4},{8,11},{9,10},{10,... | collective-permute-start | bytes 983048 | tf_op jit(solution)/shard_map/ppermute | solution.py:732
  97.6 6.7 %collective-permute-start.22 = (bf16[128,1280]{1,0:T(8,128)(2,1)S(1)}, bf16[128,1280]{1,0:T(8,128)(2,1)S(1)}, u32[]{:S(2)}, u32[]{:S(2)}) collective-permute-start(bf16[128,1280]{1,0:T(8,128)(2,1)S(1)} %get-tuple-element.222), channel_id=1, source_target_pairs={{0,1},{1,0},{2,3},{3,2},{4,5},{5,4},{6,7},{7,6},{8,9},{9,8},{10,11... | collective-permute-start | bytes 983048 | tf_op jit(solution)/shard_map/ppermute | solution.py:732
  97.6 3.5 %collective-permute-start.24 = (f32[8,1792]{1,0:T(8,128)S(1)}, f32[8,1792]{1,0:T(8,128)S(1)}, u32[]{:S(2)}, u32[]{:S(2)}) collective-permute-start(f32[8,1792]{1,0:T(8,128)S(1)} %get-tuple-element.226), channel_id=1, source_target_pairs={{0,1},{1,0},{2,3},{3,2},{4,5},{5,4},{6,7},{7,6},{8,9},{9,8},{10,11... | collective-permute-start | bytes 172040 | tf_op jit(solution)/shard_map/ppermute | solution.py:732
  98.1 4.5 %collective-permute-start.25 = (f32[8,1792]{1,0:T(8,128)S(1)}, f32[8,1792]{1,0:T(8,128)S(1)}, u32[]{:S(2)}, u32[]{:S(2)}) collective-permute-start(f32[8,1792]{1,0:T(8,128)S(1)} %get-tuple-element.227), channel_id=1, source_target_pairs={{0,2},{1,3},{2,0},{3,1},{4,6},{5,7},{6,4},{7,5},{8,10},{9,11},{10,... | collective-permute-start | bytes 172040 | tf_op jit(solution)/shard_map/ppermute | solution.py:732
  100.1 4.2 %collective-permute-start.26 = (f32[8,1792]{1,0:T(8,128)S(1)}, f32[8,1792]{1,0:T(8,128)S(1)}, u32[]{:S(2)}, u32[]{:S(2)}) collective-permute-start(f32[8,1792]{1,0:T(8,128)S(1)} %get-tuple-element.228), channel_id=1, source_target_pairs={{0,3},{1,2},{2,1},{3,0},{4,7},{5,6},{6,5},{7,4},{8,11},{9,10},{10,... | collective-permute-start | bytes 172040 | tf_op jit(solution)/shard_map/ppermute | solution.py:732
  (3 other events, 2.0 us)

commit v5 on v4

--- a/solution.py
+++ b/solution.py
@@ -67,13 +67,15 @@
 
 
 def head_sums(products, matrix):
-    high, low = halves(products)
-    return mm(matrix, high, NT) + mm(matrix, low, NT)
+    return mm(
+        jnp.concatenate([matrix] * 2, axis=1), jnp.concatenate(halves(products), axis=1), NT
+    )
 
 
 def by_triangle(values, triangle):
-    high, mid, low = thirds(values)
-    return mm(high, triangle, NN) + (mm(mid, triangle, NN) + mm(low, triangle, NN))
+    return mm(
+        jnp.concatenate(thirds(values), axis=1), jnp.concatenate([triangle] * 3, axis=0), NN
+    )
 
 
 def triangle(size, kind):

time: 107 us -> 108 us (level)
  no operation moved by 1% of the time
where the time goes in v5:
time: 108 us; the launch traced here: 107 us
  Pallas kernels  47.2 us (44%)
  starting transfers between devices  37.1 us (34%)
  waiting for transfers between devices  15.7 us (15%)
  local copies, waits for them, and re-layouts  5.27 us (5%)
  between operations  1.13 us (1%)
    pallas_call x18, Pallas kernels, call(): pl.pallas_call(kernel, out_shape=[pltpu.VMEM(shape, kind) if vmem else ja...  47.2 us
    ppermute x18, starting transfers between devices, swapped(): return lax.ppermute(value, 'ctx', [(i, i ^ bits) for i in range(count)])  22 us
    ppermute x5, starting transfers between devices, shifted(): return lax.ppermute(value, 'ctx', pairs)  12.5 us
    ppermute x18, waiting for transfers between devices, swapped(): return lax.ppermute(value, 'ctx', [(i, i ^ bits) for i in range(count)])  8.76 us
    ppermute x5, waiting for transfers between devices, shifted(): return lax.ppermute(value, 'ctx', pairs)  6.98 us
    unnamed x16, local copies, waits for them, and re-layouts  5.27 us
    ppermute x4, starting transfers between devices, body(): rims.append(lax.ppermute(edges[k], 'ctx', pairs))  2.64 us
  transfers between devices with their start and end apart: 27, of which 9 were waited for; matrix products, arithmetic and copies ran while one was open for 0% of the time, Pallas kernels for 40%

profile of v5, /device:TPU:0, one launch (start us, length us, event | category | flops | bytes accessed | tf_op | source)
XLA Modules:
  0.0 107.1 jit_solution(17320567097003512897)
XLA Ops:
  1.4 1.3 %copy-done.1 = bf16[128,5120]{1,0:T(8,128)(2,1)S(1)} copy-done((bf16[128,5120]{1,0:T(8,128)(2,1)S(1)}, bf16[128,5120]{1,0:T(8,128)(2,1)}, u32[]{:S(2)}) %copy-start.1) | copy-done | bytes 1310744
  4.7 2.6 %collective-permute-start.4 = (bf16[136,1280]{1,0:T(8,128)(2,1)S(1)}, bf16[136,1280]{1,0:T(8,128)(2,1)S(1)}, u32[]{:S(2)}, u32[]{:S(2)}) collective-permute-start(bf16[136,1280]{1,0:T(8,128)(2,1)S(1)} %get-tuple-element.130), channel_id=1, source_target_pairs={{0,2},{1,3},{2,0},{3,1},{4,6},{5,7},{6,4},{7,5},{8,10},{9,11},{10,... | collective-permute-start | bytes 1044488 | tf_op jit(solution)/shard_map/ppermute | solution.py:734
  13.9 2.5 %conv.1 = (f32[4,128,1280]{2,1,0:T(8,128)S(1)}, f32[4,128,1280]{2,1,0:T(8,128)S(1)}, bf16[528,1280]{1,0:T(8,128)(2,1)S(1)}) custom-call(s32[6]{0:T(128)S(1)} %pad_add_fusion.s, bf16[136,1280]{1,0:T(8,128)(2,1)S(1)} %get-tuple-element.119.x0, bf16[136,1280]{1,0:T(8,128)(2,1)S(1)} %collective-permute-done.x1, f32[4,5120]{1,0:T(4,128)S(1)} %copy-done, ...), custom_call_target="tpu_custom_call" | custom-call | flops 1 | bytes 1 | tf_op jit(solution)/shard_map/conv/pallas_call | solution.py:708
  16.4 6.9 %collective-permute-start.1 = (bf16[128,1024]{1,0:T(8,128)(2,1)S(1)}, bf16[128,1024]{1,0:T(8,128)(2,1)S(1)}, u32[]{:S(2)}, u32[]{:S(2)}) collective-permute-start(bf16[128,1024]{1,0:T(8,128)(2,1)S(1)} %get-tuple-element.127), channel_id=1, source_target_pairs={{0,1},{1,0},{2,3},{3,2},{4,5},{5,4},{6,7},{7,6},{8,9},{9,8},{10,11... | collective-permute-start | bytes 786440 | tf_op jit(solution)/shard_map/ppermute | solution.py:734
  23.6 1.6 %collective-permute-start.3 = (bf16[128,1024]{1,0:T(8,128)(2,1)S(1)}, bf16[128,1024]{1,0:T(8,128)(2,1)S(1)}, u32[]{:S(2)}, u32[]{:S(2)}) collective-permute-start(bf16[128,1024]{1,0:T(8,128)(2,1)S(1)} %get-tuple-element.129), channel_id=1, source_target_pairs={{0,3},{1,2},{2,1},{3,0},{4,7},{5,6},{6,5},{7,4},{8,11},{9,10},{10,... | collective-permute-start | bytes 786440 | tf_op jit(solution)/shard_map/ppermute | solution.py:734
  25.1 4.6 %conv_state.1 = (f32[4,128,1280]{2,1,0:T(8,128)S(1)}, f32[4,128,1280]{2,1,0:T(8,128)S(1)}, bf16[528,1280]{1,0:T(8,128)(2,1)S(1)}, f32[136,1024]{1,0:T(8,128)S(1)...) custom-call(s32[6]{0:T(128)S(1)} %pad_add_fusion.s, ...), custom_call_target="tpu_custom_call", output_to_operand_aliasing={{0}: (16, {}), {1}: (17, {}), {2}: (18, {})} | custom-call | flops 1 | bytes 1 | tf_op jit(solution)/shard_map/conv_state/pallas_call | solution.py:708
  29.8 3.6 %collective-permute-start.11 = (f32[136,1024]{1,0:T(8,128)S(1)}, f32[136,1024]{1,0:T(8,128)S(1)}, u32[]{:S(2)}, u32[]{:S(2)}) collective-permute-start(f32[136,1024]{1,0:T(8,128)S(1)} %get-tuple-element.147.pay_in.pay), channel_id=1, source_target_pairs={{0,4},{1,5},{2,6},{3,7},{4,8},{5,9},{6,10},{7,11},{8,12},{9,13},{1... | collective-permute-start | bytes 1671176 | tf_op jit(solution)/shard_map/ppermute | solution.py:740
  33.4 2.0 %within.1 = (f32[4,128,1024]{2,1,0:T(8,128)S(1)}, f32[4,128,1024]{2,1,0:T(8,128)S(1)}, f32[4,128,128]{2,1,0:T(8,128)S(1)}, f32[4,128,128]{2,1,0:T(8,128)S(1)}) custom-call(s32[6]{0:T(128)S(1)} %pad_add_fusion.s, f32[4,128,1280]{2,1,0:T(8,128)S(1)} %get-tuple-element.140.act_ref, f32[4,8,16,128]{3,2,1,0:T(8,128)S(1)} %get-tuple-element.141.vec_ref, ...), custom_call_target="tpu_custom_call" | custom-call | flops 1 | bytes 1 | tf_op jit(solution)/shard_map/within/pallas_call | solution.py:708
  35.4 1.7 %collective-permute-done.3.g3 = bf16[128,1024]{1,0:T(8,128)(2,1)S(1)} collective-permute-done((bf16[128,1024]{1,0:T(8,128)(2,1)S(1)}, bf16[128,1024]{1,0:T(8,128)(2,1)S(1)}, u32[]{:S(2)}, u32[]{:S(2)}) %collective-permute-start.3) | collective-permute-done | bytes 262176 | tf_op jit(solution)/shard_map/ppermute | solution.py:734
  37.2 2.4 %grad_state.1 = (bf16[4,128,1024]{2,1,0:T(8,128)(2,1)S(1)}, f32[136,1024]{1,0:T(8,128)S(1)}, f32[4,128,1024]{2,1,0:T(8,128)S(1)}) custom-call(s32[6]{0:T(128)S(1)} %pad_add_fusion.s, bf16[128,1024]{1,0:T(8,128)(2,1)S(1)} %get-tuple-element.143.g_ref.g0, bf16[128,1024]{1,0:T(8,128)(2,1)S(1)} %collective-permute-done.1.g1, ...), custom_call_target="tpu_custom_call" | custom-call | flops 1 | bytes 1 | tf_op jit(solution)/shard_map/grad_state/pallas_call | solution.py:708
  39.6 1.5 %collective-permute-start.10 = (f32[136,1024]{1,0:T(8,128)S(1)}, f32[136,1024]{1,0:T(8,128)S(1)}, u32[]{:S(2)}, u32[]{:S(2)}) collective-permute-start(f32[136,1024]{1,0:T(8,128)S(1)} %get-tuple-element.148), channel_id=1, source_target_pairs={{4,0},{5,1},{6,2},{7,3},{8,4},{9,5},{10,6},{11,7},{12,8},{13,9},{1... | collective-permute-start | bytes 1671176 | tf_op jit(solution)/shard_map/ppermute | solution.py:740
  41.0 5.7 %local.3 = (f32[4,128,1024]{2,1,0:T(8,128)S(1)}, f32[4,128,1024]{2,1,0:T(8,128)S(1)}, f32[4,128,128]{2,1,0:T(8,128)S(1)}, f32[4,128,128]{2,1,0:T(8,128)S(1)}, f3...) custom-call(s32[6]{0:T(128)S(1)} %pad_add_fusion.s, ...), custom_call_target="tpu_custom_call", output_to_operand_aliasing={{0}: (6, {}), {1}: (7, {}), {2}: (8, {}), {3}: (9, {})} | custom-call | flops 1 | bytes 1 | tf_op jit(solution)/shard_map/local/pallas_call | solution.py:708
  46.8 4.6 %collective-permute-start.13 = (f32[136,1024]{1,0:T(8,128)S(1)}, f32[136,1024]{1,0:T(8,128)S(1)}, u32[]{:S(2)}, u32[]{:S(2)}) collective-permute-start(f32[136,1024]{1,0:T(8,128)S(1)} %collective-permute-done.11.one), channel_id=1, source_target_pairs={{0,4},{1,5},{2,6},{3,7},{4,8},{5,9},{6,10},{7,11},{8,12},{9,13},{1... | collective-permute-start | bytes 1671176 | tf_op jit(solution)/shard_map/ppermute | solution.py:740
  51.3 3.8 %local.4 = (f32[4,128,1024]{2,1,0:T(8,128)S(1)}, f32[4,128,1024]{2,1,0:T(8,128)S(1)}, f32[4,128,128]{2,1,0:T(8,128)S(1)}, f32[4,128,128]{2,1,0:T(8,128)S(1)}, f3...) custom-call(s32[6]{0:T(128)S(1)} %pad_add_fusion.s, ...), custom_call_target="tpu_custom_call", output_to_operand_aliasing={{0}: (6, {}), {1}: (7, {}), {2}: (8, {}), {3}: (9, {}), {4}... | custom-call | flops 1 | bytes 1 | tf_op jit(solution)/shard_map/local/pallas_call | solution.py:708
  55.2 1.3 %collective-permute-done.10.one = f32[136,1024]{1,0:T(8,128)S(1)} collective-permute-done((f32[136,1024]{1,0:T(8,128)S(1)}, f32[136,1024]{1,0:T(8,128)S(1)}, u32[]{:S(2)}, u32[]{:S(2)}) %collective-permute-start.10) | collective-permute-done | bytes 557088 | tf_op jit(solution)/shard_map/ppermute | solution.py:740
  56.5 1.3 %collective-permute-start.12 = (f32[136,1024]{1,0:T(8,128)S(1)}, f32[136,1024]{1,0:T(8,128)S(1)}, u32[]{:S(2)}, u32[]{:S(2)}) collective-permute-start(f32[136,1024]{1,0:T(8,128)S(1)} %collective-permute-done.10.one), channel_id=1, source_target_pairs={{4,0},{5,1},{6,2},{7,3},{8,4},{9,5},{10,6},{11,7},{12,8},{13,9},{1... | collective-permute-start | bytes 1671176 | tf_op jit(solution)/shard_map/ppermute | solution.py:740
  57.8 3.8 %local.5 = (f32[4,128,1024]{2,1,0:T(8,128)S(1)}, f32[4,128,1024]{2,1,0:T(8,128)S(1)}, f32[4,128,128]{2,1,0:T(8,128)S(1)}, f32[4,128,128]{2,1,0:T(8,128)S(1)}, f3...) custom-call(s32[6]{0:T(128)S(1)} %pad_add_fusion.s, ...), custom_call_target="tpu_custom_call", output_to_operand_aliasing={{0}: (6, {}), {1}: (7, {}), {2}: (8, {}), {3}: (9, {}), {4}... | custom-call | flops 1 | bytes 1 | tf_op jit(solution)/shard_map/local/pallas_call | solution.py:708
  61.6 1.9 %collective-permute-done.13.two = f32[136,1024]{1,0:T(8,128)S(1)} collective-permute-done((f32[136,1024]{1,0:T(8,128)S(1)}, f32[136,1024]{1,0:T(8,128)S(1)}, u32[]{:S(2)}, u32[]{:S(2)}) %collective-permute-start.13) | collective-permute-done | bytes 557088 | tf_op jit(solution)/shard_map/ppermute | solution.py:740
  63.6 3.8 %out.1 = (bf16[128,1024]{1,0:T(8,128)(2,1)S(1)}, bf16[128,1024]{1,0:T(8,128)(2,1)S(1)}, bf16[128,1024]{1,0:T(8,128)(2,1)S(1)}, bf16[128,1024]{1,0:T(8,128)(2,1)S...) custom-call(s32[6]{0:T(128)S(1)} %pad_add_fusion.s, ...), custom_call_target="tpu_custom_call" | custom-call | flops 1 | bytes 1 | tf_op jit(solution)/shard_map/out/pallas_call | solution.py:708
  69.3 3.7 %collective-permute-done.12.two = f32[136,1024]{1,0:T(8,128)S(1)} collective-permute-done((f32[136,1024]{1,0:T(8,128)S(1)}, f32[136,1024]{1,0:T(8,128)S(1)}, u32[]{:S(2)}, u32[]{:S(2)}) %collective-permute-start.12) | collective-permute-done | bytes 557088 | tf_op jit(solution)/shard_map/ppermute | solution.py:740
  74.2 1.5 %collective-permute-start.14 = (f32[8,1280]{1,0:T(8,128)S(1)}, f32[8,1280]{1,0:T(8,128)S(1)}, u32[]{:S(2)}, u32[]{:S(2)}) collective-permute-start(f32[8,1280]{1,0:T(8,128)S(1)} %get-tuple-element.199), channel_id=1, source_target_pairs={{4,0},{5,1},{6,2},{7,3},{8,4},{9,5},{10,6},{11,7},{12,8},{13,9},{1... | collective-permute-start | bytes 122888 | tf_op jit(solution)/shard_map/ppermute | solution.py:740
  75.7 4.0 %back_far.1 = (f32[512,1280]{1,0:T(8,128)S(1)}, f32[8,1536]{1,0:T(8,128)S(1)}, f32[3,16,128]{2,1,0:T(8,128)S(1)}) custom-call(s32[6]{0:T(128)S(1)} %pad_add_fusion.s, bf16[128,1024]{1,0:T(8,128)(2,1)S(1)} %get-tuple-element.187.high_ref, bf16[128,1024]{1,0:T(8,128)(2,1)S(1)} %get-tuple-element.188.low_ref, f32[4,128,1280]{2,1,0:T(8,128)S(1)} %get-tuple-element.140.act_ref, ...), custom_call_target="tpu_custom_call" | custom-call | flops 1 | bytes 1 | tf_op jit(solution)/shard_map/back_far/pallas_call | solution.py:708
  79.7 4.4 %back_near.1 = (f32[512,1280]{1,0:T(8,128)S(1)}, f32[8,1536]{1,0:T(8,128)S(1)}, f32[16,128]{1,0:T(8,128)S(1)}, f32[16,128]{1,0:T(8,128)S(1)}, f32[16,128]{1,0:T(8,128)S(1)}, /*index=5*/f32[16,128]{1,0:T(8,128)S(1)}) custom-call(s32[6]{0:T(128)S(1)} %pad_add_fusion.s, ...), custom_call_target="tpu_custom_call", output_to_operand_aliasing={{0}: (20, {})} | custom-call | flops 1 | bytes 1 | tf_op jit(solution)/shard_map/back_near/pallas_call | solution.py:708
  84.2 1.6 %conv_back_far.1 = (bf16[128,1280]{1,0:T(8,128)(2,1)S(1)}, bf16[128,1280]{1,0:T(8,128)(2,1)S(1)}) custom-call(s32[6]{0:T(128)S(1)} %pad_add_fusion.s, f32[512,1280]{1,0:T(8,128)S(1)} %get-tuple-element.220.du_ref, f32[8,1280]{1,0:T(8,128)S(1)} %collective-permute-done.14.rim_ref, f32[4,5120]{1,0:T(4,128)S(1)} %copy-done, f32[4,5120]{1,0:T(4,128)S(1)} %copy-done, ...), custom_call_target="tpu_custom_call" | custom-call | flops 1 | bytes 1 | tf_op jit(solution)/shard_map/conv_back_far/pallas_call | solution.py:708
  85.8 4.9 %collective-permute-start.19 = (f32[8,1536]{1,0:T(8,128)S(1)}, f32[8,1536]{1,0:T(8,128)S(1)}, u32[]{:S(2)}, u32[]{:S(2)}) collective-permute-start(f32[8,1536]{1,0:T(8,128)S(1)} %get-tuple-element.210.first), channel_id=1, source_target_pairs={{0,12},{1,13},{2,14},{3,15},{4,8},{5,9},{6,10},{7,11},{8,4},{9,5},... | collective-permute-start | bytes 147464 | tf_op jit(solution)/shard_map/ppermute | solution.py:734
  91.4 1.5 %join_out.1 = bf16[128,4096]{1,0:T(8,128)(2,1)} custom-call(s32[6]{0:T(128)S(1)} %pad_add_fusion.s, bf16[128,1024]{1,0:T(8,128)(2,1)S(1)} %get-tuple-element.206.p0, bf16[128,1024]{1,0:T(8,128)(2,1)S(1)} %collective-permute-done.15.p1, bf16[128,1024]{1,0:T(8,128)(2,1)S(1)} %collective-permute-done.16.p2, bf16[128,1024]{1,0:T(8,128)(2,1)S(1)} %collective-permute-done.17.p3), custom_call_target="tpu_custom_call" | custom-call | flops 1 | bytes 1 | tf_op jit(solution)/shard_map/join_out/pallas_call | solution.py:708
  93.1 2.6 %collective-permute-done.20.refs_1_ = f32[8,1536]{1,0:T(8,128)S(1)} collective-permute-done((f32[8,1536]{1,0:T(8,128)S(1)}, f32[8,1536]{1,0:T(8,128)S(1)}, u32[]{:S(2)}, u32[]{:S(2)}) %collective-permute-start.20) | collective-permute-done | bytes 49184 | tf_op jit(solution)/shard_map/ppermute | solution.py:734
  96.3 1.6 %conv_back_near.1 = (bf16[128,1280]{1,0:T(8,128)(2,1)S(1)}, bf16[128,1280]{1,0:T(8,128)(2,1)S(1)}) custom-call(s32[6]{0:T(128)S(1)} %pad_add_fusion.s, f32[512,1280]{1,0:T(8,128)S(1)} %get-tuple-element.220.du_ref, f32[8,1280]{1,0:T(8,128)S(1)} %collective-permute-done.14.rim_ref, f32[4,5120]{1,0:T(4,128)S(1)} %copy-done, f32[4,5120]{1,0:T(4,128)S(1)} %copy-done, ...), custom_call_target="tpu_custom_call" | custom-call | flops 1 | bytes 1 | tf_op jit(solution)/shard_map/conv_back_near/pallas_call | solution.py:708
  98.5 1.9 %collective-permute-start.25 = (f32[8,1792]{1,0:T(8,128)S(1)}, f32[8,1792]{1,0:T(8,128)S(1)}, u32[]{:S(2)}, u32[]{:S(2)}) collective-permute-start(f32[8,1792]{1,0:T(8,128)S(1)} %get-tuple-element.227), channel_id=1, source_target_pairs={{0,2},{1,3},{2,0},{3,1},{4,6},{5,7},{6,4},{7,5},{8,10},{9,11},{10,... | collective-permute-start | bytes 172040 | tf_op jit(solution)/shard_map/ppermute | solution.py:734
  101.4 1.5 %collective-permute-done.25.g2 = f32[8,1792]{1,0:T(8,128)S(1)} collective-permute-done((f32[8,1792]{1,0:T(8,128)S(1)}, f32[8,1792]{1,0:T(8,128)S(1)}, u32[]{:S(2)}, u32[]{:S(2)}) %collective-permute-start.25) | collective-permute-done | bytes 57376 | tf_op jit(solution)/shard_map/ppermute | solution.py:734
  103.0 1.6 %collective-permute-done.26.g3 = f32[8,1792]{1,0:T(8,128)S(1)} collective-permute-done((f32[8,1792]{1,0:T(8,128)S(1)}, f32[8,1792]{1,0:T(8,128)S(1)}, u32[]{:S(2)}, u32[]{:S(2)}) %collective-permute-start.26) | collective-permute-done | bytes 57376 | tf_op jit(solution)/shard_map/ppermute | solution.py:734
  104.6 2.4 %join_grads.1 = (bf16[128,5120]{1,0:T(8,128)(2,1)}, f32[64,128]{1,0:T(8,128)}, f32[5,5120]{1,0:T(8,128)}, f32[3,64]{1,0:T(4,128)}) custom-call(s32[6]{0:T(128)S(1)} %pad_add_fusion.s, bf16[128,1280]{1,0:T(8,128)(2,1)S(1)} %get-tuple-element.221.p0, bf16[128,1280]{1,0:T(8,128)(2,1)S(1)} %collective-permute-done.22.p1, ...), custom_call_target="tpu_custom_call" | custom-call | flops 1 | bytes 1 | tf_op jit(solution)/shard_map/join_grads/pallas_call | solution.py:708
  (57 shorter events, 15.8 us)
Async XLA Ops:
  0.6 13.3 %copy-start = (f32[4,5120]{1,0:T(4,128)S(1)}, f32[4,5120]{1,0:T(4,128)}, u32[]{:S(2)}) copy-start(f32[4,5120]{1,0:T(4,128)} %wc.7) | copy-start | bytes 245764
  1.4 1.3 %copy-start.1 = (bf16[128,5120]{1,0:T(8,128)(2,1)S(1)}, bf16[128,5120]{1,0:T(8,128)(2,1)}, u32[]{:S(2)}) copy-start(bf16[128,5120]{1,0:T(8,128)(2,1)} %x_ref.1) | copy-start | bytes 3932164
  2.7 0.8 copy-start.4
  3.5 10.4 %copy-start.3 = (f32[5120]{0:T(1024)S(1)}, f32[5120]{0:T(1024)}, u32[]{:S(2)}) copy-start(f32[5120]{0:T(1024)} %param.15) | copy-start | bytes 61444
  4.2 5.2 %collective-permute-start = (bf16[136,1280]{1,0:T(8,128)(2,1)S(1)}, bf16[136,1280]{1,0:T(8,128)(2,1)S(1)}, u32[]{:S(2)}, u32[]{:S(2)}) collective-permute-start(bf16[136,1280]{1,0:T(8,128)(2,1)S(1)} %get-tuple-element.120), channel_id=1, source_target_pairs={{0,1},{1,0},{2,3},{3,2},{4,5},{5,4},{6,7},{7,6},{8,9},{9,8},{10,11... | collective-permute-start | bytes 1044488 | tf_op jit(solution)/shard_map/ppermute | solution.py:734
  4.7 20.4 %collective-permute-start.4 = (bf16[136,1280]{1,0:T(8,128)(2,1)S(1)}, bf16[136,1280]{1,0:T(8,128)(2,1)S(1)}, u32[]{:S(2)}, u32[]{:S(2)}) collective-permute-start(bf16[136,1280]{1,0:T(8,128)(2,1)S(1)} %get-tuple-element.130), channel_id=1, source_target_pairs={{0,2},{1,3},{2,0},{3,1},{4,6},{5,7},{6,4},{7,5},{8,10},{9,11},{10,... | collective-permute-start | bytes 1044488 | tf_op jit(solution)/shard_map/ppermute | solution.py:734
  7.3 17.8 %collective-permute-start.5 = (bf16[136,1280]{1,0:T(8,128)(2,1)S(1)}, bf16[136,1280]{1,0:T(8,128)(2,1)S(1)}, u32[]{:S(2)}, u32[]{:S(2)}) collective-permute-start(bf16[136,1280]{1,0:T(8,128)(2,1)S(1)} %get-tuple-element.131), channel_id=1, source_target_pairs={{0,3},{1,2},{2,1},{3,0},{4,7},{5,6},{6,5},{7,4},{8,11},{9,10},{10,... | collective-permute-start | bytes 1044488 | tf_op jit(solution)/shard_map/ppermute | solution.py:734
  7.4 1.3 %collective-permute-start.6 = (bf16[16,1280]{1,0:T(8,128)(2,1)S(1)}, bf16[16,1280]{1,0:T(8,128)(2,1)S(1)}, u32[]{:S(2)}, u32[]{:S(2)}) collective-permute-start(bf16[16,1280]{1,0:T(8,128)(2,1)S(1)} %get-tuple-element.132), channel_id=1, source_target_pairs={{3,7},{7,11},{11,15},{19,23},{23,27},{27,31}} | collective-permute-start | bytes 122888 | tf_op jit(solution)/shard_map/ppermute | solution.py:822
  8.0 8.4 %collective-permute-start.7 = (bf16[16,1280]{1,0:T(8,128)(2,1)S(1)}, bf16[16,1280]{1,0:T(8,128)(2,1)S(1)}, u32[]{:S(2)}, u32[]{:S(2)}) collective-permute-start(bf16[16,1280]{1,0:T(8,128)(2,1)S(1)} %get-tuple-element.133), channel_id=1, source_target_pairs={{3,6},{7,10},{11,14},{19,22},{23,26},{27,30}} | collective-permute-start | bytes 122888 | tf_op jit(solution)/shard_map/ppermute | solution.py:822
  8.7 14.6 %collective-permute-start.8 = (bf16[16,1280]{1,0:T(8,128)(2,1)S(1)}, bf16[16,1280]{1,0:T(8,128)(2,1)S(1)}, u32[]{:S(2)}, u32[]{:S(2)}) collective-permute-start(bf16[16,1280]{1,0:T(8,128)(2,1)S(1)} %get-tuple-element.134), channel_id=1, source_target_pairs={{1,3},{3,5},{5,7},{7,9},{9,11},{11,13},{13,15},{17,19},{19,21},{21... | collective-permute-start | bytes 122888 | tf_op jit(solution)/shard_map/ppermute | solution.py:822
  9.4 14.2 %collective-permute-start.9 = (bf16[16,1280]{1,0:T(8,128)(2,1)S(1)}, bf16[16,1280]{1,0:T(8,128)(2,1)S(1)}, u32[]{:S(2)}, u32[]{:S(2)}) collective-permute-start(bf16[16,1280]{1,0:T(8,128)(2,1)S(1)} %get-tuple-element.135), channel_id=1, source_target_pairs={{1,2},{3,4},{5,6},{7,8},{9,10},{11,12},{13,14},{17,18},{19,20},{21... | collective-permute-start | bytes 122888 | tf_op jit(solution)/shard_map/ppermute | solution.py:822
  10.1 1.2 %copy-start.2 = (bf16[128,4096]{1,0:T(8,128)(2,1)S(1)}, bf16[128,4096]{1,0:T(8,128)(2,1)}, u32[]{:S(2)}) copy-start(bf16[128,4096]{1,0:T(8,128)(2,1)} %g_ref.1) | copy-start | bytes 3145732
  16.4 19.0 %collective-permute-start.1 = (bf16[128,1024]{1,0:T(8,128)(2,1)S(1)}, bf16[128,1024]{1,0:T(8,128)(2,1)S(1)}, u32[]{:S(2)}, u32[]{:S(2)}) collective-permute-start(bf16[128,1024]{1,0:T(8,128)(2,1)S(1)} %get-tuple-element.127), channel_id=1, source_target_pairs={{0,1},{1,0},{2,3},{3,2},{4,5},{5,4},{6,7},{7,6},{8,9},{9,8},{10,11... | collective-permute-start | bytes 786440 | tf_op jit(solution)/shard_map/ppermute | solution.py:734
  23.3 12.1 %collective-permute-start.2 = (bf16[128,1024]{1,0:T(8,128)(2,1)S(1)}, bf16[128,1024]{1,0:T(8,128)(2,1)S(1)}, u32[]{:S(2)}, u32[]{:S(2)}) collective-permute-start(bf16[128,1024]{1,0:T(8,128)(2,1)S(1)} %get-tuple-element.128), channel_id=1, source_target_pairs={{0,2},{1,3},{2,0},{3,1},{4,6},{5,7},{6,4},{7,5},{8,10},{9,11},{10,... | collective-permute-start | bytes 786440 | tf_op jit(solution)/shard_map/ppermute | solution.py:734
  23.6 13.6 %collective-permute-start.3 = (bf16[128,1024]{1,0:T(8,128)(2,1)S(1)}, bf16[128,1024]{1,0:T(8,128)(2,1)S(1)}, u32[]{:S(2)}, u32[]{:S(2)}) collective-permute-start(bf16[128,1024]{1,0:T(8,128)(2,1)S(1)} %get-tuple-element.129), channel_id=1, source_target_pairs={{0,3},{1,2},{2,1},{3,0},{4,7},{5,6},{6,5},{7,4},{8,11},{9,10},{10,... | collective-permute-start | bytes 786440 | tf_op jit(solution)/shard_map/ppermute | solution.py:734
  29.8 17.0 %collective-permute-start.11 = (f32[136,1024]{1,0:T(8,128)S(1)}, f32[136,1024]{1,0:T(8,128)S(1)}, u32[]{:S(2)}, u32[]{:S(2)}) collective-permute-start(f32[136,1024]{1,0:T(8,128)S(1)} %get-tuple-element.147.pay_in.pay), channel_id=1, source_target_pairs={{0,4},{1,5},{2,6},{3,7},{4,8},{5,9},{6,10},{7,11},{8,12},{9,13},{1... | collective-permute-start | bytes 1671176 | tf_op jit(solution)/shard_map/ppermute | solution.py:740
  39.6 16.9 %collective-permute-start.10 = (f32[136,1024]{1,0:T(8,128)S(1)}, f32[136,1024]{1,0:T(8,128)S(1)}, u32[]{:S(2)}, u32[]{:S(2)}) collective-permute-start(f32[136,1024]{1,0:T(8,128)S(1)} %get-tuple-element.148), channel_id=1, source_target_pairs={{4,0},{5,1},{6,2},{7,3},{8,4},{9,5},{10,6},{11,7},{12,8},{13,9},{1... | collective-permute-start | bytes 1671176 | tf_op jit(solution)/shard_map/ppermute | solution.py:740
  46.8 16.8 %collective-permute-start.13 = (f32[136,1024]{1,0:T(8,128)S(1)}, f32[136,1024]{1,0:T(8,128)S(1)}, u32[]{:S(2)}, u32[]{:S(2)}) collective-permute-start(f32[136,1024]{1,0:T(8,128)S(1)} %collective-permute-done.11.one), channel_id=1, source_target_pairs={{0,4},{1,5},{2,6},{3,7},{4,8},{5,9},{6,10},{7,11},{8,12},{9,13},{1... | collective-permute-start | bytes 1671176 | tf_op jit(solution)/shard_map/ppermute | solution.py:740
  56.5 16.5 %collective-permute-start.12 = (f32[136,1024]{1,0:T(8,128)S(1)}, f32[136,1024]{1,0:T(8,128)S(1)}, u32[]{:S(2)}, u32[]{:S(2)}) collective-permute-start(f32[136,1024]{1,0:T(8,128)S(1)} %collective-permute-done.10.one), channel_id=1, source_target_pairs={{4,0},{5,1},{6,2},{7,3},{8,4},{9,5},{10,6},{11,7},{12,8},{13,9},{1... | collective-permute-start | bytes 1671176 | tf_op jit(solution)/shard_map/ppermute | solution.py:740
  67.3 16.8 %collective-permute-start.15 = (bf16[128,1024]{1,0:T(8,128)(2,1)S(1)}, bf16[128,1024]{1,0:T(8,128)(2,1)S(1)}, u32[]{:S(2)}, u32[]{:S(2)}) collective-permute-start(bf16[128,1024]{1,0:T(8,128)(2,1)S(1)} %get-tuple-element.201), channel_id=1, source_target_pairs={{0,1},{1,0},{2,3},{3,2},{4,5},{5,4},{6,7},{7,6},{8,9},{9,8},{10,11... | collective-permute-start | bytes 786440 | tf_op jit(solution)/shard_map/ppermute | solution.py:734
  67.4 16.7 %collective-permute-start.16 = (bf16[128,1024]{1,0:T(8,128)(2,1)S(1)}, bf16[128,1024]{1,0:T(8,128)(2,1)S(1)}, u32[]{:S(2)}, u32[]{:S(2)}) collective-permute-start(bf16[128,1024]{1,0:T(8,128)(2,1)S(1)} %get-tuple-element.202), channel_id=1, source_target_pairs={{0,2},{1,3},{2,0},{3,1},{4,6},{5,7},{6,4},{7,5},{8,10},{9,11},{10,... | collective-permute-start | bytes 786440 | tf_op jit(solution)/shard_map/ppermute | solution.py:734
  68.3 15.9 %collective-permute-start.17 = (bf16[128,1024]{1,0:T(8,128)(2,1)S(1)}, bf16[128,1024]{1,0:T(8,128)(2,1)S(1)}, u32[]{:S(2)}, u32[]{:S(2)}) collective-permute-start(bf16[128,1024]{1,0:T(8,128)(2,1)S(1)} %get-tuple-element.203), channel_id=1, source_target_pairs={{0,3},{1,2},{2,1},{3,0},{4,7},{5,6},{6,5},{7,4},{8,11},{9,10},{10,... | collective-permute-start | bytes 786440 | tf_op jit(solution)/shard_map/ppermute | solution.py:734
  74.2 10.0 %collective-permute-start.14 = (f32[8,1280]{1,0:T(8,128)S(1)}, f32[8,1280]{1,0:T(8,128)S(1)}, u32[]{:S(2)}, u32[]{:S(2)}) collective-permute-start(f32[8,1280]{1,0:T(8,128)S(1)} %get-tuple-element.199), channel_id=1, source_target_pairs={{4,0},{5,1},{6,2},{7,3},{8,4},{9,5},{10,6},{11,7},{12,8},{13,9},{1... | collective-permute-start | bytes 122888 | tf_op jit(solution)/shard_map/ppermute | solution.py:740
  85.8 10.5 %collective-permute-start.18 = (bf16[128,1280]{1,0:T(8,128)(2,1)S(1)}, bf16[128,1280]{1,0:T(8,128)(2,1)S(1)}, u32[]{:S(2)}, u32[]{:S(2)}) collective-permute-start(bf16[128,1280]{1,0:T(8,128)(2,1)S(1)} %get-tuple-element.205), channel_id=1, source_target_pairs={{0,2},{1,3},{2,0},{3,1},{4,6},{5,7},{6,4},{7,5},{8,10},{9,11},{10,... | collective-permute-start | bytes 983048 | tf_op jit(solution)/shard_map/ppermute | solution.py:734
  85.8 7.3 %collective-permute-start.19 = (f32[8,1536]{1,0:T(8,128)S(1)}, f32[8,1536]{1,0:T(8,128)S(1)}, u32[]{:S(2)}, u32[]{:S(2)}) collective-permute-start(f32[8,1536]{1,0:T(8,128)S(1)} %get-tuple-element.210.first), channel_id=1, source_target_pairs={{0,12},{1,13},{2,14},{3,15},{4,8},{5,9},{6,10},{7,11},{8,4},{9,5},... | collective-permute-start | bytes 147464 | tf_op jit(solution)/shard_map/ppermute | solution.py:734
  90.7 5.0 %collective-permute-start.20 = (f32[8,1536]{1,0:T(8,128)S(1)}, f32[8,1536]{1,0:T(8,128)S(1)}, u32[]{:S(2)}, u32[]{:S(2)}) collective-permute-start(f32[8,1536]{1,0:T(8,128)S(1)} %get-tuple-element.210.first), channel_id=1, source_target_pairs={{0,8},{1,9},{2,10},{3,11},{4,12},{5,13},{6,14},{7,15},{8,0},{9,1},... | collective-permute-start | bytes 147464 | tf_op jit(solution)/shard_map/ppermute | solution.py:734
  90.7 5.0 %collective-permute-start.21 = (f32[8,1536]{1,0:T(8,128)S(1)}, f32[8,1536]{1,0:T(8,128)S(1)}, u32[]{:S(2)}, u32[]{:S(2)}) collective-permute-start(f32[8,1536]{1,0:T(8,128)S(1)} %get-tuple-element.210.first), channel_id=1, source_target_pairs={{0,4},{1,5},{2,6},{3,7},{4,0},{5,1},{6,2},{7,3},{8,12},{9,13},{10,... | collective-permute-start | bytes 147464 | tf_op jit(solution)/shard_map/ppermute | solution.py:734
  91.4 10.1 %collective-permute-start.23 = (bf16[128,1280]{1,0:T(8,128)(2,1)S(1)}, bf16[128,1280]{1,0:T(8,128)(2,1)S(1)}, u32[]{:S(2)}, u32[]{:S(2)}) collective-permute-start(bf16[128,1280]{1,0:T(8,128)(2,1)S(1)} %get-tuple-element.224), channel_id=1, source_target_pairs={{0,3},{1,2},{2,1},{3,0},{4,7},{5,6},{6,5},{7,4},{8,11},{9,10},{10,... | collective-permute-start | bytes 983048 | tf_op jit(solution)/shard_map/ppermute | solution.py:734
  97.9 6.7 %collective-permute-start.22 = (bf16[128,1280]{1,0:T(8,128)(2,1)S(1)}, bf16[128,1280]{1,0:T(8,128)(2,1)S(1)}, u32[]{:S(2)}, u32[]{:S(2)}) collective-permute-start(bf16[128,1280]{1,0:T(8,128)(2,1)S(1)} %get-tuple-element.222), channel_id=1, source_target_pairs={{0,1},{1,0},{2,3},{3,2},{4,5},{5,4},{6,7},{7,6},{8,9},{9,8},{10,11... | collective-permute-start | bytes 983048 | tf_op jit(solution)/shard_map/ppermute | solution.py:734
  98.0 3.5 %collective-permute-start.24 = (f32[8,1792]{1,0:T(8,128)S(1)}, f32[8,1792]{1,0:T(8,128)S(1)}, u32[]{:S(2)}, u32[]{:S(2)}) collective-permute-start(f32[8,1792]{1,0:T(8,128)S(1)} %get-tuple-element.226), channel_id=1, source_target_pairs={{0,1},{1,0},{2,3},{3,2},{4,5},{5,4},{6,7},{7,6},{8,9},{9,8},{10,11... | collective-permute-start | bytes 172040 | tf_op jit(solution)/shard_map/ppermute | solution.py:734
  98.5 4.5 %collective-permute-start.25 = (f32[8,1792]{1,0:T(8,128)S(1)}, f32[8,1792]{1,0:T(8,128)S(1)}, u32[]{:S(2)}, u32[]{:S(2)}) collective-permute-start(f32[8,1792]{1,0:T(8,128)S(1)} %get-tuple-element.227), channel_id=1, source_target_pairs={{0,2},{1,3},{2,0},{3,1},{4,6},{5,7},{6,4},{7,5},{8,10},{9,11},{10,... | collective-permute-start | bytes 172040 | tf_op jit(solution)/shard_map/ppermute | solution.py:734
  100.4 4.2 %collective-permute-start.26 = (f32[8,1792]{1,0:T(8,128)S(1)}, f32[8,1792]{1,0:T(8,128)S(1)}, u32[]{:S(2)}, u32[]{:S(2)}) collective-permute-start(f32[8,1792]{1,0:T(8,128)S(1)} %get-tuple-element.228), channel_id=1, source_target_pairs={{0,3},{1,2},{2,1},{3,0},{4,7},{5,6},{6,5},{7,4},{8,11},{9,10},{10,... | collective-permute-start | bytes 172040 | tf_op jit(solution)/shard_map/ppermute | solution.py:734
  (3 other events, 2.0 us)
